TPU v7x, 256 devices: a whole 4x4x8 slice. The times are simulated.
256 devices in a mesh: gx: 16 (over x_lo, z), gy: 16 (over y, x_hi, core).
Axes of the slice: x: 4 (x_hi: 2, x_lo: 2; x = x_hi * 2 + x_lo), y: 4, z: 8, core: 2. Of those that a mesh axis runs over, the one named last changes fastest.
Arguments:
- polar: float32 [1024, 12288], P('gx', 'gy'), may hold values from -3.140625 to 3.140625
- azimuth: float32 [1024, 12288], P('gx', 'gy'), may hold values from -3.140625 to 3.140625
- grains: int32 [1024, 12288], P('gx', 'gy'), may hold values from 0 to 255, as said below
- stiffness: float32 [256], replicated, may hold values from 0.5 to 2
- anisotropy: float32 [256], replicated, may hold values from 0.2 to 2
- axis_polar: float32 [256], replicated, may hold values from -3.140625 to 3.140625
- axis_azimuth: float32 [256], replicated, may hold values from -3.140625 to 3.140625
- applied_field: float32 [3], replicated, may hold values from -3 to 3
Outputs:
- moment: float32 [3, 1024, 12288], P(None, 'gx', 'gy')
- spin_flip: float32 [1024, 1024], P(('gx', 'gy'))
- non_flip: float32 [1024, 1024], P(('gx', 'gy'))
Inputs may be any that keep to these rules, and one draw needn't show every extreme that they name: `grains`: grain label of each cell, a row of the grain tables.
All inputs are finite; a program needn't handle non-finite values.
Results may differ from a plain program's by a relative error of at most 0.0003.
Values sent between devices are 32-bit elements; how exact they have to be, the bound alone decides.
No kernel may reach another device: no remote copies, remote signals or barrier semaphores. Data moves between devices by JAX's collectives and lax.ppermute only.
A program may use at most 128 MiB of HBM per device.

v0:
```python
import math

import jax
import jax.numpy as jnp
import numpy as np
from jax import lax
from jax.experimental import pallas as pl
from jax.experimental.pallas import tpu as pltpu
from jax.sharding import PartitionSpec as P

NZ = 12
STEPS = 4
DAMPING = 0.5
TIME_STEP = 0.12
GAIN = TIME_STEP / (1.0 + DAMPING * DAMPING)

WX = 64
WY = 64
COLS = WY * NZ
LANES = COLS + 128
ROWS = WX + 8
STRIPS = ROWS // 8
NGRAIN = 256

COS_POLY = (
    1.0,
    -0.5,
    0.0416666641831398,
    -0.0013888862449675798,
    2.4800550818326883e-05,
    -2.753476167072222e-07,
    2.060329462594268e-09,
    -9.721622812319808e-12,
)
SIN_POLY = (
    1.0,
    -0.1666666567325592,
    0.008333321660757065,
    -0.00019840530876535922,
    2.7535795652511297e-06,
    -2.472832427713456e-08,
    1.361144114087054e-10,
)


def poly(coefs, t):
    acc = coefs[-1] * t + coefs[-2]
    for c in coefs[-3::-1]:
        acc = acc * t + c
    return acc


def sincos(x):
    t = x * x
    return x * poly(SIN_POLY, t), poly(COS_POLY, t)


def split(x):
    hi = x.astype(jnp.bfloat16)
    lo = (x - hi.astype(jnp.float32)).astype(jnp.bfloat16)
    return hi, lo


def mm(a, b):
    return jnp.dot(a, b, preferred_element_type=jnp.float32)


def iota(shape, dim):
    return lax.broadcasted_iota(jnp.int32, shape, dim)


def llg_kernel(
    polar, azimuth, grains, halo_y, halo_xh, halo_xl, tables, applied, sum_z,
    moment, payload,
    pe, ae, ge, m0, m1, wt, cx, cxd, cy, cz, ks, ux, uy, uz,
):
    for i, (src, dst) in enumerate(((polar, pe), (azimuth, ae), (grains, ge))):
        dst[0:WX, 0:COLS] = src[...].astype(jnp.float32)
        dst[0:WX, COLS:LANES] = halo_y[i * WX : (i + 1) * WX, :]
        sub = iota((8, LANES), 0)
        dst[WX:ROWS, :] = jnp.where(
            sub < 4, halo_xh[8 * i : 8 * i + 8, :], halo_xl[8 * i : 8 * i + 8, :]
        )
    tabs = [
        [jnp.broadcast_to(tables[r : r + 1, h * 128 : h * 128 + 128], (8, 128)) for h in range(2)]
        for r in range(5)
    ]

    def strip(ref, s, *lead):
        start = pl.multiple_of(s * 8, 8)
        return ref[(*lead, pl.ds(start, 8), slice(None))]

    def put(ref, s, value, *lead):
        start = pl.multiple_of(s * 8, 8)
        ref[(*lead, pl.ds(start, 8), slice(None))] = value

    def nxt(s):
        return jnp.where(s == STRIPS - 1, 0, s + 1)

    def prv(s):
        return jnp.where(s == 0, STRIPS - 1, s - 1)

    def up(cur, following):
        return pltpu.roll(jnp.where(iota(cur.shape, 0) == 0, following, cur), 7, 0)

    def down(cur, previous):
        return pltpu.roll(jnp.where(iota(cur.shape, 0) == 7, previous, cur), 1, 0)

    def setup(s, carry):
        sp, cp = sincos(strip(pe, s))
        sa, ca = sincos(strip(ae, s))
        put(m0, s, sp * ca, 0)
        put(m0, s, sp * sa, 1)
        put(m0, s, cp, 2)
        labels = strip(ge, s).astype(jnp.int32)
        low = labels & 127
        first = labels < 128
        for r, ref in enumerate((wt, ks, ux, uy, uz)):
            parts = []
            for t in range(LANES // 128):
                sl = slice(128 * t, 128 * t + 128)
                a = jnp.take_along_axis(tabs[r][0], low[:, sl], axis=1, mode="promise_in_bounds")
                b = jnp.take_along_axis(tabs[r][1], low[:, sl], axis=1, mode="promise_in_bounds")
                parts.append(jnp.where(first[:, sl], a, b))
            put(ref, s, jnp.concatenate(parts, axis=1))
        return carry

    lax.fori_loop(0, STRIPS, setup, 0)

    def couple(p, q):
        return 2.0 * p * q / (p + q)

    def couplings(s, carry):
        w = strip(wt, s)
        put(cx, s, couple(w, up(w, strip(wt, nxt(s)))))
        put(cxd, s, couple(w, down(w, strip(wt, prv(s)))))
        put(cy, s, couple(w, pltpu.roll(w, LANES - NZ, 1)))
        lane = iota(w.shape, 1)
        depth = jnp.where(lane < COLS + 64, lane, lane - LANES + 6 * NZ + COLS) % NZ
        linked = depth != NZ - 1
        put(cz, s, jnp.where(linked, couple(w, pltpu.roll(w, LANES - 1, 1)), 0.0))
        return carry

    lax.fori_loop(0, STRIPS, couplings, 0)

    def step(src, dst, s):
        after, before = nxt(s), prv(s)
        m = [strip(src, s, c) for c in range(3)]
        u = [strip(r, s) for r in (ux, uy, uz)]
        kx, kxd, ky, kz = strip(cx, s), strip(cxd, s), strip(cy, s), strip(cz, s)
        proj = strip(ks, s) * (u[0] * m[0] + u[1] * m[1] + u[2] * m[2])
        h = []
        for c in range(3):
            f = kx * (up(m[c], strip(src, after, c)) - m[c])
            f = f + kxd * (down(m[c], strip(src, before, c)) - m[c])
            fy = ky * (pltpu.roll(m[c], LANES - NZ, 1) - m[c])
            f = f + fy - pltpu.roll(fy, NZ, 1)
            fz = kz * (pltpu.roll(m[c], LANES - 1, 1) - m[c])
            f = f + fz - pltpu.roll(fz, 1, 1)
            h.append(f + proj * u[c] + applied[c])
        t = cross(m, h)
        d = cross(m, t)
        v = [m[c] - GAIN * (t[c] + DAMPING * d[c]) for c in range(3)]
        r = lax.rsqrt(v[0] * v[0] + v[1] * v[1] + v[2] * v[2])
        for c in range(3):
            put(dst, s, v[c] * r, c)

    def one(src, dst, count):
        def body(s, carry):
            step(src, dst, s)
            return carry

        lax.fori_loop(0, count, body, 0)

    one(m0, m1, STRIPS)
    one(m1, m0, STRIPS)
    one(m0, m1, STRIPS)
    one(m1, m0, STRIPS - 1)

    for c in range(3):
        moment[c] = m0[c, 0:WX, 0:COLS]

    m = jnp.concatenate([m0[c, 0:WX, 0:COLS] for c in range(3)], axis=0)
    hi, lo = split(m)
    out = mm(hi, sum_z[...]) + mm(lo, sum_z[...])
    lane = iota((WX, 128), 1)
    sides = []
    for half in range(2):
        o = [out[c * WX : (c + 1) * WX, half * 128 : half * 128 + 128] for c in range(3)]
        sides.append(jnp.where(lane < 32, o[0], jnp.where(lane < 64, o[1], o[2])))
    turned = jnp.concatenate(sides, axis=0).T
    for cp in range(8):
        payload[pl.ds(cp, 16, stride=8), :] = turned[cp * 16 : cp * 16 + 16, :]


def cross(first, second):
    return [
        first[1] * second[2] - first[2] * second[1],
        first[2] * second[0] - first[0] * second[2],
        first[0] * second[1] - first[1] * second[0],
    ]


def x_kernel(got, twiddle, waves_hi, waves_lo, out):
    f = [got[8 * i : 8 * i + 8, :] for i in range(16)]
    even = [f[i] + f[16 - i] for i in range(1, 8)]
    odd = [f[i] - f[16 - i] for i in range(1, 8)]
    real, imag = [], []
    for r in range(9):
        acc = f[0] + f[8] if r % 2 == 0 else f[0] - f[8]
        for i in range(1, 8):
            w = math.cos(2.0 * math.pi * ((r * i) % 16) / 16)
            acc = acc + even[i - 1] * w
        real.append(acc)
        acc = None
        if r not in (0, 8):
            for i in range(1, 8):
                w = -math.sin(2.0 * math.pi * ((r * i) % 16) / 16)
                acc = odd[i - 1] * w if acc is None else acc + odd[i - 1] * w
        imag.append(acc)
    rows_re, rows_im = [], []
    for r in range(16):
        gr = real[r] if r <= 8 else real[16 - r]
        gi = imag[r] if r <= 8 else -imag[16 - r]
        c = twiddle[r : r + 1, :]
        s = twiddle[16 + r : 17 + r, :]
        if gi is None:
            rows_re.append(gr * c)
            rows_im.append(-gr * s)
        else:
            rows_re.append(gr * c + gi * s)
            rows_im.append(gi * c - gr * s)
    order = []
    for top in range(4):
        order += [rows_re[4 * top + low] for low in range(4)]
        order += [rows_im[4 * top + low] for low in range(4)]
    turned = jnp.concatenate(order, axis=0).T
    lane = iota((WX, 128), 1)
    imaginary = lane % 64 >= 32
    full = []
    for h in range(2):
        hi, lo = split(turned[h * 64 : h * 64 + 64, :])
        both = mm(waves_hi[...], hi) + (mm(waves_hi[...], lo) + mm(waves_lo[...], hi))
        tiles = []
        for t in range(2):
            p = both[0:64, t * 128 : t * 128 + 128]
            q = both[64:128, t * 128 : t * 128 + 128]
            tiles.append(
                p + jnp.where(imaginary, -pltpu.roll(q, 32, 1), pltpu.roll(q, 96, 1))
            )
        full.append(tiles)
    for top in range(4):
        a, b = full[0][top // 2], full[1][top // 2]
        if top % 2 == 0:
            b = pltpu.roll(b, 64, 1)
        else:
            a = pltpu.roll(a, 64, 1)
        out[pl.ds(top, 64, stride=4), :] = jnp.where(lane < 64, a, b)


def y_kernel(first_row, got, waves_hi, waves_lo, twiddle, spin_flip, non_flip, turned):
    for t in range(2):
        turned[t] = got[128 * t : 128 * t + 128, :].T
    tiles = []
    for h in range(2):
        for p in range(2):
            for c in range(3):
                rows = pl.ds(h * 64 + 2 * c + p, 8, stride=8)
                tiles.append(jnp.concatenate([turned[t, rows, :] for t in range(2)], axis=1))
    hi, lo = split(jnp.concatenate(tiles, axis=0))
    both = mm(hi, waves_hi[...]) + (mm(lo, waves_hi[...]) + mm(hi, waves_lo[...]))
    width = 256
    sign = jnp.where(iota((8, width), 0) < 4, 1.0, -1.0)

    def spin(z):
        return pltpu.roll(z, 4, 0) * sign

    parts = {}
    for h in range(2):
        for p in range(2):
            b = 2 * p + h
            for c in range(3):
                row = ((h * 2 + p) * 3 + c) * 8
                z = both[row : row + 8, 0:width] + spin(both[row : row + 8, width : 2 * width])
                if b:
                    z = z * twiddle[b : b + 1, :] + spin(z) * twiddle[4 + b : 5 + b, :]
                parts[h, p, c] = z
    spectrum = [[None] * 3 for _ in range(4)]
    for c in range(3):
        plus = [parts[h, 0, c] + parts[h, 1, c] for h in range(2)]
        minus = [parts[h, 0, c] - parts[h, 1, c] for h in range(2)]
        turn = spin(minus[1])
        spectrum[0][c] = plus[0] + plus[1]
        spectrum[2][c] = plus[0] - plus[1]
        spectrum[1][c] = minus[0] + turn
        spectrum[3][c] = minus[0] - turn
    kx = first_row[0] + iota((8, width), 0) % 4
    wave_x = jnp.where(kx < 512, kx, kx - 1024).astype(jnp.float32)
    scale = 1.0 / (NZ * 1024.0 * 1024.0)
    for d in range(4):
        ky = iota((8, width), 1) + 256 * d
        wave_y = jnp.where(ky < 512, ky, ky - 1024).astype(jnp.float32)
        squared = wave_x * wave_x + wave_y * wave_y
        inverse = lax.rsqrt(jnp.maximum(squared, 1.0))
        unit_x = wave_x * inverse
        unit_y = wave_y * inverse
        stop = jnp.where(squared > 0.5, scale, 0.0)
        sx, sy, sz = spectrum[d]
        along = unit_x * sx + unit_y * sy
        px = sx - unit_x * along
        py = sy - unit_y * along
        nf = px * px
        sf = py * py + sz * sz
        nf = (nf + pltpu.roll(nf, 4, 0)) * stop
        sf = (sf + pltpu.roll(sf, 4, 0)) * stop
        non_flip[:, width * d : width * d + width] = nf[0:4, :]
        spin_flip[:, width * d : width * d + width] = sf[0:4, :]


def pieces(x):
    hi = x.astype(jnp.bfloat16)
    lo = (x - hi.astype(np.float64)).astype(jnp.bfloat16)
    return jnp.asarray(hi), jnp.asarray(lo)


def sum_matrix():
    y = np.arange(COLS) // NZ
    col = np.arange(256)
    h, p, j = col // 128, col % 32 // 16, col % 16
    return jnp.asarray((y[:, None] == (4 * j + 2 * p + h)[None, :]).astype(jnp.bfloat16))


def x_tables():
    r = np.arange(16)[:, None]
    x = (np.arange(128) % 64)[None, :]
    phase = 2.0 * np.pi * (r * x) / 1024.0
    twiddle = jnp.asarray(np.concatenate([np.cos(phase), np.sin(phase)]).astype(np.float32))
    q = np.arange(64)
    phase = 2.0 * np.pi * (np.outer(q, q) % 64) / 64.0
    return (twiddle, *pieces(np.concatenate([np.cos(phase), np.sin(phase)])))


def y_tables():
    s = np.arange(256)
    a = 16 * (s % 16) + s // 16
    k = np.arange(256)
    phase = 2.0 * np.pi * (np.outer(a, k) % 256) / 256.0
    waves = pieces(np.concatenate([np.cos(phase), np.sin(phase)], axis=1))
    phase = 2.0 * np.pi * np.outer(np.arange(4), k) / 1024.0
    twiddle = np.concatenate([np.cos(phase), np.sin(phase)]).astype(np.float32)
    return (*waves, jnp.asarray(twiddle))


def f32(*shape):
    return jax.ShapeDtypeStruct(shape, jnp.float32)


def vmem(n):
    return [pl.BlockSpec(memory_space=pltpu.VMEM)] * n


def shards(polar, azimuth, grains, stiffness, anisotropy, axis_polar, axis_azimuth, applied_field):
    count_x = lax.axis_size("gx")
    count_y = lax.axis_size("gy")
    forward_x = [(i, (i + 1) % count_x) for i in range(count_x)]
    backward_x = [(t, s) for s, t in forward_x]
    forward_y = [(i, (i + 1) % count_y) for i in range(count_y)]
    backward_y = [(t, s) for s, t in forward_y]
    fields = (polar, azimuth, grains)
    low_edge = jnp.concatenate([f[:, :128].astype(jnp.float32) for f in fields], axis=0)
    high_edge = jnp.concatenate(
        [f[:, COLS - 128 :].astype(jnp.float32) for f in fields], axis=0
    )
    from_high = lax.ppermute(low_edge, "gy", backward_y)
    from_low = lax.ppermute(high_edge, "gy", forward_y)
    lane = lax.broadcasted_iota(jnp.int32, (3 * WX, 128), 1)
    halo_y = jnp.where(lane < 64, from_high, from_low)

    def edge(start):
        return jnp.concatenate(
            [
                jnp.concatenate(
                    [
                        f[start : start + 8].astype(jnp.float32),
                        halo_y[i * WX + start : i * WX + start + 8],
                    ],
                    axis=1,
                )
                for i, f in enumerate(fields)
            ],
            axis=0,
        )

    halo_xh = lax.ppermute(edge(0), "gx", backward_x)
    halo_xl = lax.ppermute(edge(WX - 8), "gx", forward_x)
    tables = jnp.stack(
        [
            stiffness,
            anisotropy,
            jnp.sin(axis_polar) * jnp.cos(axis_azimuth),
            jnp.sin(axis_polar) * jnp.sin(axis_azimuth),
            jnp.cos(axis_polar),
        ],
        axis=0,
    )
    wide = pltpu.VMEM((ROWS, LANES), jnp.float32)
    triple = pltpu.VMEM((3, ROWS, LANES), jnp.float32)
    in_specs = vmem(7) + [pl.BlockSpec(memory_space=pltpu.SMEM)] + vmem(1)
    moment, payload = pl.pallas_call(
        llg_kernel,
        out_shape=(f32(3, WX, COLS), f32(128, 128)),
        in_specs=in_specs,
        out_specs=tuple(vmem(2)),
        scratch_shapes=[wide] * 3 + [triple] * 2 + [wide] * 9,
        compiler_params=pltpu.CompilerParams(vmem_limit_bytes=32 << 20),
        name="llg",
    )(polar, azimuth, grains, halo_y, halo_xh, halo_xl, tables, applied_field, sum_matrix())

    columns = lax.all_to_all(
        payload.reshape(16, 8, 128), "gx", split_axis=0, concat_axis=0, tiled=True
    ).reshape(128, 128)
    rows = pl.pallas_call(
        x_kernel,
        out_shape=f32(256, 128),
        in_specs=vmem(4),
        out_specs=vmem(1)[0],
        name="along_x",
    )(columns, *x_tables())
    mine = lax.all_to_all(
        rows.reshape(256, 1, 128), ("gx", "gy"), split_axis=0, concat_axis=0, tiled=True
    ).reshape(256, 128)
    first_row = (lax.axis_index("gx") * WX + lax.axis_index("gy") * 4).astype(jnp.int32)
    spin_flip, non_flip = pl.pallas_call(
        y_kernel,
        out_shape=(f32(4, 1024), f32(4, 1024)),
        in_specs=[pl.BlockSpec(memory_space=pltpu.SMEM)] + vmem(4),
        out_specs=tuple(vmem(2)),
        scratch_shapes=[pltpu.VMEM((2, 128, 128), jnp.float32)],
        name="along_y",
    )(first_row.reshape(1), mine, *y_tables())
    return (moment, spin_flip, non_flip)


def solution(mesh):
    in_specs = (P("gx", "gy"), P("gx", "gy"), P("gx", "gy"), P(), P(), P(), P(), P())
    out_specs = (P(None, "gx", "gy"), P(("gx", "gy"), None), P(("gx", "gy"), None))
    return jax.shard_map(shards, mesh=mesh, in_specs=in_specs, out_specs=out_specs, check_vma=False)
```

profile of v0, /device:TPU:1, one launch (start us, length us, event | category | flops | bytes accessed | tf_op | source)
XLA Modules:
  0.0 72.8 jit_solution(4140555302374374562)
XLA Ops:
  0.6 0.8 %slice_convert_fusion = (f32[64,128]{1,0:T(8,128)S(1)}, f32[64,128]{1,0:T(8,128)S(1)}) fusion(s32[64,768]{1,0:T(8,128)} %grains.1), kind=kLoop, calls=%fused_computation.5 | loop fusion | flops 16384 | bytes 131072 | tf_op jit(solution)/shard_map/convert_element_type | solution.py:372
  1.4 0.8 %fusion.2 = (f32[64,128]{1,0:T(8,128)S(1)}, f32[64,128]{1,0:T(8,128)S(1)}, f32[64,128]{1,0:T(8,128)S(1)}, f32[64,128]{1,0:T(8,128)S(1)}) fusion(f32[64,768]{1,0:T(8,128)} %polar.1, f32[64,768]{1,0:T(8,128)} %azimuth.1), kind=kLoop, calls=%fused_computation.14 | loop fusion | bytes 262144 | tf_op jit(solution)/shard_map/slice | solution.py:372
  2.2 0.0 copy-start.1
  2.2 0.0 copy-start.2
  2.3 4.2 %collective-permute-start.1 = (f32[192,128]{1,0:T(8,128)S(1)}, f32[192,128]{1,0:T(8,128)S(1)}, u32[]{:S(2)}, u32[]{:S(2)}) collective-permute-start(f32[192,128]{1,0:T(8,128)S(1)} %pad_maximum_fusion.1), channel_id=1, source_target_pairs={{0,1},{1,2},{2,3},{3,4},{4,5},{5,6},{6,7},{7,8},{8,9},{9,10},{10,1... | collective-permute-start | bytes 294920 | tf_op jit(solution)/shard_map/ppermute | solution.py:375
  6.5 0.0 copy-start
  6.5 0.1 collective-permute-start
  6.6 0.0 copy-done.1
  6.6 0.0 copy-done.2
  6.6 0.8 %copy-done = s32[64,768]{1,0:T(8,128)S(1)} copy-done((s32[64,768]{1,0:T(8,128)S(1)}, s32[64,768]{1,0:T(8,128)}, u32[]{:S(2)}) %copy-start) | copy-done | bytes 196632
  7.4 0.0 copy-start.6
  7.4 0.7 copy-done.6
  8.1 0.0 copy-start.3
  8.1 0.0 collective-permute-done.1
  8.2 4.3 %collective-permute-done = f32[192,128]{1,0:T(8,128)S(1)} collective-permute-done((f32[192,128]{1,0:T(8,128)S(1)}, f32[192,128]{1,0:T(8,128)S(1)}, u32[]{:S(2)}, u32[]{:S(2)}) %collective-permute-start) | collective-permute-done | bytes 98336 | tf_op jit(solution)/shard_map/ppermute | solution.py:374
  12.5 1.4 %collective-permute-start.3 = (f32[24,896]{1,0:T(8,128)S(1)}, f32[24,896]{1,0:T(8,128)S(1)}, u32[]{:S(2)}, u32[]{:S(2)}) collective-permute-start(f32[24,896]{1,0:T(8,128)S(1)} %maximum_maximum_fusion.1), channel_id=1, source_target_pairs={{0,16},{16,32},{32,48},{48,64},{64,80},{80,96},{96,112},{112,128},... | collective-permute-start | bytes 258056 | tf_op jit(solution)/shard_map/ppermute | solution.py:395
  13.9 0.0 copy-start.7
  13.9 4.1 %collective-permute-start.2 = (f32[24,896]{1,0:T(8,128)S(1)}, f32[24,896]{1,0:T(8,128)S(1)}, u32[]{:S(2)}, u32[]{:S(2)}) collective-permute-start(f32[24,896]{1,0:T(8,128)S(1)} %maximum_maximum_fusion), channel_id=1, source_target_pairs={{16,0},{32,16},{48,32},{64,48},{80,64},{96,80},{112,96},{128,112},... | collective-permute-start | bytes 258056 | tf_op jit(solution)/shard_map/ppermute | solution.py:394
  18.0 0.0 copy-start.9
  18.0 0.0 copy-done.7
  18.0 0.0 copy-start.8
  18.0 0.6 copy-done.9
  18.6 0.1 copy-done.8
  18.7 0.0 copy-start.4
  18.7 1.8 %collective-permute-done.3.halo_xl = f32[24,896]{1,0:T(8,128)S(1)} collective-permute-done((f32[24,896]{1,0:T(8,128)S(1)}, f32[24,896]{1,0:T(8,128)S(1)}, u32[]{:S(2)}, u32[]{:S(2)}) %collective-permute-start.3) | collective-permute-done | bytes 86048 | tf_op jit(solution)/shard_map/ppermute | solution.py:395
  20.5 0.0 collective-permute-done.2.halo_xh
  20.5 0.0 copy-done.3
  20.5 0.0 copy-done.4
  20.6 12.8 %llg.1 = (f32[3,64,768]{2,1,0:T(8,128)}, f32[128,128]{1,0:T(8,128)S(1)}) custom-call(f32[64,768]{1,0:T(8,128)S(1)} %copy-done.1, f32[64,768]{1,0:T(8,128)S(1)} %copy-done.2, s32[64,768]{1,0:T(8,128)S(1)} %copy-done, f32[192,128]{1,0:T(8,128)S(1)} %broadcast_select_fusion.halo_y, f32[24,896]{1,0:T(8,128)S(1)} %collective-permute-done.2.halo_xh, ...), custom_call_target="tpu_custom_call" | custom-call | tf_op jit(solution)/shard_map/llg/pallas_call | solution.py:409
  33.4 13.3 %all_to_all.10 = f32[16,8,128]{2,1,0:T(8,128)} all-to-all(f32[16,8,128]{2,1,0:T(8,128)S(1)} %bitcast.12), channel_id=1, replica_groups=mesh['gx'=16,'gy'=16] {'gx'}, dimensions={0} | all-to-all | bytes 131072 | tf_op jit(solution)/shard_map/all_to_all | solution.py:419
  46.6 2.0 %along_x.1 = f32[256,128]{1,0:T(8,128)} custom-call(f32[128,128]{1,0:T(8,128)} %bitcast.15, f32[32,128]{1,0:T(8,128)} %constant.27.clone.twiddle, bf16[128,64]{1,0:T(8,128)(2,1)} %constant.28.clone.waves_hi, bf16[128,64]{1,0:T(8,128)(2,1)} %constant.29.clone.waves_lo), custom_call_target="tpu_custom_call" | custom-call | tf_op jit(solution)/shard_map/along_x/pallas_call | solution.py:422
  48.7 8.3 %all-to-all-start.1 = ((f32[256,1,128]{2,1,0:T(1,128)}), f32[256,1,128]{2,1,0:T(1,128)S(1)}, u32[]{:S(2)}, u32[]{:S(2)}) async-start(f32[256,1,128]{2,1,0:T(1,128)} %bitcast.13), calls=%async_computation.1 | async-start | bytes 262144 | tf_op jit(solution)/shard_map/all_to_all | solution.py:429
  57.0 13.1 %all-to-all-done.1 = f32[256,1,128]{2,1,0:T(1,128)S(1)} async-done(((f32[256,1,128]{2,1,0:T(1,128)}), f32[256,1,128]{2,1,0:T(1,128)S(1)}, u32[]{:S(2)}, u32[]{:S(2)}) %all-to-all-start.1) | async-done | bytes 131104 | tf_op jit(solution)/shard_map/all_to_all | solution.py:429
  70.1 0.0 copy-start.5
  70.1 0.6 copy-done.5
  70.7 2.1 %along_y.1 = (f32[4,1024]{1,0:T(4,128)}, f32[4,1024]{1,0:T(4,128)}) custom-call(s32[1]{0:T(128)} %bitcast.5.first_row, f32[256,128]{1,0:T(8,128)} %bitcast.14, bf16[256,512]{1,0:T(8,128)(2,1)} %constant.30.clone.waves_hi, bf16[256,512]{1,0:T(8,128)(2,1)} %constant.31.clone.waves_lo, f32[8,256]{1,0:T(8,128)} %constant.32.clone.twiddle), custom_call_target="tpu_custom_call" | custom-call | tf_op jit(solution)/shard_map/along_y/pallas_call | solution.py:433
  (12 shorter events, 0.2 us)
Async XLA Ops:
  2.2 4.4 %copy-start.1 = (f32[64,768]{1,0:T(8,128)S(1)}, f32[64,768]{1,0:T(8,128)}, u32[]{:S(2)}) copy-start(f32[64,768]{1,0:T(8,128)} %polar.1) | copy-start | bytes 589828
  2.2 4.4 %copy-start.2 = (f32[64,768]{1,0:T(8,128)S(1)}, f32[64,768]{1,0:T(8,128)}, u32[]{:S(2)}) copy-start(f32[64,768]{1,0:T(8,128)} %azimuth.1) | copy-start | bytes 589828
  2.3 5.9 %collective-permute-start.1 = (f32[192,128]{1,0:T(8,128)S(1)}, f32[192,128]{1,0:T(8,128)S(1)}, u32[]{:S(2)}, u32[]{:S(2)}) collective-permute-start(f32[192,128]{1,0:T(8,128)S(1)} %pad_maximum_fusion.1), channel_id=1, source_target_pairs={{0,1},{1,2},{2,3},{3,4},{4,5},{5,6},{6,7},{7,8},{8,9},{9,10},{10,1... | collective-permute-start | bytes 294920 | tf_op jit(solution)/shard_map/ppermute | solution.py:375
  6.5 0.9 %copy-start = (s32[64,768]{1,0:T(8,128)S(1)}, s32[64,768]{1,0:T(8,128)}, u32[]{:S(2)}) copy-start(s32[64,768]{1,0:T(8,128)} %grains.1) | copy-start | bytes 589828
  6.5 5.9 %collective-permute-start = (f32[192,128]{1,0:T(8,128)S(1)}, f32[192,128]{1,0:T(8,128)S(1)}, u32[]{:S(2)}, u32[]{:S(2)}) collective-permute-start(f32[192,128]{1,0:T(8,128)S(1)} %pad_maximum_fusion), channel_id=1, source_target_pairs={{1,0},{2,1},{3,2},{4,3},{5,4},{6,5},{7,6},{8,7},{9,8},{10,9},{11,1... | collective-permute-start | bytes 294920 | tf_op jit(solution)/shard_map/ppermute | solution.py:374
  7.4 0.7 copy-start.6
  8.1 12.5 %copy-start.3 = (bf16[768,256]{1,0:T(8,128)(2,1)S(1)}, bf16[768,256]{1,0:T(8,128)(2,1)}, u32[]{:S(2)}) copy-start(bf16[768,256]{1,0:T(8,128)(2,1)} %constant.26.clone.sum_z) | copy-start | bytes 1179652
  12.5 8.1 %collective-permute-start.3 = (f32[24,896]{1,0:T(8,128)S(1)}, f32[24,896]{1,0:T(8,128)S(1)}, u32[]{:S(2)}, u32[]{:S(2)}) collective-permute-start(f32[24,896]{1,0:T(8,128)S(1)} %maximum_maximum_fusion.1), channel_id=1, source_target_pairs={{0,16},{16,32},{32,48},{48,64},{64,80},{80,96},{96,112},{112,128},... | collective-permute-start | bytes 258056 | tf_op jit(solution)/shard_map/ppermute | solution.py:395
  13.9 4.1 %copy-start.7 = (f32[256]{0:T(256)S(1)}, f32[256]{0:T(256)}, u32[]{:S(2)}) copy-start(f32[256]{0:T(256)} %param.21) | copy-start | bytes 3076
  13.9 6.6 %collective-permute-start.2 = (f32[24,896]{1,0:T(8,128)S(1)}, f32[24,896]{1,0:T(8,128)S(1)}, u32[]{:S(2)}, u32[]{:S(2)}) collective-permute-start(f32[24,896]{1,0:T(8,128)S(1)} %maximum_maximum_fusion), channel_id=1, source_target_pairs={{16,0},{32,16},{48,32},{64,48},{80,64},{96,80},{112,96},{128,112},... | collective-permute-start | bytes 258056 | tf_op jit(solution)/shard_map/ppermute | solution.py:394
  18.0 0.7 copy-start.9
  18.0 0.7 copy-start.8
  18.7 1.8 %copy-start.4 = (f32[3]{0:T(128)S(1)}, f32[3]{0:T(128)}, u32[]{:S(2)}) copy-start(f32[3]{0:T(128)} %applied.1) | copy-start | bytes 40
  48.7 21.4 %all-to-all-start.1 = ((f32[256,1,128]{2,1,0:T(1,128)}), f32[256,1,128]{2,1,0:T(1,128)S(1)}, u32[]{:S(2)}, u32[]{:S(2)}) async-start(f32[256,1,128]{2,1,0:T(1,128)} %bitcast.13), calls=%async_computation.1 | async-start | bytes 262144 | tf_op jit(solution)/shard_map/all_to_all | solution.py:429
  70.1 0.6 copy-start.5
where the time goes:
time: 73.2 us; the launch traced here: 72.8 us
  waiting for transfers between devices  19.2 us (26%)
  starting transfers between devices  18.1 us (25%)
  Pallas kernels  16.9 us (23%)
  blocking collectives  13.3 us (18%)
  local copies, waits for them, and re-layouts  3.7 us (5%)
  other arithmetic  0.88 us (1%)
  between operations  0.77 us (1%)
    all_to_all x1, blocking collectives, shards(): lax.all_to_all(payload.reshape(16, 8, 128), 'gx', split_axis=0, concat_ax...  13.3 us
    all_to_all x1, waiting for transfers between devices, shards(): lax.all_to_all(rows.reshape(256, 1, 128), ('gx', 'gy'), split_axis=0, con...  13.1 us
    pallas_call x1, Pallas kernels, shards(): pl.pallas_call(llg_kernel, out_shape=(f32(3, WX, COLS), f32(128, 128)), i...  12.8 us
    all_to_all x1, starting transfers between devices, shards(): lax.all_to_all(rows.reshape(256, 1, 128), ('gx', 'gy'), split_axis=0, con...  8.31 us
    ppermute x1, waiting for transfers between devices, shards(): from_high = lax.ppermute(low_edge, 'gy', backward_y)  4.26 us
    ppermute x1, starting transfers between devices, shards(): from_low = lax.ppermute(high_edge, 'gy', forward_y)  4.21 us
    ppermute x1, starting transfers between devices, shards(): halo_xh = lax.ppermute(edge(0), 'gx', backward_x)  4.07 us
    unnamed x20, local copies, waits for them, and re-layouts  2.8 us
  transfers between devices with their start and end apart: 5, of which 3 were waited for; matrix products, arithmetic and copies ran while one was open for 0% of the time, Pallas kernels for 0%

commit v1 on v0

v1 whole, which is shorter than its diff:
```python
import math

import jax
import jax.numpy as jnp
import numpy as np
from jax import lax
from jax.experimental import pallas as pl
from jax.experimental.pallas import tpu as pltpu
from jax.sharding import PartitionSpec as P

NZ = 12
STEPS = 4
DAMPING = 0.5
TIME_STEP = 0.12
GAIN = TIME_STEP / (1.0 + DAMPING * DAMPING)

WX = 64
WY = 64
COLS = WY * NZ
LANES = COLS + 128
ROWS = WX + 8
STRIPS = ROWS // 8
NGRAIN = 256

COS_POLY = (
    1.0,
    -0.5,
    0.0416666641831398,
    -0.0013888862449675798,
    2.4800550818326883e-05,
    -2.753476167072222e-07,
    2.060329462594268e-09,
    -9.721622812319808e-12,
)
SIN_POLY = (
    1.0,
    -0.1666666567325592,
    0.008333321660757065,
    -0.00019840530876535922,
    2.7535795652511297e-06,
    -2.472832427713456e-08,
    1.361144114087054e-10,
)


def poly(coefs, t):
    acc = coefs[-1] * t + coefs[-2]
    for c in coefs[-3::-1]:
        acc = acc * t + c
    return acc


def sincos(x):
    t = x * x
    return x * poly(SIN_POLY, t), poly(COS_POLY, t)


def split(x):
    hi = x.astype(jnp.bfloat16)
    lo = (x - hi.astype(jnp.float32)).astype(jnp.bfloat16)
    return hi, lo


def mm(a, b):
    return jnp.dot(a, b, preferred_element_type=jnp.float32)


def iota(shape, dim):
    return lax.broadcasted_iota(jnp.int32, shape, dim)


def strip(ref, s, *lead):
    return ref[(*lead, pl.ds(pl.multiple_of(s * 8, 8), 8), slice(None))]


def put(ref, s, value, *lead):
    ref[(*lead, pl.ds(pl.multiple_of(s * 8, 8), 8), slice(None))] = value


def up(cur, following):
    return pltpu.roll(jnp.where(iota(cur.shape, 0) == 0, following, cur), 7, 0)


def down(cur, previous):
    return pltpu.roll(jnp.where(iota(cur.shape, 0) == 7, previous, cur), 1, 0)


def grain_tables(rows):
    return [
        [jnp.broadcast_to(row[:, h * 128 : h * 128 + 128], (8, 128)) for h in range(2)]
        for row in rows
    ]


def look_up(pair, labels):
    low = labels & 127
    first = labels < 128
    parts = []
    for t in range(labels.shape[1] // 128):
        sl = slice(128 * t, 128 * t + 128)
        a = jnp.take_along_axis(pair[0], low[:, sl], axis=1, mode="promise_in_bounds")
        b = jnp.take_along_axis(pair[1], low[:, sl], axis=1, mode="promise_in_bounds")
        parts.append(jnp.where(first[:, sl], a, b))
    return jnp.concatenate(parts, axis=1)


def start_cells(polar, azimuth):
    sp, cp = sincos(polar)
    sa, ca = sincos(azimuth)
    return sp * ca, sp * sa, cp


def couple(p, q):
    return (2.0 * GAIN) * p * q / (p + q)


def edges_kernel(p_low, a_low, g_low, p_high, a_high, g_high, low, high):
    for dst, refs in ((low, (p_low, a_low, g_low)), (high, (p_high, a_high, g_high))):
        for i, ref in enumerate(refs):
            dst[i * WX : (i + 1) * WX, :] = ref[...].astype(jnp.float32)


def cells_kernel(
    polar, azimuth, grains, stiffness, anisotropy, axis_polar, axis_azimuth, cells, props, tables
):
    ax, ay, az = start_cells(axis_polar[...], axis_azimuth[...])
    rows = [stiffness[...], GAIN * anisotropy[...], ax, ay, az]
    for r, row in enumerate(rows):
        tables[r : r + 1, :] = row
    tabs = grain_tables(rows)

    def body(s, carry):
        start = start_cells(strip(polar, s), strip(azimuth, s))
        for c in range(3):
            put(cells, s, start[c], c)
        labels = strip(grains, s)
        for r in range(5):
            put(props, s, look_up(tabs[r], labels), r)
        return carry

    lax.fori_loop(0, WX // 8, body, 0, unroll=2)


def steps_kernel(
    cells, props, halo_y, halo_xh, halo_xl, tables, applied, sum_z,
    moment, payload,
    m0, m1, wt, cxu, cxd, cyu, cyd, czu, czd, ks, ux, uy, uz,
):
    tabs = grain_tables([tables[r : r + 1, :] for r in range(5)])
    for c in range(3):
        m0[c, 0:WX, 0:COLS] = cells[c]
    for r, ref in enumerate((wt, ks, ux, uy, uz)):
        ref[0:WX, 0:COLS] = props[r]

    def fill(rows, cols, polar, azimuth, labels):
        start = start_cells(polar, azimuth)
        for c in range(3):
            m0[c, rows, cols] = start[c]
        labels = labels.astype(jnp.int32)
        for r, ref in enumerate((wt, ks, ux, uy, uz)):
            ref[rows, cols] = look_up(tabs[r], labels)

    def side(s, carry):
        rows = pl.ds(pl.multiple_of(s * 8, 8), 8)
        fill(rows, slice(COLS, LANES), *(strip(halo_y, s + i * (WX // 8)) for i in range(3)))
        return carry

    lax.fori_loop(0, WX // 8, side, 0, unroll=4)
    upper = iota((8, LANES), 0) < 4
    fill(
        slice(WX, ROWS),
        slice(0, LANES),
        *(
            jnp.where(upper, halo_xh[8 * i : 8 * i + 8, :], halo_xl[8 * i : 8 * i + 8, :])
            for i in range(3)
        ),
    )

    def nxt(s):
        return jnp.where(s == STRIPS - 1, 0, s + 1)

    def prv(s):
        return jnp.where(s == 0, STRIPS - 1, s - 1)

    def couplings(s, carry):
        w = strip(wt, s)
        put(cxu, s, couple(w, up(w, strip(wt, nxt(s)))))
        put(cxd, s, couple(w, down(w, strip(wt, prv(s)))))
        y = couple(w, pltpu.roll(w, LANES - NZ, 1))
        put(cyu, s, y)
        put(cyd, s, pltpu.roll(y, NZ, 1))
        lane = iota(w.shape, 1)
        depth = jnp.where(lane < COLS + 64, lane, lane - LANES + 6 * NZ + COLS) % NZ
        z = jnp.where(depth != NZ - 1, couple(w, pltpu.roll(w, LANES - 1, 1)), 0.0)
        put(czu, s, z)
        put(czd, s, pltpu.roll(z, 1, 1))
        return carry

    lax.fori_loop(0, STRIPS, couplings, 0, unroll=3)
    field = [GAIN * applied[c] for c in range(3)]

    def step(src, dst, s):
        after, before = nxt(s), prv(s)
        m = [strip(src, s, c) for c in range(3)]
        u = [strip(r, s) for r in (ux, uy, uz)]
        xu, xd, yu, yd, zu, zd = (strip(r, s) for r in (cxu, cxd, cyu, cyd, czu, czd))
        proj = strip(ks, s) * (u[0] * m[0] + u[1] * m[1] + u[2] * m[2])
        h = []
        for c in range(3):
            f = yu * (pltpu.roll(m[c], LANES - NZ, 1) - m[c])
            f = f + yd * (pltpu.roll(m[c], NZ, 1) - m[c])
            f = f + zu * (pltpu.roll(m[c], LANES - 1, 1) - m[c])
            f = f + zd * (pltpu.roll(m[c], 1, 1) - m[c])
            f = f + xu * (up(m[c], strip(src, after, c)) - m[c])
            f = f + xd * (down(m[c], strip(src, before, c)) - m[c])
            h.append(f + proj * u[c] + field[c])
        t = cross(m, h)
        d = cross(m, t)
        v = [m[c] - (t[c] + DAMPING * d[c]) for c in range(3)]
        r = lax.rsqrt(v[0] * v[0] + v[1] * v[1] + v[2] * v[2])
        for c in range(3):
            put(dst, s, v[c] * r, c)

    def one(src, dst, count, unroll):
        def body(s, carry):
            step(src, dst, s)
            return carry

        lax.fori_loop(0, count, body, 0, unroll=unroll)

    one(m0, m1, STRIPS, 3)
    one(m1, m0, STRIPS, 3)
    one(m0, m1, STRIPS, 3)
    one(m1, m0, STRIPS - 1, 4)

    for c in range(3):
        moment[c] = m0[c, 0:WX, 0:COLS]

    m = jnp.concatenate([m0[c, 0:WX, 0:COLS] for c in range(3)], axis=0)
    hi, lo = split(m)
    out = mm(hi, sum_z[...]) + mm(lo, sum_z[...])
    block = iota((16, 128), 1) // 32
    for half in range(2):
        for c in range(3):
            rows = [
                out[c * WX + 16 * g : c * WX + 16 * g + 16, half * 128 : half * 128 + 128]
                for g in range(4)
            ]
            merged = rows[3]
            for g in range(3):
                merged = jnp.where(block == (g + c) % 4, rows[g], merged)
            for peer in range(half, 16, 2):
                payload[peer * 48 + 16 * c : peer * 48 + 16 * c + 16, :] = merged


def cross(first, second):
    return [
        first[1] * second[2] - first[2] * second[1],
        first[2] * second[0] - first[0] * second[2],
        first[0] * second[1] - first[1] * second[0],
    ]


def x_kernel(pair, got, waves_hi, waves_lo, out, d_hi, d_lo):
    turn = (pair[0] * iota((8, 128), 0) + 4) % 8 - 4
    sine, cosine = sincos(turn.astype(jnp.float32) * (math.pi / 4.0))
    sine = jnp.concatenate([sine] * 2, axis=0)
    cosine = jnp.concatenate([cosine] * 2, axis=0)
    block = iota((16, 128), 1) // 32

    def unpack(source, carry):
        parts = []
        for c in range(3):
            start = pl.multiple_of(source * 48 + 16 * c, 16)
            parts.append(got[pl.ds(start, 16), :])
        for g in range(4):
            d = jnp.where(
                block == g, parts[0], jnp.where(block == (g + 1) % 4, parts[1], parts[2])
            )
            if g:
                d = pltpu.roll(d, 128 - 32 * g, 1)
            start = pl.multiple_of(source * 64 + 16 * g, 16)
            for i, factor in enumerate((cosine, sine)):
                hi, lo = split(d * factor)
                d_hi[pl.ds(start, 16), 128 * i : 128 * i + 128] = hi
                d_lo[pl.ds(start, 16), 128 * i : 128 * i + 128] = lo
        return carry

    lax.fori_loop(0, 16, unpack, 0, unroll=2)
    both = mm(waves_hi[...], d_hi[...]) + (
        mm(waves_hi[...], d_lo[...]) + mm(waves_lo[...], d_hi[...])
    )
    sign = jnp.where(iota((8, 128), 0) < 4, 1.0, -1.0)
    for t in range(32):
        rows = slice(8 * t, 8 * t + 8)
        out[rows, :] = both[rows, 0:128] + sign * pltpu.roll(both[rows, 128:256], 4, 0)


def y_kernel(
    first_row, got, waves_hi, waves_lo, twiddle, last_hi, last_lo,
    spin_flip, non_flip, flat, placed,
):
    parts = []
    for ri in range(2):
        rows = [got[pl.ds(4 * ri + low, 32, stride=8), :] for low in range(4)]
        hi, lo = split(jnp.concatenate(rows, axis=0).T[0:96, :])
        parts.append(
            mm(hi, waves_hi[...]) + (mm(lo, waves_hi[...]) + mm(hi, waves_lo[...]))
        )
    re = parts[0][:, 0:128] + parts[1][:, 128:256]
    im = parts[1][:, 0:128] - parts[0][:, 128:256]
    cosine, sine = twiddle[0:32, :], twiddle[32:64, :]
    turned = []
    for c in range(3):
        r, i = re[32 * c : 32 * c + 32, :], im[32 * c : 32 * c + 32, :]
        turned.append(
            jnp.concatenate([r * cosine + i * sine, i * cosine - r * sine], axis=0)
        )
    hi, lo = split(jnp.concatenate(turned, axis=1))
    full = mm(last_hi[...], hi) + (mm(last_hi[...], lo) + mm(last_lo[...], hi))
    lane = iota((32, 128), 1)
    kx = first_row[0] + lane // 32
    ky = iota((32, 128), 0) * 32 + lane % 32
    wave_x = jnp.where(kx < 512, kx, kx - 1024).astype(jnp.float32)
    wave_y = jnp.where(ky < 512, ky, ky - 1024).astype(jnp.float32)
    squared = wave_x * wave_x + wave_y * wave_y
    inverse = lax.rsqrt(jnp.maximum(squared, 1.0))
    unit_x = wave_x * inverse
    unit_y = wave_y * inverse
    stop = jnp.where(squared > 0.5, 1.0 / (NZ * 1024.0 * 1024.0), 0.0)
    nf = sf = 0.0
    for ri in range(2):
        sx, sy, sz = (full[32 * ri : 32 * ri + 32, 128 * c : 128 * c + 128] for c in range(3))
        along = unit_x * sx + unit_y * sy
        px = sx - unit_x * along
        py = sy - unit_y * along
        nf = nf + px * px
        sf = sf + (py * py + sz * sz)
    block = iota((8, 128), 1) // 32
    for value, dst in ((sf, spin_flip), (nf, non_flip)):
        flat[...] = value * stop
        for low in range(4):
            row = None
            for u in range(4):
                piece = flat[pl.ds(u, 8, stride=4), :]
                if u != low:
                    piece = pltpu.roll(piece, (u - low) % 4 * 32, 1)
                row = piece if row is None else jnp.where(block == u, piece, row)
            placed[pl.ds(low, 8, stride=4), :] = row
        for t in range(8):
            dst[:, 128 * t : 128 * t + 128] = placed[4 * t : 4 * t + 4, :]


def pieces(x):
    hi = x.astype(jnp.bfloat16)
    lo = (x - hi.astype(np.float64)).astype(jnp.bfloat16)
    return jnp.asarray(hi), jnp.asarray(lo)


def sum_matrix():
    y = np.arange(COLS) // NZ
    col = np.arange(256)
    return jnp.asarray(
        (y[:, None] == (col // 128 * 32 + col % 32)[None, :]).astype(jnp.bfloat16)
    )


def x_tables():
    row = np.arange(256)
    k = row // 8 * 4 + row % 4
    phase = 2.0 * np.pi * (np.outer(k, np.arange(1024)) % 1024) / 1024.0
    real = (row % 8 < 4)[:, None]
    return pieces(np.where(real, np.cos(phase), -np.sin(phase)))


def y_tables():
    lane = np.arange(128)
    block = 2 * (lane % 16) + lane % 32 // 16
    k = np.arange(128)
    phase = 2.0 * np.pi * (np.outer(block, k % 32) % 32) / 32.0
    same = (lane // 32)[:, None] == (k // 32)[None, :]
    waves = pieces(
        np.concatenate([np.where(same, np.cos(phase), 0.0), np.where(same, np.sin(phase), 0.0)], axis=1)
    )
    q = np.arange(32)
    phase = 2.0 * np.pi * np.outer(q, k % 32) / 1024.0
    twiddle = np.concatenate([np.cos(phase), np.sin(phase)]).astype(np.float32)
    phase = 2.0 * np.pi * (np.outer(q, q) % 32) / 32.0
    c, s = np.cos(phase), np.sin(phase)
    return (*waves, jnp.asarray(twiddle), *pieces(np.block([[c, s], [-s, c]])))


def f32(*shape):
    return jax.ShapeDtypeStruct(shape, jnp.float32)


def vmem(n):
    return [pl.BlockSpec(memory_space=pltpu.VMEM)] * n


def shards(polar, azimuth, grains, stiffness, anisotropy, axis_polar, axis_azimuth, applied_field):
    count_x = lax.axis_size("gx")
    count_y = lax.axis_size("gy")
    forward_x = [(i, (i + 1) % count_x) for i in range(count_x)]
    backward_x = [(t, s) for s, t in forward_x]
    forward_y = [(i, (i + 1) % count_y) for i in range(count_y)]
    backward_y = [(t, s) for s, t in forward_y]
    fields = (polar, azimuth, grains)
    first = pl.BlockSpec((WX, 128), lambda i: (0, 0))
    last = pl.BlockSpec((WX, 128), lambda i: (0, COLS // 128 - 1))
    low_edge, high_edge = pl.pallas_call(
        edges_kernel,
        grid=(1,),
        out_shape=(f32(3 * WX, 128), f32(3 * WX, 128)),
        in_specs=[first] * 3 + [last] * 3,
        out_specs=(pl.BlockSpec((3 * WX, 128), lambda i: (0, 0)),) * 2,
        name="edges",
    )(*fields, *fields)
    from_high = lax.ppermute(low_edge, "gy", backward_y)
    from_low = lax.ppermute(high_edge, "gy", forward_y)
    lane = lax.broadcasted_iota(jnp.int32, (3 * WX, 128), 1)
    halo_y = jnp.where(lane < 64, from_high, from_low)

    def edge(start):
        return jnp.concatenate(
            [
                jnp.concatenate(
                    [
                        f[start : start + 8].astype(jnp.float32),
                        halo_y[i * WX + start : i * WX + start + 8],
                    ],
                    axis=1,
                )
                for i, f in enumerate(fields)
            ],
            axis=0,
        )

    halo_xh = lax.ppermute(edge(0), "gx", backward_x)
    halo_xl = lax.ppermute(edge(WX - 8), "gx", forward_x)
    per_grain = [
        v.reshape(1, NGRAIN) for v in (stiffness, anisotropy, axis_polar, axis_azimuth)
    ]
    params = pltpu.CompilerParams(vmem_limit_bytes=32 << 20)
    cells, props, tables = pl.pallas_call(
        cells_kernel,
        out_shape=(f32(3, WX, COLS), f32(5, WX, COLS), f32(8, NGRAIN)),
        in_specs=vmem(7),
        out_specs=tuple(vmem(3)),
        compiler_params=params,
        name="cells",
    )(*fields, *per_grain)
    moment, payload = pl.pallas_call(
        steps_kernel,
        out_shape=(f32(3, WX, COLS), f32(16 * 48, 128)),
        in_specs=vmem(6) + [pl.BlockSpec(memory_space=pltpu.SMEM)] + vmem(1),
        out_specs=tuple(vmem(2)),
        scratch_shapes=[pltpu.VMEM((3, ROWS, LANES), jnp.float32)] * 2
        + [pltpu.VMEM((ROWS, LANES), jnp.float32)] * 11,
        compiler_params=params,
        name="steps",
    )(cells, props, halo_y, halo_xh, halo_xl, tables, applied_field, sum_matrix())

    columns = lax.all_to_all(
        payload.reshape(16, 48, 128), "gx", split_axis=0, concat_axis=0, tiled=True
    ).reshape(16 * 48, 128)
    at_x = lax.axis_index("gx").astype(jnp.int32)
    at_y = lax.axis_index("gy").astype(jnp.int32)
    smem = [pl.BlockSpec(memory_space=pltpu.SMEM)]
    rows = pl.pallas_call(
        x_kernel,
        out_shape=f32(256, 128),
        in_specs=smem + vmem(3),
        out_specs=vmem(1)[0],
        scratch_shapes=[pltpu.VMEM((1024, 256), jnp.bfloat16)] * 2,
        compiler_params=params,
        name="along_x",
    )((at_x // 2).reshape(1), columns, *x_tables())
    groups = [
        [gx * 16 + gy for gx in (base, base + 1) for gy in range(16)] for base in range(0, 16, 2)
    ]
    mine = lax.all_to_all(
        rows.reshape(32, 8, 128), ("gx", "gy"), split_axis=0, concat_axis=0, tiled=True,
        axis_index_groups=groups,
    ).reshape(256, 128)
    spin_flip, non_flip = pl.pallas_call(
        y_kernel,
        out_shape=(f32(4, 1024), f32(4, 1024)),
        in_specs=smem + vmem(6),
        out_specs=tuple(vmem(2)),
        scratch_shapes=[pltpu.VMEM((32, 128), jnp.float32)] * 2,
        name="along_y",
    )((at_x * WX + at_y * 4).reshape(1), mine, *y_tables())
    return (moment, spin_flip, non_flip)


def solution(mesh):
    in_specs = (P("gx", "gy"), P("gx", "gy"), P("gx", "gy"), P(), P(), P(), P(), P())
    out_specs = (P(None, "gx", "gy"), P(("gx", "gy"), None), P(("gx", "gy"), None))
    return jax.shard_map(shards, mesh=mesh, in_specs=in_specs, out_specs=out_specs, check_vma=False)
```

time: 73.2 us -> 71.8 us (0.981)
  blocking collectives: 13.3 us -> 0 us
  starting transfers between devices: 18.1 us -> 28.7 us
  waiting for transfers between devices: 19.2 us -> 24.3 us
  local copies, waits for them, and re-layouts: 3.7 us -> 1.37 us
  other arithmetic: 0.88 us -> 0.04 us
    all_to_all x1 -> x0, blocking collectives: 13.3 us -> none  [shards(): lax.all_to_all(payload.reshape(16, 8, 128), 'gx', split_axis=0, concat_ax...]
    all_to_all x1 -> x2, starting transfers between devices: 8.31 us -> 18.8 us  [the longest x1 15.1 us: shards(): lax.all_to_all(rows.reshape(32, 8, 128), ('gx', 'gy'), split_axis=0, conc...]
    all_to_all x1 -> x2, waiting for transfers between devices: 13.1 us -> 17.5 us  [the longest x1 9.08 us: shards(): lax.all_to_all(payload.reshape(16, 48, 128), 'gx', split_axis=0, concat_a...]
    ppermute x1, starting transfers between devices: 4.21 us -> 0.9 us  [shards(): from_low = lax.ppermute(high_edge, 'gy', forward_y)]
    ppermute x1, starting transfers between devices: 0.08 us -> 3.24 us  [shards(): from_high = lax.ppermute(low_edge, 'gy', backward_y)]
    ppermute x1, waiting for transfers between devices: 4.26 us -> 2.45 us  [shards(): from_high = lax.ppermute(low_edge, 'gy', backward_y)]
    ppermute x1, waiting for transfers between devices: 1.82 us -> 3.59 us  [shards(): halo_xl = lax.ppermute(edge(WX - 8), 'gx', forward_x)]
    ppermute x1, starting transfers between devices: 4.07 us -> 5.75 us  [shards(): halo_xh = lax.ppermute(edge(0), 'gx', backward_x)]
  transfers between devices with their start and end apart: 5 -> 6, of which waited for: 3 -> 5; matrix products, arithmetic and copies ran while one was open for 0% -> 0% of each run, Pallas kernels for 0% -> 2%
where the time goes in v1:
time: 71.8 us; the launch traced here: 71.5 us
  starting transfers between devices  28.7 us (40%)
  waiting for transfers between devices  24.3 us (34%)
  Pallas kernels  16.2 us (23%)
  local copies, waits for them, and re-layouts  1.37 us (2%)
  between operations  0.85 us (1%)
    all_to_all x1, starting transfers between devices, shards(): lax.all_to_all(rows.reshape(32, 8, 128), ('gx', 'gy'), split_axis=0, conc...  15.1 us
    all_to_all x1, waiting for transfers between devices, shards(): lax.all_to_all(payload.reshape(16, 48, 128), 'gx', split_axis=0, concat_a...  9.08 us
    pallas_call x1, Pallas kernels, shards(): pl.pallas_call(steps_kernel, out_shape=(f32(3, WX, COLS), f32(16 * 48, 12...  8.65 us
    all_to_all x1, waiting for transfers between devices, shards(): lax.all_to_all(rows.reshape(32, 8, 128), ('gx', 'gy'), split_axis=0, conc...  8.41 us
    ppermute x1, starting transfers between devices, shards(): halo_xh = lax.ppermute(edge(0), 'gx', backward_x)  5.75 us
    all_to_all x1, starting transfers between devices, shards(): lax.all_to_all(payload.reshape(16, 48, 128), 'gx', split_axis=0, concat_a...  3.68 us
    ppermute x1, waiting for transfers between devices, shards(): halo_xl = lax.ppermute(edge(WX - 8), 'gx', forward_x)  3.59 us
    ppermute x1, starting transfers between devices, shards(): from_high = lax.ppermute(low_edge, 'gy', backward_y)  3.24 us
  transfers between devices with their start and end apart: 6, of which 5 were waited for; matrix products, arithmetic and copies ran while one was open for 0% of the time, Pallas kernels for 2%

profile of v1, /device:TPU:1, one launch (start us, length us, event | category | flops | bytes accessed | tf_op | source)
XLA Modules:
  0.0 71.5 jit_solution(9143661767606554949)
XLA Ops:
  0.6 0.0 copy-start
  0.6 0.0 copy-start.1
  0.7 0.0 copy-start.2
  0.7 1.6 %edges.1 = (f32[192,128]{1,0:T(8,128)}, f32[192,128]{1,0:T(8,128)}) custom-call(f32[64,768]{1,0:T(8,128)} %p_high.1, f32[64,768]{1,0:T(8,128)} %a_high.1, s32[64,768]{1,0:T(8,128)} %g_high.1, f32[64,768]{1,0:T(8,128)} %p_high.1, f32[64,768]{1,0:T(8,128)} %a_high.1, s32[64,768]{1,0:T(8,128)} %g_high.1), custom_call_target="tpu_custom_call" | custom-call | tf_op jit(solution)/shard_map/edges/pallas_call | solution.py:411
  2.2 3.2 %collective-permute-start = (f32[192,128]{1,0:T(8,128)}, f32[192,128]{1,0:T(8,128)S(1)}, u32[]{:S(2)}, u32[]{:S(2)}) collective-permute-start(f32[192,128]{1,0:T(8,128)} %get-tuple-element.14), channel_id=1, source_target_pairs={{1,0},{2,1},{3,2},{4,3},{5,4},{6,5},{7,6},{8,7},{9,8},{10,9},{11,1... | collective-permute-start | bytes 294920 | tf_op jit(solution)/shard_map/ppermute | solution.py:419
  5.5 0.9 %collective-permute-start.1 = (f32[192,128]{1,0:T(8,128)}, f32[192,128]{1,0:T(8,128)S(1)}, u32[]{:S(2)}, u32[]{:S(2)}) collective-permute-start(f32[192,128]{1,0:T(8,128)} %get-tuple-element.15), channel_id=1, source_target_pairs={{0,1},{1,2},{2,3},{3,4},{4,5},{5,6},{6,7},{7,8},{8,9},{9,10},{10,1... | collective-permute-start | bytes 294920 | tf_op jit(solution)/shard_map/ppermute | solution.py:420
  6.4 0.0 copy-done.2
  6.4 0.0 copy-done
  6.4 0.0 copy-done.1
  6.4 2.4 %collective-permute-done = f32[192,128]{1,0:T(8,128)S(1)} collective-permute-done((f32[192,128]{1,0:T(8,128)}, f32[192,128]{1,0:T(8,128)S(1)}, u32[]{:S(2)}, u32[]{:S(2)}) %collective-permute-start) | collective-permute-done | bytes 98336 | tf_op jit(solution)/shard_map/ppermute | solution.py:419
  8.9 0.8 %collective-permute-done.1 = f32[192,128]{1,0:T(8,128)S(1)} collective-permute-done((f32[192,128]{1,0:T(8,128)}, f32[192,128]{1,0:T(8,128)S(1)}, u32[]{:S(2)}, u32[]{:S(2)}) %collective-permute-start.1) | collective-permute-done | bytes 98336 | tf_op jit(solution)/shard_map/ppermute | solution.py:420
  9.7 0.0 copy-start.6
  9.7 0.0 copy-start.7
  9.7 0.0 copy-start.8
  9.7 0.0 copy-start.9
  9.8 5.7 %collective-permute-start.2 = (f32[24,896]{1,0:T(8,128)S(1)}, f32[24,896]{1,0:T(8,128)S(1)}, u32[]{:S(2)}, u32[]{:S(2)}) collective-permute-start(f32[24,896]{1,0:T(8,128)S(1)} %maximum_maximum_fusion), channel_id=1, source_target_pairs={{16,0},{32,16},{48,32},{64,48},{80,64},{96,80},{112,96},{128,112},... | collective-permute-start | bytes 258056 | tf_op jit(solution)/shard_map/ppermute | solution.py:439
  15.5 0.0 copy-start.5
  15.5 0.1 collective-permute-start.3
  15.6 0.0 copy-done.6
  15.6 0.0 copy-done.7
  15.6 0.0 copy-done.8
  15.6 0.0 copy-done.9
  15.7 1.8 %cells.1 = (f32[3,64,768]{2,1,0:T(8,128)S(1)}, f32[5,64,768]{2,1,0:T(8,128)S(1)}, f32[8,256]{1,0:T(8,128)S(1)}) custom-call(f32[64,768]{1,0:T(8,128)S(1)} %copy-done, f32[64,768]{1,0:T(8,128)S(1)} %copy-done.1, s32[64,768]{1,0:T(8,128)S(1)} %copy-done.2, f32[1,256]{1,0:T(1,128)S(1)} %bitcast.11, f32[1,256]{1,0:T(1,128)S(1)} %bitcast.12, ...), custom_call_target="tpu_custom_call" | custom-call | tf_op jit(solution)/shard_map/cells/pallas_call | solution.py:445
  17.4 0.0 collective-permute-done.2.halo_xh
  17.5 3.6 %collective-permute-done.3.halo_xl = f32[24,896]{1,0:T(8,128)S(1)} collective-permute-done((f32[24,896]{1,0:T(8,128)S(1)}, f32[24,896]{1,0:T(8,128)S(1)}, u32[]{:S(2)}, u32[]{:S(2)}) %collective-permute-start.3) | collective-permute-done | bytes 86048 | tf_op jit(solution)/shard_map/ppermute | solution.py:440
  21.0 0.0 copy-start.10
  21.0 0.0 copy-done.5
  21.1 0.7 copy-done.10
  21.7 0.0 copy-start.4
  21.7 8.6 %steps.1 = (f32[3,64,768]{2,1,0:T(8,128)}, f32[768,128]{1,0:T(8,128)}) custom-call(f32[3,64,768]{2,1,0:T(8,128)S(1)} %get-tuple-element.12.cells, f32[5,64,768]{2,1,0:T(8,128)S(1)} %get-tuple-element.13.props, f32[192,128]{1,0:T(8,128)S(1)} %broadcast_select_fusion.halo_y, f32[24,896]{1,0:T(8,128)S(1)} %collective-permute-done.2.halo_xh, ...), custom_call_target="tpu_custom_call" | custom-call | tf_op jit(solution)/shard_map/steps/pallas_call | solution.py:453
  30.4 0.0 copy-start.3
  30.4 3.7 %all-to-all-start = ((f32[16,48,128]{2,1,0:T(8,128)}), f32[16,48,128]{2,1,0:T(8,128)S(1)}, u32[]{:S(2)}, u32[]{:S(2)}) async-start(f32[16,48,128]{2,1,0:T(8,128)} %bitcast.6), calls=%async_computation | async-start | bytes 786432 | tf_op jit(solution)/shard_map/all_to_all | solution.py:464
  34.1 9.1 %all-to-all-done = f32[16,48,128]{2,1,0:T(8,128)S(1)} async-done(((f32[16,48,128]{2,1,0:T(8,128)}), f32[16,48,128]{2,1,0:T(8,128)S(1)}, u32[]{:S(2)}, u32[]{:S(2)}) %all-to-all-start) | async-done | bytes 393248 | tf_op jit(solution)/shard_map/all_to_all | solution.py:464
  43.1 0.0 copy-done.4
  43.1 0.0 copy-done.3
  43.2 2.0 %along_x.1 = f32[256,128]{1,0:T(8,128)} custom-call(s32[1]{0:T(128)} %bitcast.5.pair, f32[768,128]{1,0:T(8,128)S(1)} %bitcast.10, bf16[256,1024]{1,0:T(8,128)(2,1)S(1)} %copy-done.3, bf16[256,1024]{1,0:T(8,128)(2,1)S(1)} %copy-done.4), custom_call_target="tpu_custom_call" | custom-call | tf_op jit(solution)/shard_map/along_x/pallas_call | solution.py:470
  45.2 15.1 %all-to-all-start.1 = ((f32[32,8,128]{2,1,0:T(8,128)}), f32[32,8,128]{2,1,0:T(8,128)S(1)}, u32[]{:S(2)}, u32[]{:S(2)}) async-start(f32[32,8,128]{2,1,0:T(8,128)} %bitcast.8), calls=%async_computation.1 | async-start | bytes 262144 | tf_op jit(solution)/shard_map/all_to_all | solution.py:482
  60.3 8.4 %all-to-all-done.1 = f32[32,8,128]{2,1,0:T(8,128)S(1)} async-done(((f32[32,8,128]{2,1,0:T(8,128)}), f32[32,8,128]{2,1,0:T(8,128)S(1)}, u32[]{:S(2)}, u32[]{:S(2)}) %all-to-all-start.1) | async-done | bytes 131104 | tf_op jit(solution)/shard_map/all_to_all | solution.py:482
  68.7 0.0 copy-start.11
  68.7 0.7 copy-done.11
  69.3 2.1 %along_y.1 = (f32[4,1024]{1,0:T(4,128)}, f32[4,1024]{1,0:T(4,128)}) custom-call(s32[1]{0:T(128)} %bitcast.4.first_row, f32[256,128]{1,0:T(8,128)} %bitcast.15, bf16[128,256]{1,0:T(8,128)(2,1)} %constant.45.clone.waves_hi, bf16[128,256]{1,0:T(8,128)(2,1)} %constant.46.clone.waves_lo, f32[64,128]{1,0:T(8,128)} %constant.47.clone.twiddle, ...), custom_call_target="tpu_custom_call" | custom-call | tf_op jit(solution)/shard_map/along_y/pallas_call | solution.py:486
  (7 shorter events, 0.1 us)
Async XLA Ops:
  0.6 5.8 %copy-start = (f32[64,768]{1,0:T(8,128)S(1)}, f32[64,768]{1,0:T(8,128)}, u32[]{:S(2)}) copy-start(f32[64,768]{1,0:T(8,128)} %p_high.1) | copy-start | bytes 589828
  0.6 5.8 %copy-start.1 = (f32[64,768]{1,0:T(8,128)S(1)}, f32[64,768]{1,0:T(8,128)}, u32[]{:S(2)}) copy-start(f32[64,768]{1,0:T(8,128)} %a_high.1) | copy-start | bytes 589828
  0.7 5.7 %copy-start.2 = (s32[64,768]{1,0:T(8,128)S(1)}, s32[64,768]{1,0:T(8,128)}, u32[]{:S(2)}) copy-start(s32[64,768]{1,0:T(8,128)} %g_high.1) | copy-start | bytes 589828
  2.2 6.6 %collective-permute-start = (f32[192,128]{1,0:T(8,128)}, f32[192,128]{1,0:T(8,128)S(1)}, u32[]{:S(2)}, u32[]{:S(2)}) collective-permute-start(f32[192,128]{1,0:T(8,128)} %get-tuple-element.14), channel_id=1, source_target_pairs={{1,0},{2,1},{3,2},{4,3},{5,4},{6,5},{7,6},{8,7},{9,8},{10,9},{11,1... | collective-permute-start | bytes 294920 | tf_op jit(solution)/shard_map/ppermute | solution.py:419
  5.5 4.2 %collective-permute-start.1 = (f32[192,128]{1,0:T(8,128)}, f32[192,128]{1,0:T(8,128)S(1)}, u32[]{:S(2)}, u32[]{:S(2)}) collective-permute-start(f32[192,128]{1,0:T(8,128)} %get-tuple-element.15), channel_id=1, source_target_pairs={{0,1},{1,2},{2,3},{3,4},{4,5},{5,6},{6,7},{7,8},{8,9},{9,10},{10,1... | collective-permute-start | bytes 294920 | tf_op jit(solution)/shard_map/ppermute | solution.py:420
  9.7 5.9 %copy-start.6 = (f32[256]{0:T(256)S(1)}, f32[256]{0:T(256)}, u32[]{:S(2)}) copy-start(f32[256]{0:T(256)} %param.19) | copy-start | bytes 3076
  9.7 5.9 %copy-start.7 = (f32[256]{0:T(256)S(1)}, f32[256]{0:T(256)}, u32[]{:S(2)}) copy-start(f32[256]{0:T(256)} %param.20) | copy-start | bytes 3076
  9.7 5.9 %copy-start.8 = (f32[256]{0:T(256)S(1)}, f32[256]{0:T(256)}, u32[]{:S(2)}) copy-start(f32[256]{0:T(256)} %param.21) | copy-start | bytes 3076
  9.7 5.9 %copy-start.9 = (f32[256]{0:T(256)S(1)}, f32[256]{0:T(256)}, u32[]{:S(2)}) copy-start(f32[256]{0:T(256)} %param.22) | copy-start | bytes 3076
  9.8 7.7 %collective-permute-start.2 = (f32[24,896]{1,0:T(8,128)S(1)}, f32[24,896]{1,0:T(8,128)S(1)}, u32[]{:S(2)}, u32[]{:S(2)}) collective-permute-start(f32[24,896]{1,0:T(8,128)S(1)} %maximum_maximum_fusion), channel_id=1, source_target_pairs={{16,0},{32,16},{48,32},{64,48},{80,64},{96,80},{112,96},{128,112},... | collective-permute-start | bytes 258056 | tf_op jit(solution)/shard_map/ppermute | solution.py:439
  15.5 5.5 %copy-start.5 = (bf16[768,256]{1,0:T(8,128)(2,1)S(1)}, bf16[768,256]{1,0:T(8,128)(2,1)}, u32[]{:S(2)}) copy-start(bf16[768,256]{1,0:T(8,128)(2,1)} %constant.42.clone.sum_z) | copy-start | bytes 1179652
  15.5 5.5 %collective-permute-start.3 = (f32[24,896]{1,0:T(8,128)S(1)}, f32[24,896]{1,0:T(8,128)S(1)}, u32[]{:S(2)}, u32[]{:S(2)}) collective-permute-start(f32[24,896]{1,0:T(8,128)S(1)} %maximum_maximum_fusion.1), channel_id=1, source_target_pairs={{0,16},{16,32},{32,48},{48,64},{64,80},{80,96},{96,112},{112,128},... | collective-permute-start | bytes 258056 | tf_op jit(solution)/shard_map/ppermute | solution.py:440
  21.0 0.7 copy-start.10
  21.7 21.4 %copy-start.4 = (bf16[256,1024]{1,0:T(8,128)(2,1)S(1)}, bf16[256,1024]{1,0:T(8,128)(2,1)}, u32[]{:S(2)}) copy-start(bf16[256,1024]{1,0:T(8,128)(2,1)} %constant.44.clone.waves_lo) | copy-start | bytes 1572868
  30.4 12.8 %copy-start.3 = (bf16[256,1024]{1,0:T(8,128)(2,1)S(1)}, bf16[256,1024]{1,0:T(8,128)(2,1)}, u32[]{:S(2)}) copy-start(bf16[256,1024]{1,0:T(8,128)(2,1)} %constant.43.clone.waves_hi) | copy-start | bytes 1572868
  30.4 12.8 %all-to-all-start = ((f32[16,48,128]{2,1,0:T(8,128)}), f32[16,48,128]{2,1,0:T(8,128)S(1)}, u32[]{:S(2)}, u32[]{:S(2)}) async-start(f32[16,48,128]{2,1,0:T(8,128)} %bitcast.6), calls=%async_computation | async-start | bytes 786432 | tf_op jit(solution)/shard_map/all_to_all | solution.py:464
  45.2 23.5 %all-to-all-start.1 = ((f32[32,8,128]{2,1,0:T(8,128)}), f32[32,8,128]{2,1,0:T(8,128)S(1)}, u32[]{:S(2)}, u32[]{:S(2)}) async-start(f32[32,8,128]{2,1,0:T(8,128)} %bitcast.8), calls=%async_computation.1 | async-start | bytes 262144 | tf_op jit(solution)/shard_map/all_to_all | solution.py:482
  68.7 0.7 copy-start.11

commit v2 on v1

--- a/solution.py
+++ b/solution.py
@@ -115,18 +115,30 @@
 
 
 def edges_kernel(p_low, a_low, g_low, p_high, a_high, g_high, low, high):
-    for dst, refs in ((low, (p_low, a_low, g_low)), (high, (p_high, a_high, g_high))):
-        for i, ref in enumerate(refs):
-            dst[i * WX : (i + 1) * WX, :] = ref[...].astype(jnp.float32)
+    half = WX // 2
+    lane = iota((half, 128), 1)
+    for i, src in enumerate((p_low, a_low, g_low)):
+        v = src[...].astype(jnp.float32)
+        low[i * half : (i + 1) * half, :] = jnp.where(
+            lane < 48, v[0:half, :], pltpu.roll(v[half:WX, :], 48, 1)
+        )
+    for i, src in enumerate((p_high, a_high, g_high)):
+        v = src[...].astype(jnp.float32)
+        high[i * half : (i + 1) * half, :] = jnp.where(
+            lane >= 80, v[0:half, :], pltpu.roll(v[half:WX, :], 80, 1)
+        )
 
 
 def cells_kernel(
-    polar, azimuth, grains, stiffness, anisotropy, axis_polar, axis_azimuth, cells, props, tables
+    polar, azimuth, grains, stiffness, anisotropy, axis_polar, axis_azimuth, applied,
+    cells, props, tables,
 ):
     ax, ay, az = start_cells(axis_polar[...], axis_azimuth[...])
     rows = [stiffness[...], GAIN * anisotropy[...], ax, ay, az]
     for r, row in enumerate(rows):
         tables[r : r + 1, :] = row
+    for c in range(3):
+        tables[5 + c : 6 + c, :] = jnp.full((1, NGRAIN), GAIN * applied[c])
     tabs = grain_tables(rows)
 
     def body(s, carry):
@@ -142,9 +154,9 @@
 
 
 def steps_kernel(
-    cells, props, halo_y, halo_xh, halo_xl, tables, applied, sum_z,
+    cells, props, from_high, from_low, halo_xh, halo_xl, tables, sum_z,
     moment, payload,
-    m0, m1, wt, cxu, cxd, cyu, cyd, czu, czd, ks, ux, uy, uz,
+    m0, m1, wt, cxu, cxd, cyu, cyd, czu, czd, ks, ux, uy, uz, raw,
 ):
     tabs = grain_tables([tables[r : r + 1, :] for r in range(5)])
     for c in range(3):
@@ -160,21 +172,30 @@
         for r, ref in enumerate((wt, ks, ux, uy, uz)):
             ref[rows, cols] = look_up(tabs[r], labels)
 
-    def side(s, carry):
-        rows = pl.ds(pl.multiple_of(s * 8, 8), 8)
-        fill(rows, slice(COLS, LANES), *(strip(halo_y, s + i * (WX // 8)) for i in range(3)))
-        return carry
-
-    lax.fori_loop(0, WX // 8, side, 0, unroll=4)
-    upper = iota((8, LANES), 0) < 4
-    fill(
-        slice(WX, ROWS),
-        slice(0, LANES),
-        *(
-            jnp.where(upper, halo_xh[8 * i : 8 * i + 8, :], halo_xl[8 * i : 8 * i + 8, :])
-            for i in range(3)
-        ),
-    )
+    near = iota((8, 128), 1) < 64
+
+    def side(bottom):
+        def body(s, carry):
+            values = []
+            for i in range(3):
+                high = strip(from_high, s + i * (WX // 16))
+                low = strip(from_low, s + i * (WX // 16))
+                if bottom:
+                    high, low = pltpu.roll(high, 80, 1), pltpu.roll(low, 48, 1)
+                values.append(jnp.where(near, high, low))
+            start = s + (WX // 16 if bottom else 0)
+            rows = pl.ds(pl.multiple_of(start * 8, 8), 8)
+            fill(rows, slice(COLS, LANES), *values)
+            return carry
+
+        lax.fori_loop(0, WX // 16, body, 0, unroll=4)
+
+    side(False)
+    side(True)
+    for i in range(3):
+        raw[i, 0:4, :] = halo_xh[i]
+        raw[i, 4:8, :] = halo_xl[i]
+    fill(slice(WX, ROWS), slice(0, LANES), raw[0], raw[1], raw[2])
 
     def nxt(s):
         return jnp.where(s == STRIPS - 1, 0, s + 1)
@@ -197,7 +218,7 @@
         return carry
 
     lax.fori_loop(0, STRIPS, couplings, 0, unroll=3)
-    field = [GAIN * applied[c] for c in range(3)]
+    field = [jnp.broadcast_to(tables[5 + c : 6 + c, 0:1], (8, LANES)) for c in range(3)]
 
     def step(src, dst, s):
         after, before = nxt(s), prv(s)
@@ -406,67 +427,69 @@
     forward_y = [(i, (i + 1) % count_y) for i in range(count_y)]
     backward_y = [(t, s) for s, t in forward_y]
     fields = (polar, azimuth, grains)
+    params = pltpu.CompilerParams(vmem_limit_bytes=32 << 20)
+    smem = [pl.BlockSpec(memory_space=pltpu.SMEM)]
     first = pl.BlockSpec((WX, 128), lambda i: (0, 0))
     last = pl.BlockSpec((WX, 128), lambda i: (0, COLS // 128 - 1))
     low_edge, high_edge = pl.pallas_call(
         edges_kernel,
         grid=(1,),
-        out_shape=(f32(3 * WX, 128), f32(3 * WX, 128)),
+        out_shape=(f32(3 * WX // 2, 128), f32(3 * WX // 2, 128)),
         in_specs=[first] * 3 + [last] * 3,
-        out_specs=(pl.BlockSpec((3 * WX, 128), lambda i: (0, 0)),) * 2,
+        out_specs=tuple(vmem(2)),
         name="edges",
     )(*fields, *fields)
     from_high = lax.ppermute(low_edge, "gy", backward_y)
     from_low = lax.ppermute(high_edge, "gy", forward_y)
-    lane = lax.broadcasted_iota(jnp.int32, (3 * WX, 128), 1)
-    halo_y = jnp.where(lane < 64, from_high, from_low)
-
-    def edge(start):
-        return jnp.concatenate(
-            [
+
+    def edge(start, row, high, low):
+        blank = jnp.zeros((4, 32), jnp.float32)
+        parts = []
+        for i, f in enumerate(fields):
+            halo = slice(i * WX // 2 + row, i * WX // 2 + row + 4)
+            parts.append(
                 jnp.concatenate(
                     [
-                        f[start : start + 8].astype(jnp.float32),
-                        halo_y[i * WX + start : i * WX + start + 8],
+                        f[start : start + 4].astype(jnp.float32),
+                        from_high[halo, high : high + 48],
+                        blank,
+                        from_low[halo, low : low + 48],
                     ],
                     axis=1,
                 )
-                for i, f in enumerate(fields)
-            ],
-            axis=0,
-        )
-
-    halo_xh = lax.ppermute(edge(0), "gx", backward_x)
-    halo_xl = lax.ppermute(edge(WX - 8), "gx", forward_x)
+            )
+        return jnp.stack(parts)
+
+    halo_xh = lax.ppermute(edge(0, 0, 0, 80), "gx", backward_x)
+    halo_xl = lax.ppermute(edge(WX - 4, WX // 2 - 4, 48, 32), "gx", forward_x)
     per_grain = [
         v.reshape(1, NGRAIN) for v in (stiffness, anisotropy, axis_polar, axis_azimuth)
     ]
-    params = pltpu.CompilerParams(vmem_limit_bytes=32 << 20)
     cells, props, tables = pl.pallas_call(
         cells_kernel,
         out_shape=(f32(3, WX, COLS), f32(5, WX, COLS), f32(8, NGRAIN)),
-        in_specs=vmem(7),
+        in_specs=vmem(7) + smem,
         out_specs=tuple(vmem(3)),
         compiler_params=params,
         name="cells",
-    )(*fields, *per_grain)
+    )(*fields, *per_grain, applied_field)
     moment, payload = pl.pallas_call(
         steps_kernel,
         out_shape=(f32(3, WX, COLS), f32(16 * 48, 128)),
-        in_specs=vmem(6) + [pl.BlockSpec(memory_space=pltpu.SMEM)] + vmem(1),
+        in_specs=vmem(8),
         out_specs=tuple(vmem(2)),
         scratch_shapes=[pltpu.VMEM((3, ROWS, LANES), jnp.float32)] * 2
-        + [pltpu.VMEM((ROWS, LANES), jnp.float32)] * 11,
+        + [pltpu.VMEM((ROWS, LANES), jnp.float32)] * 11
+        + [pltpu.VMEM((3, 8, LANES), jnp.float32)],
         compiler_params=params,
         name="steps",
-    )(cells, props, halo_y, halo_xh, halo_xl, tables, applied_field, sum_matrix())
+    )(cells, props, from_high, from_low, halo_xh, halo_xl, tables, sum_matrix())
 
     columns = lax.all_to_all(
         payload.reshape(16, 48, 128), "gx", split_axis=0, concat_axis=0, tiled=True
     ).reshape(16 * 48, 128)
     at_x = lax.axis_index("gx").astype(jnp.int32)
     at_y = lax.axis_index("gy").astype(jnp.int32)
-    smem = [pl.BlockSpec(memory_space=pltpu.SMEM)]
     rows = pl.pallas_call(
         x_kernel,
         out_shape=f32(256, 128),
@@ -489,6 +512,7 @@
         in_specs=smem + vmem(6),
         out_specs=tuple(vmem(2)),
         scratch_shapes=[pltpu.VMEM((32, 128), jnp.float32)] * 2,
+        compiler_params=params,
         name="along_y",
     )((at_x * WX + at_y * 4).reshape(1), mine, *y_tables())
     return (moment, spin_flip, non_flip)

time: 71.8 us -> 67 us (0.933)
  waiting for transfers between devices: 24.3 us -> 20.6 us
  local copies, waits for them, and re-layouts: 1.37 us -> 0.31 us
  starting transfers between devices: 28.7 us -> 29.6 us
  Pallas kernels: 16.2 us -> 15.3 us
    ppermute x2, waiting for transfers between devices: 3.59 us -> 0.01 us  [the longest x1 0.01 us: shards(): halo_xl = lax.ppermute(edge(WX - 4, WX // 2 - 4, 48, 32), 'gx', forward_x)]
    all_to_all x1, starting transfers between devices: 3.68 us -> 5.5 us  [shards(): lax.all_to_all(payload.reshape(16, 48, 128), 'gx', split_axis=0, concat_a...]
    unnamed x24 -> x32, local copies, waits for them, and re-layouts: 1.35 us -> 0.07 us
    pallas_call x1, Pallas kernels: 2.15 us -> 1.18 us  [shards(): pl.pallas_call(y_kernel, out_shape=(f32(4, 1024), f32(4, 1024)), in_specs...]
    all_to_all x1, starting transfers between devices: 15.1 us -> 14.2 us  [shards(): lax.all_to_all(rows.reshape(32, 8, 128), ('gx', 'gy'), split_axis=0, conc...]
  transfers between devices with their start and end apart: 6 -> 6, of which waited for: 5 -> 4; matrix products, arithmetic and copies ran while one was open for 0% -> 0% of each run, Pallas kernels for 2% -> 3%
where the time goes in v2:
time: 67 us; the launch traced here: 66.7 us
  starting transfers between devices  29.6 us (44%)
  waiting for transfers between devices  20.6 us (31%)
  Pallas kernels  15.3 us (23%)
  between operations  0.85 us (1%)
    all_to_all x1, starting transfers between devices, shards(): lax.all_to_all(rows.reshape(32, 8, 128), ('gx', 'gy'), split_axis=0, conc...  14.2 us
    all_to_all x1, waiting for transfers between devices, shards(): lax.all_to_all(payload.reshape(16, 48, 128), 'gx', split_axis=0, concat_a...  9.15 us
    all_to_all x1, waiting for transfers between devices, shards(): lax.all_to_all(rows.reshape(32, 8, 128), ('gx', 'gy'), split_axis=0, conc...  8.41 us
    pallas_call x1, Pallas kernels, shards(): pl.pallas_call(steps_kernel, out_shape=(f32(3, WX, COLS), f32(16 * 48, 12...  8.15 us
    all_to_all x1, starting transfers between devices, shards(): lax.all_to_all(payload.reshape(16, 48, 128), 'gx', split_axis=0, concat_a...  5.5 us
    ppermute x1, starting transfers between devices, shards(): halo_xh = lax.ppermute(edge(0, 0, 0, 80), 'gx', backward_x)  4.06 us
    ppermute x1, starting transfers between devices, shards(): from_high = lax.ppermute(low_edge, 'gy', backward_y)  3.24 us
    pallas_call x1, Pallas kernels, shards(): pl.pallas_call(cells_kernel, out_shape=(f32(3, WX, COLS), f32(5, WX, COLS...  2.32 us
  transfers between devices with their start and end apart: 6, of which 4 were waited for; matrix products, arithmetic and copies ran while one was open for 0% of the time, Pallas kernels for 3%

profile of v2, /device:TPU:1, one launch (start us, length us, event | category | flops | bytes accessed | tf_op | source)
XLA Modules:
  0.0 66.7 jit_solution(6437466742180202453)
XLA Ops:
  0.6 0.0 copy-start
  0.6 0.0 copy-start.1
  0.7 0.0 copy-start.2
  0.7 1.6 %edges.1 = (f32[96,128]{1,0:T(8,128)}, f32[96,128]{1,0:T(8,128)}) custom-call(f32[64,768]{1,0:T(8,128)} %p_high.1, f32[64,768]{1,0:T(8,128)} %a_high.1, s32[64,768]{1,0:T(8,128)} %g_high.1, f32[64,768]{1,0:T(8,128)} %p_high.1, f32[64,768]{1,0:T(8,128)} %a_high.1, s32[64,768]{1,0:T(8,128)} %g_high.1), custom_call_target="tpu_custom_call" | custom-call | tf_op jit(solution)/shard_map/edges/pallas_call | solution.py:434
  2.3 3.2 %collective-permute-start = (f32[96,128]{1,0:T(8,128)}, f32[96,128]{1,0:T(8,128)S(1)}, u32[]{:S(2)}, u32[]{:S(2)}) collective-permute-start(f32[96,128]{1,0:T(8,128)} %get-tuple-element.14), channel_id=1, source_target_pairs={{1,0},{2,1},{3,2},{4,3},{5,4},{6,5},{7,6},{8,7},{9,8},{10,9},{11,1... | collective-permute-start | bytes 147464 | tf_op jit(solution)/shard_map/ppermute | solution.py:442
  5.5 0.9 %collective-permute-start.1 = (f32[96,128]{1,0:T(8,128)}, f32[96,128]{1,0:T(8,128)S(1)}, u32[]{:S(2)}, u32[]{:S(2)}) collective-permute-start(f32[96,128]{1,0:T(8,128)} %get-tuple-element.15), channel_id=1, source_target_pairs={{0,1},{1,2},{2,3},{3,4},{4,5},{5,6},{6,7},{7,8},{8,9},{9,10},{10,1... | collective-permute-start | bytes 147464 | tf_op jit(solution)/shard_map/ppermute | solution.py:443
  6.4 0.0 copy-done
  6.4 0.0 copy-done.1
  6.4 0.0 copy-done.2
  6.5 0.1 pad.28.clone
  6.5 1.8 %collective-permute-done.from_high = f32[96,128]{1,0:T(8,128)S(1)} collective-permute-done((f32[96,128]{1,0:T(8,128)}, f32[96,128]{1,0:T(8,128)S(1)}, u32[]{:S(2)}, u32[]{:S(2)}) %collective-permute-start) | collective-permute-done | bytes 49184 | tf_op jit(solution)/shard_map/ppermute | solution.py:442
  8.4 0.1 fusion.2
  8.5 1.2 %collective-permute-done.1.from_low = f32[96,128]{1,0:T(8,128)S(1)} collective-permute-done((f32[96,128]{1,0:T(8,128)}, f32[96,128]{1,0:T(8,128)S(1)}, u32[]{:S(2)}, u32[]{:S(2)}) %collective-permute-start.1) | collective-permute-done | bytes 49184 | tf_op jit(solution)/shard_map/ppermute | solution.py:443
  9.6 0.1 fusion.3
  9.7 0.0 copy-start.11
  9.7 0.0 copy-start.13
  9.7 0.0 copy-start.14
  9.7 0.0 copy-start.15
  9.7 0.1 maximum_bitcast_fusion.3
  9.8 0.0 copy-start.5
  9.8 1.7 %collective-permute-start.3 = (f32[3,4,896]{2,1,0:T(4,128)S(1)}, f32[3,4,896]{2,1,0:T(4,128)S(1)}, u32[]{:S(2)}, u32[]{:S(2)}) collective-permute-start(f32[3,4,896]{2,1,0:T(4,128)S(1)} %pad_maximum_fusion.1), channel_id=1, source_target_pairs={{0,16},{16,32},{32,48},{48,64},{64,80},{80,96},{96,112},{112,128},... | collective-permute-start | bytes 129032 | tf_op jit(solution)/shard_map/ppermute | solution.py:464
  11.6 4.1 %collective-permute-start.2 = (f32[3,4,896]{2,1,0:T(4,128)S(1)}, f32[3,4,896]{2,1,0:T(4,128)S(1)}, u32[]{:S(2)}, u32[]{:S(2)}) collective-permute-start(f32[3,4,896]{2,1,0:T(4,128)S(1)} %pad_maximum_fusion), channel_id=1, source_target_pairs={{16,0},{32,16},{48,32},{64,48},{80,64},{96,80},{112,96},{128,112},... | collective-permute-start | bytes 129032 | tf_op jit(solution)/shard_map/ppermute | solution.py:463
  15.6 0.0 copy-done.11
  15.6 0.0 copy-done.12
  15.6 0.0 copy-done.13
  15.6 0.0 copy-done.14
  15.7 0.0 copy-done.15
  15.7 2.3 %cells.1 = (f32[3,64,768]{2,1,0:T(8,128)S(1)}, f32[5,64,768]{2,1,0:T(8,128)S(1)}, f32[8,256]{1,0:T(8,128)S(1)}) custom-call(f32[64,768]{1,0:T(8,128)S(1)} %copy-done, f32[64,768]{1,0:T(8,128)S(1)} %copy-done.1, s32[64,768]{1,0:T(8,128)S(1)} %copy-done.2, f32[1,256]{1,0:T(1,128)S(1)} %bitcast.24, f32[1,256]{1,0:T(1,128)S(1)} %bitcast.25, ...), custom_call_target="tpu_custom_call" | custom-call | tf_op jit(solution)/shard_map/cells/pallas_call | solution.py:468
  18.0 0.0 collective-permute-done.3.halo_xl
  18.0 0.0 collective-permute-done.2.halo_xh
  18.0 0.0 copy-done.5
  18.0 0.0 copy-start.4
  18.0 8.2 %steps.1 = (f32[3,64,768]{2,1,0:T(8,128)}, f32[768,128]{1,0:T(8,128)}) custom-call(f32[3,64,768]{2,1,0:T(8,128)S(1)} %get-tuple-element.12.cells, f32[5,64,768]{2,1,0:T(8,128)S(1)} %get-tuple-element.13.props, f32[96,128]{1,0:T(8,128)S(1)} %collective-permute-done.from_high, f32[96,128]{1,0:T(8,128)S(1)} %collective-permute-done.1.from_low, ...), custom_call_target="tpu_custom_call" | custom-call | tf_op jit(solution)/shard_map/steps/pallas_call | solution.py:476
  26.2 0.0 copy-start.3
  26.2 5.5 %all-to-all-start = ((f32[16,48,128]{2,1,0:T(8,128)}), f32[16,48,128]{2,1,0:T(8,128)S(1)}, u32[]{:S(2)}, u32[]{:S(2)}) async-start(f32[16,48,128]{2,1,0:T(8,128)} %bitcast.12), calls=%async_computation | async-start | bytes 786432 | tf_op jit(solution)/shard_map/all_to_all | solution.py:488
  31.7 9.1 %all-to-all-done = f32[16,48,128]{2,1,0:T(8,128)S(1)} async-done(((f32[16,48,128]{2,1,0:T(8,128)}), f32[16,48,128]{2,1,0:T(8,128)S(1)}, u32[]{:S(2)}, u32[]{:S(2)}) %all-to-all-start) | async-done | bytes 393248 | tf_op jit(solution)/shard_map/all_to_all | solution.py:488
  40.9 0.0 copy-done.4
  40.9 0.0 copy-done.3
  40.9 2.0 %along_x.1 = f32[256,128]{1,0:T(8,128)} custom-call(s32[1]{0:T(128)} %bitcast.11.pair, f32[768,128]{1,0:T(8,128)S(1)} %bitcast.22, bf16[256,1024]{1,0:T(8,128)(2,1)S(1)} %copy-done.3, bf16[256,1024]{1,0:T(8,128)(2,1)S(1)} %copy-done.4), custom_call_target="tpu_custom_call" | custom-call | tf_op jit(solution)/shard_map/along_x/pallas_call | solution.py:493
  42.9 0.0 copy-start.10
  42.9 14.2 %all-to-all-start.1 = ((f32[32,8,128]{2,1,0:T(8,128)}), f32[32,8,128]{2,1,0:T(8,128)S(1)}, u32[]{:S(2)}, u32[]{:S(2)}) async-start(f32[32,8,128]{2,1,0:T(8,128)} %bitcast.14), calls=%async_computation.1 | async-start | bytes 262144 | tf_op jit(solution)/shard_map/all_to_all | solution.py:505
  57.1 8.4 %all-to-all-done.1 = f32[32,8,128]{2,1,0:T(8,128)S(1)} async-done(((f32[32,8,128]{2,1,0:T(8,128)}), f32[32,8,128]{2,1,0:T(8,128)S(1)}, u32[]{:S(2)}, u32[]{:S(2)}) %all-to-all-start.1) | async-done | bytes 131104 | tf_op jit(solution)/shard_map/all_to_all | solution.py:505
  65.5 0.0 copy-done.6
  65.5 0.0 copy-done.7
  65.5 0.0 copy-done.8
  65.5 0.0 copy-done.9
  65.5 0.0 copy-done.10
  65.5 1.2 %along_y.1 = (f32[4,1024]{1,0:T(4,128)}, f32[4,1024]{1,0:T(4,128)}) custom-call(s32[1]{0:T(128)} %bitcast.10.first_row, f32[256,128]{1,0:T(8,128)S(1)} %bitcast.23, bf16[128,256]{1,0:T(8,128)(2,1)S(1)} %copy-done.6, bf16[128,256]{1,0:T(8,128)(2,1)S(1)} %copy-done.7, f32[64,128]{1,0:T(8,128)S(1)} %copy-done.8, bf16[64,64]{1,0:T(8,128)(2,1)S(1)} %copy-done.9, ...), custom_call_target="tpu_custom_call" | custom-call | tf_op jit(solution)/shard_map/along_y/pallas_call | solution.py:509
  (10 shorter events, 0.1 us)
Async XLA Ops:
  0.6 5.8 %copy-start = (f32[64,768]{1,0:T(8,128)S(1)}, f32[64,768]{1,0:T(8,128)}, u32[]{:S(2)}) copy-start(f32[64,768]{1,0:T(8,128)} %p_high.1) | copy-start | bytes 589828
  0.6 5.8 %copy-start.1 = (f32[64,768]{1,0:T(8,128)S(1)}, f32[64,768]{1,0:T(8,128)}, u32[]{:S(2)}) copy-start(f32[64,768]{1,0:T(8,128)} %a_high.1) | copy-start | bytes 589828
  0.7 5.8 %copy-start.2 = (s32[64,768]{1,0:T(8,128)S(1)}, s32[64,768]{1,0:T(8,128)}, u32[]{:S(2)}) copy-start(s32[64,768]{1,0:T(8,128)} %g_high.1) | copy-start | bytes 589828
  2.3 6.1 %collective-permute-start = (f32[96,128]{1,0:T(8,128)}, f32[96,128]{1,0:T(8,128)S(1)}, u32[]{:S(2)}, u32[]{:S(2)}) collective-permute-start(f32[96,128]{1,0:T(8,128)} %get-tuple-element.14), channel_id=1, source_target_pairs={{1,0},{2,1},{3,2},{4,3},{5,4},{6,5},{7,6},{8,7},{9,8},{10,9},{11,1... | collective-permute-start | bytes 147464 | tf_op jit(solution)/shard_map/ppermute | solution.py:442
  5.5 4.1 %collective-permute-start.1 = (f32[96,128]{1,0:T(8,128)}, f32[96,128]{1,0:T(8,128)S(1)}, u32[]{:S(2)}, u32[]{:S(2)}) collective-permute-start(f32[96,128]{1,0:T(8,128)} %get-tuple-element.15), channel_id=1, source_target_pairs={{0,1},{1,2},{2,3},{3,4},{4,5},{5,6},{6,7},{7,8},{8,9},{9,10},{10,1... | collective-permute-start | bytes 147464 | tf_op jit(solution)/shard_map/ppermute | solution.py:443
  9.7 5.9 %copy-start.11 = (f32[256]{0:T(256)S(1)}, f32[256]{0:T(256)}, u32[]{:S(2)}) copy-start(f32[256]{0:T(256)} %param.19) | copy-start | bytes 3076
  9.7 5.9 %copy-start.12 = (f32[256]{0:T(256)S(1)}, f32[256]{0:T(256)}, u32[]{:S(2)}) copy-start(f32[256]{0:T(256)} %param.20) | copy-start | bytes 3076
  9.7 5.9 %copy-start.13 = (f32[256]{0:T(256)S(1)}, f32[256]{0:T(256)}, u32[]{:S(2)}) copy-start(f32[256]{0:T(256)} %param.21) | copy-start | bytes 3076
  9.7 5.9 %copy-start.14 = (f32[256]{0:T(256)S(1)}, f32[256]{0:T(256)}, u32[]{:S(2)}) copy-start(f32[256]{0:T(256)} %param.22) | copy-start | bytes 3076
  9.7 5.9 %copy-start.15 = (f32[3]{0:T(128)S(1)}, f32[3]{0:T(128)}, u32[]{:S(2)}) copy-start(f32[3]{0:T(128)} %applied.1) | copy-start | bytes 40
  9.8 8.2 %copy-start.5 = (bf16[768,256]{1,0:T(8,128)(2,1)S(1)}, bf16[768,256]{1,0:T(8,128)(2,1)}, u32[]{:S(2)}) copy-start(bf16[768,256]{1,0:T(8,128)(2,1)} %constant.43.clone.sum_z) | copy-start | bytes 1179652
  9.8 8.1 %collective-permute-start.3 = (f32[3,4,896]{2,1,0:T(4,128)S(1)}, f32[3,4,896]{2,1,0:T(4,128)S(1)}, u32[]{:S(2)}, u32[]{:S(2)}) collective-permute-start(f32[3,4,896]{2,1,0:T(4,128)S(1)} %pad_maximum_fusion.1), channel_id=1, source_target_pairs={{0,16},{16,32},{32,48},{48,64},{64,80},{80,96},{96,112},{112,128},... | collective-permute-start | bytes 129032 | tf_op jit(solution)/shard_map/ppermute | solution.py:464
  11.6 6.4 %collective-permute-start.2 = (f32[3,4,896]{2,1,0:T(4,128)S(1)}, f32[3,4,896]{2,1,0:T(4,128)S(1)}, u32[]{:S(2)}, u32[]{:S(2)}) collective-permute-start(f32[3,4,896]{2,1,0:T(4,128)S(1)} %pad_maximum_fusion), channel_id=1, source_target_pairs={{16,0},{32,16},{48,32},{64,48},{80,64},{96,80},{112,96},{128,112},... | collective-permute-start | bytes 129032 | tf_op jit(solution)/shard_map/ppermute | solution.py:463
  18.0 22.8 %copy-start.4 = (bf16[256,1024]{1,0:T(8,128)(2,1)S(1)}, bf16[256,1024]{1,0:T(8,128)(2,1)}, u32[]{:S(2)}) copy-start(bf16[256,1024]{1,0:T(8,128)(2,1)} %constant.45.clone.waves_lo) | copy-start | bytes 1572868
  26.2 14.7 %copy-start.3 = (bf16[256,1024]{1,0:T(8,128)(2,1)S(1)}, bf16[256,1024]{1,0:T(8,128)(2,1)}, u32[]{:S(2)}) copy-start(bf16[256,1024]{1,0:T(8,128)(2,1)} %constant.44.clone.waves_hi) | copy-start | bytes 1572868
  26.2 14.7 %all-to-all-start = ((f32[16,48,128]{2,1,0:T(8,128)}), f32[16,48,128]{2,1,0:T(8,128)S(1)}, u32[]{:S(2)}, u32[]{:S(2)}) async-start(f32[16,48,128]{2,1,0:T(8,128)} %bitcast.12), calls=%async_computation | async-start | bytes 786432 | tf_op jit(solution)/shard_map/all_to_all | solution.py:488
  42.9 22.6 %copy-start.6 = (bf16[128,256]{1,0:T(8,128)(2,1)S(1)}, bf16[128,256]{1,0:T(8,128)(2,1)}, u32[]{:S(2)}) copy-start(bf16[128,256]{1,0:T(8,128)(2,1)} %constant.46.clone.waves_hi) | copy-start | bytes 196612
  42.9 22.6 %copy-start.7 = (bf16[128,256]{1,0:T(8,128)(2,1)S(1)}, bf16[128,256]{1,0:T(8,128)(2,1)}, u32[]{:S(2)}) copy-start(bf16[128,256]{1,0:T(8,128)(2,1)} %constant.47.clone.waves_lo) | copy-start | bytes 196612
  42.9 22.6 %copy-start.8 = (f32[64,128]{1,0:T(8,128)S(1)}, f32[64,128]{1,0:T(8,128)}, u32[]{:S(2)}) copy-start(f32[64,128]{1,0:T(8,128)} %constant.48.clone.twiddle) | copy-start | bytes 98308
  42.9 22.6 %copy-start.9 = (bf16[64,64]{1,0:T(8,128)(2,1)S(1)}, bf16[64,64]{1,0:T(8,128)(2,1)}, u32[]{:S(2)}) copy-start(bf16[64,64]{1,0:T(8,128)(2,1)} %constant.49.clone.last_hi) | copy-start | bytes 24580
  42.9 22.6 %copy-start.10 = (bf16[64,64]{1,0:T(8,128)(2,1)S(1)}, bf16[64,64]{1,0:T(8,128)(2,1)}, u32[]{:S(2)}) copy-start(bf16[64,64]{1,0:T(8,128)(2,1)} %constant.50.clone.last_lo) | copy-start | bytes 24580
  42.9 22.6 %all-to-all-start.1 = ((f32[32,8,128]{2,1,0:T(8,128)}), f32[32,8,128]{2,1,0:T(8,128)S(1)}, u32[]{:S(2)}, u32[]{:S(2)}) async-start(f32[32,8,128]{2,1,0:T(8,128)} %bitcast.14), calls=%async_computation.1 | async-start | bytes 262144 | tf_op jit(solution)/shard_map/all_to_all | solution.py:505

commit v3 on v2

--- a/solution.py
+++ b/solution.py
@@ -114,19 +114,16 @@
     return (2.0 * GAIN) * p * q / (p + q)
 
 
-def edges_kernel(p_low, a_low, g_low, p_high, a_high, g_high, low, high):
+def edges_kernel(is_even, p_low, a_low, g_low, p_high, a_high, g_high, first, second):
     half = WX // 2
     lane = iota((half, 128), 1)
-    for i, src in enumerate((p_low, a_low, g_low)):
-        v = src[...].astype(jnp.float32)
-        low[i * half : (i + 1) * half, :] = jnp.where(
-            lane < 48, v[0:half, :], pltpu.roll(v[half:WX, :], 48, 1)
-        )
-    for i, src in enumerate((p_high, a_high, g_high)):
-        v = src[...].astype(jnp.float32)
-        high[i * half : (i + 1) * half, :] = jnp.where(
-            lane >= 80, v[0:half, :], pltpu.roll(v[half:WX, :], 80, 1)
-        )
+    even = is_even[0] == 1
+    for i, (l, h) in enumerate(((p_low, p_high), (a_low, a_high), (g_low, g_high))):
+        l, h = l[...].astype(jnp.float32), h[...].astype(jnp.float32)
+        l = jnp.where(lane < 48, l[0:half, :], pltpu.roll(l[half:WX, :], 48, 1))
+        h = jnp.where(lane >= 80, h[0:half, :], pltpu.roll(h[half:WX, :], 80, 1))
+        first[i * half : (i + 1) * half, :] = jnp.where(even, h, l)
+        second[i * half : (i + 1) * half, :] = jnp.where(even, l, h)
 
 
 def cells_kernel(
@@ -134,11 +131,12 @@
     cells, props, tables,
 ):
     ax, ay, az = start_cells(axis_polar[...], axis_azimuth[...])
-    rows = [stiffness[...], GAIN * anisotropy[...], ax, ay, az]
+    root = jnp.sqrt(GAIN * anisotropy[...])
+    rows = [stiffness[...], root * ax, root * ay, root * az]
     for r, row in enumerate(rows):
         tables[r : r + 1, :] = row
     for c in range(3):
-        tables[5 + c : 6 + c, :] = jnp.full((1, NGRAIN), GAIN * applied[c])
+        tables[4 + c : 5 + c, :] = jnp.full((1, NGRAIN), GAIN * applied[c])
     tabs = grain_tables(rows)
 
     def body(s, carry):
@@ -146,7 +144,7 @@
         for c in range(3):
             put(cells, s, start[c], c)
         labels = strip(grains, s)
-        for r in range(5):
+        for r in range(4):
             put(props, s, look_up(tabs[r], labels), r)
         return carry
 
@@ -156,12 +154,12 @@
 def steps_kernel(
     cells, props, from_high, from_low, halo_xh, halo_xl, tables, sum_z,
     moment, payload,
-    m0, m1, wt, cxu, cxd, cyu, cyd, czu, czd, ks, ux, uy, uz, raw,
+    m0, m1, wt, cxu, cxd, cyu, cyd, czu, czd, cs, ux, uy, uz, raw,
 ):
-    tabs = grain_tables([tables[r : r + 1, :] for r in range(5)])
+    tabs = grain_tables([tables[r : r + 1, :] for r in range(4)])
     for c in range(3):
         m0[c, 0:WX, 0:COLS] = cells[c]
-    for r, ref in enumerate((wt, ks, ux, uy, uz)):
+    for r, ref in enumerate((wt, ux, uy, uz)):
         ref[0:WX, 0:COLS] = props[r]
 
     def fill(rows, cols, polar, azimuth, labels):
@@ -169,7 +167,7 @@
         for c in range(3):
             m0[c, rows, cols] = start[c]
         labels = labels.astype(jnp.int32)
-        for r, ref in enumerate((wt, ks, ux, uy, uz)):
+        for r, ref in enumerate((wt, ux, uy, uz)):
             ref[rows, cols] = look_up(tabs[r], labels)
 
     near = iota((8, 128), 1) < 64
@@ -205,36 +203,40 @@
 
     def couplings(s, carry):
         w = strip(wt, s)
-        put(cxu, s, couple(w, up(w, strip(wt, nxt(s)))))
-        put(cxd, s, couple(w, down(w, strip(wt, prv(s)))))
-        y = couple(w, pltpu.roll(w, LANES - NZ, 1))
-        put(cyu, s, y)
-        put(cyd, s, pltpu.roll(y, NZ, 1))
+        xu = couple(w, up(w, strip(wt, nxt(s))))
+        xd = couple(w, down(w, strip(wt, prv(s))))
+        yu = couple(w, pltpu.roll(w, LANES - NZ, 1))
+        yd = pltpu.roll(yu, NZ, 1)
         lane = iota(w.shape, 1)
         depth = jnp.where(lane < COLS + 64, lane, lane - LANES + 6 * NZ + COLS) % NZ
-        z = jnp.where(depth != NZ - 1, couple(w, pltpu.roll(w, LANES - 1, 1)), 0.0)
-        put(czu, s, z)
-        put(czd, s, pltpu.roll(z, 1, 1))
+        zu = jnp.where(depth != NZ - 1, couple(w, pltpu.roll(w, LANES - 1, 1)), 0.0)
+        zd = pltpu.roll(zu, 1, 1)
+        for ref, value in zip((cxu, cxd, cyu, cyd, czu, czd), (xu, xd, yu, yd, zu, zd)):
+            put(ref, s, value)
+        put(cs, s, (xu + xd) + (yu + yd) + (zu + zd))
         return carry
 
     lax.fori_loop(0, STRIPS, couplings, 0, unroll=3)
-    field = [jnp.broadcast_to(tables[5 + c : 6 + c, 0:1], (8, LANES)) for c in range(3)]
-
-    def step(src, dst, s):
+    field = [jnp.broadcast_to(tables[4 + c : 5 + c, 0:1], (8, LANES)) for c in range(3)]
+
+    def step(src, dst, s, width):
         after, before = nxt(s), prv(s)
-        m = [strip(src, s, c) for c in range(3)]
-        u = [strip(r, s) for r in (ux, uy, uz)]
-        xu, xd, yu, yd, zu, zd = (strip(r, s) for r in (cxu, cxd, cyu, cyd, czu, czd))
-        proj = strip(ks, s) * (u[0] * m[0] + u[1] * m[1] + u[2] * m[2])
+        whole = [strip(src, s, c) for c in range(3)]
+        m = [v[:, 0:width] for v in whole]
+        u = [strip(r, s)[:, 0:width] for r in (ux, uy, uz)]
+        xu, xd, yu, yd, zu, zd, total = (
+            strip(r, s)[:, 0:width] for r in (cxu, cxd, cyu, cyd, czu, czd, cs)
+        )
+        proj = u[0] * m[0] + u[1] * m[1] + u[2] * m[2]
         h = []
         for c in range(3):
-            f = yu * (pltpu.roll(m[c], LANES - NZ, 1) - m[c])
-            f = f + yd * (pltpu.roll(m[c], NZ, 1) - m[c])
-            f = f + zu * (pltpu.roll(m[c], LANES - 1, 1) - m[c])
-            f = f + zd * (pltpu.roll(m[c], 1, 1) - m[c])
-            f = f + xu * (up(m[c], strip(src, after, c)) - m[c])
-            f = f + xd * (down(m[c], strip(src, before, c)) - m[c])
-            h.append(f + proj * u[c] + field[c])
+            f = yu * pltpu.roll(whole[c], LANES - NZ, 1)[:, 0:width]
+            f = f + yd * pltpu.roll(whole[c], NZ, 1)[:, 0:width]
+            f = f + zu * pltpu.roll(whole[c], LANES - 1, 1)[:, 0:width]
+            f = f + zd * pltpu.roll(whole[c], 1, 1)[:, 0:width]
+            f = f + xu * up(m[c], strip(src, after, c)[:, 0:width])
+            f = f + xd * down(m[c], strip(src, before, c)[:, 0:width])
+            h.append(f - total * m[c] + proj * u[c] + field[c][:, 0:width])
         t = cross(m, h)
         d = cross(m, t)
         v = [m[c] - (t[c] + DAMPING * d[c]) for c in range(3)]
@@ -242,9 +244,9 @@
         for c in range(3):
             put(dst, s, v[c] * r, c)
 
-    def one(src, dst, count, unroll):
+    def one(src, dst, count, unroll, width=LANES):
         def body(s, carry):
-            step(src, dst, s)
+            step(src, dst, s, width)
             return carry
 
         lax.fori_loop(0, count, body, 0, unroll=unroll)
@@ -252,12 +254,9 @@
     one(m0, m1, STRIPS, 3)
     one(m1, m0, STRIPS, 3)
     one(m0, m1, STRIPS, 3)
-    one(m1, m0, STRIPS - 1, 4)
-
-    for c in range(3):
-        moment[c] = m0[c, 0:WX, 0:COLS]
-
-    m = jnp.concatenate([m0[c, 0:WX, 0:COLS] for c in range(3)], axis=0)
+    one(m1, moment, STRIPS - 1, 4, COLS)
+
+    m = jnp.concatenate([moment[c] for c in range(3)], axis=0)
     hi, lo = split(m)
     out = mm(hi, sum_z[...]) + mm(lo, sum_z[...])
     block = iota((16, 128), 1) // 32
@@ -307,7 +306,7 @@
                 d_lo[pl.ds(start, 16), 128 * i : 128 * i + 128] = lo
         return carry
 
-    lax.fori_loop(0, 16, unpack, 0, unroll=2)
+    lax.fori_loop(0, 16, unpack, 0, unroll=4)
     both = mm(waves_hi[...], d_hi[...]) + (
         mm(waves_hi[...], d_lo[...]) + mm(waves_lo[...], d_hi[...])
     )
@@ -420,27 +419,29 @@
 
 
 def shards(polar, azimuth, grains, stiffness, anisotropy, axis_polar, axis_azimuth, applied_field):
-    count_x = lax.axis_size("gx")
-    count_y = lax.axis_size("gy")
-    forward_x = [(i, (i + 1) % count_x) for i in range(count_x)]
-    backward_x = [(t, s) for s, t in forward_x]
-    forward_y = [(i, (i + 1) % count_y) for i in range(count_y)]
-    backward_y = [(t, s) for s, t in forward_y]
+    even_pairs = [(i, i ^ 1) for i in range(16)]
+    odd_pairs = [(i, (i + 1) % 16) if i % 2 else (i, (i - 1) % 16) for i in range(16)]
+    at_x = lax.axis_index("gx").astype(jnp.int32)
+    at_y = lax.axis_index("gy").astype(jnp.int32)
+    even_x = at_x % 2 == 0
+    even_y = at_y % 2 == 0
     fields = (polar, azimuth, grains)
-    params = pltpu.CompilerParams(vmem_limit_bytes=32 << 20)
+    params = pltpu.CompilerParams(vmem_limit_bytes=16 << 20)
     smem = [pl.BlockSpec(memory_space=pltpu.SMEM)]
     first = pl.BlockSpec((WX, 128), lambda i: (0, 0))
     last = pl.BlockSpec((WX, 128), lambda i: (0, COLS // 128 - 1))
-    low_edge, high_edge = pl.pallas_call(
+    to_first, to_second = pl.pallas_call(
         edges_kernel,
         grid=(1,),
         out_shape=(f32(3 * WX // 2, 128), f32(3 * WX // 2, 128)),
-        in_specs=[first] * 3 + [last] * 3,
+        in_specs=smem + [first] * 3 + [last] * 3,
         out_specs=tuple(vmem(2)),
         name="edges",
-    )(*fields, *fields)
-    from_high = lax.ppermute(low_edge, "gy", backward_y)
-    from_low = lax.ppermute(high_edge, "gy", forward_y)
+    )(even_y.astype(jnp.int32).reshape(1), *fields, *fields)
+    got_second = lax.ppermute(to_second, "gy", odd_pairs)
+    got_first = lax.ppermute(to_first, "gy", even_pairs)
+    from_high = jnp.where(even_y, got_first, got_second)
+    from_low = jnp.where(even_y, got_second, got_first)
 
     def edge(start, row, high, low):
         blank = jnp.zeros((4, 32), jnp.float32)
@@ -460,14 +461,18 @@
             )
         return jnp.stack(parts)
 
-    halo_xh = lax.ppermute(edge(0, 0, 0, 80), "gx", backward_x)
-    halo_xl = lax.ppermute(edge(WX - 4, WX // 2 - 4, 48, 32), "gx", forward_x)
+    low_edge = edge(0, 0, 0, 80)
+    high_edge = edge(WX - 4, WX // 2 - 4, 48, 32)
+    got_second = lax.ppermute(jnp.where(even_x, low_edge, high_edge), "gx", odd_pairs)
+    got_first = lax.ppermute(jnp.where(even_x, high_edge, low_edge), "gx", even_pairs)
+    halo_xh = jnp.where(even_x, got_first, got_second)
+    halo_xl = jnp.where(even_x, got_second, got_first)
     per_grain = [
         v.reshape(1, NGRAIN) for v in (stiffness, anisotropy, axis_polar, axis_azimuth)
     ]
     cells, props, tables = pl.pallas_call(
         cells_kernel,
-        out_shape=(f32(3, WX, COLS), f32(5, WX, COLS), f32(8, NGRAIN)),
+        out_shape=(f32(3, WX, COLS), f32(4, WX, COLS), f32(8, NGRAIN)),
         in_specs=vmem(7) + smem,
         out_specs=tuple(vmem(3)),
         compiler_params=params,
@@ -488,8 +493,6 @@
     columns = lax.all_to_all(
         payload.reshape(16, 48, 128), "gx", split_axis=0, concat_axis=0, tiled=True
     ).reshape(16 * 48, 128)
-    at_x = lax.axis_index("gx").astype(jnp.int32)
-    at_y = lax.axis_index("gy").astype(jnp.int32)
     rows = pl.pallas_call(
         x_kernel,
         out_shape=f32(256, 128),

time: 67 us -> 65.3 us (0.975)
  starting transfers between devices: 29.6 us -> 26.7 us
  waiting for transfers between devices: 20.6 us -> 22.8 us
  Pallas kernels: 15.3 us -> 14.2 us
    ppermute x4, waiting for transfers between devices: 3.02 us -> 5.21 us  [the longest x1 4.14 us: shards(): got_second = lax.ppermute(to_second, 'gy', odd_pairs)]
    all_to_all x1, starting transfers between devices: 5.5 us -> 3.77 us  [shards(): lax.all_to_all(payload.reshape(16, 48, 128), 'gx', split_axis=0, concat_a...]
    ppermute x4, starting transfers between devices: 9.91 us -> 9.19 us  [the longest x1 5.05 us: shards(): lax.ppermute(jnp.where(even_x, low_edge, high_edge), 'gx', odd_pairs)]
where the time goes in v3:
time: 65.3 us; the launch traced here: 65 us
  starting transfers between devices  26.7 us (41%)
  waiting for transfers between devices  22.8 us (35%)
  Pallas kernels  14.2 us (22%)
  between operations  0.9 us (1%)
    all_to_all x1, starting transfers between devices, shards(): lax.all_to_all(rows.reshape(32, 8, 128), ('gx', 'gy'), split_axis=0, conc...  13.7 us
    all_to_all x1, waiting for transfers between devices, shards(): lax.all_to_all(payload.reshape(16, 48, 128), 'gx', split_axis=0, concat_a...  9.15 us
    all_to_all x1, waiting for transfers between devices, shards(): lax.all_to_all(rows.reshape(32, 8, 128), ('gx', 'gy'), split_axis=0, conc...  8.41 us
    pallas_call x1, Pallas kernels, shards(): pl.pallas_call(steps_kernel, out_shape=(f32(3, WX, COLS), f32(16 * 48, 12...  7.59 us
    ppermute x1, starting transfers between devices, shards(): lax.ppermute(jnp.where(even_x, low_edge, high_edge), 'gx', odd_pairs)  5.05 us
    ppermute x1, waiting for transfers between devices, shards(): got_second = lax.ppermute(to_second, 'gy', odd_pairs)  4.14 us
    all_to_all x1, starting transfers between devices, shards(): lax.all_to_all(payload.reshape(16, 48, 128), 'gx', split_axis=0, concat_a...  3.77 us
    ppermute x1, starting transfers between devices, shards(): got_first = lax.ppermute(to_first, 'gy', even_pairs)  3.24 us
  transfers between devices with their start and end apart: 6, of which 4 were waited for; matrix products, arithmetic and copies ran while one was open for 0% of the time, Pallas kernels for 3%

profile of v3, /device:TPU:1, one launch (start us, length us, event | category | flops | bytes accessed | tf_op | source)
XLA Modules:
  0.0 65.0 jit_solution(6925794702404784857)
XLA Ops:
  0.6 0.0 copy-start
  0.7 0.0 copy-start.1
  0.7 0.0 copy-start.2
  0.7 1.6 %edges.1 = (f32[96,128]{1,0:T(8,128)}, f32[96,128]{1,0:T(8,128)}) custom-call(s32[1]{0:T(128)} %bitcast.4.is_even, f32[64,768]{1,0:T(8,128)} %p_high.1, f32[64,768]{1,0:T(8,128)} %a_high.1, s32[64,768]{1,0:T(8,128)} %g_high.1, f32[64,768]{1,0:T(8,128)} %p_high.1, f32[64,768]{1,0:T(8,128)} %a_high.1, s32[64,768]{1,0:T(8,128)} %g_high.1), custom_call_target="tpu_custom_call" | custom-call | tf_op jit(solution)/shard_map/edges/pallas_call | solution.py:433
  2.3 3.2 %collective-permute-start = (f32[96,128]{1,0:T(8,128)}, f32[96,128]{1,0:T(8,128)S(1)}, u32[]{:S(2)}, u32[]{:S(2)}) collective-permute-start(f32[96,128]{1,0:T(8,128)} %get-tuple-element.14), channel_id=1, source_target_pairs={{0,1},{1,0},{2,3},{3,2},{4,5},{5,4},{6,7},{7,6},{8,9},{9,8},{10,11... | collective-permute-start | bytes 147464 | tf_op jit(solution)/shard_map/ppermute | solution.py:442
  5.5 0.9 %collective-permute-start.1 = (f32[96,128]{1,0:T(8,128)}, f32[96,128]{1,0:T(8,128)S(1)}, u32[]{:S(2)}, u32[]{:S(2)}) collective-permute-start(f32[96,128]{1,0:T(8,128)} %get-tuple-element.15), channel_id=1, source_target_pairs={{0,15},{1,2},{2,1},{3,4},{4,3},{5,6},{6,5},{7,8},{8,7},{9,10},{10,... | collective-permute-start | bytes 147464 | tf_op jit(solution)/shard_map/ppermute | solution.py:441
  6.4 0.0 copy-done
  6.4 0.0 copy-done.1
  6.5 0.0 copy-done.2
  6.5 0.1 pad.28.clone
  6.6 0.0 collective-permute-done
  6.6 4.1 %collective-permute-done.1 = f32[96,128]{1,0:T(8,128)S(1)} collective-permute-done((f32[96,128]{1,0:T(8,128)}, f32[96,128]{1,0:T(8,128)S(1)}, u32[]{:S(2)}, u32[]{:S(2)}) %collective-permute-start.1) | collective-permute-done | bytes 49184 | tf_op jit(solution)/shard_map/ppermute | solution.py:441
  10.8 0.1 fusion.2
  10.9 0.1 maximum_bitcast_fusion
  10.9 0.0 copy-start.11
  10.9 0.0 copy-start.12
  11.0 0.0 copy-start.13
  11.0 0.0 copy-start.14
  11.0 0.0 copy-start.15
  11.0 0.0 copy-start.5
  11.0 5.1 %collective-permute-start.3 = (f32[3,4,896]{2,1,0:T(4,128)S(1)}, f32[3,4,896]{2,1,0:T(4,128)S(1)}, u32[]{:S(2)}, u32[]{:S(2)}) collective-permute-start(f32[3,4,896]{2,1,0:T(4,128)S(1)} %get-tuple-element.31), channel_id=1, source_target_pairs={{0,240},{16,32},{32,16},{48,64},{64,48},{80,96},{96,80},{112,128},... | collective-permute-start | bytes 129032 | tf_op jit(solution)/shard_map/ppermute | solution.py:466
  16.1 0.0 collective-permute-start.2
  16.1 0.0 copy-done.11
  16.1 0.0 copy-done.12
  16.1 0.0 copy-done.13
  16.1 0.0 copy-done.14
  16.1 0.0 copy-done.15
  16.1 2.1 %cells.1 = (f32[3,64,768]{2,1,0:T(8,128)S(1)}, f32[4,64,768]{2,1,0:T(8,128)S(1)}, f32[8,256]{1,0:T(8,128)S(1)}) custom-call(f32[64,768]{1,0:T(8,128)S(1)} %copy-done, f32[64,768]{1,0:T(8,128)S(1)} %copy-done.1, s32[64,768]{1,0:T(8,128)S(1)} %copy-done.2, f32[1,256]{1,0:T(1,128)S(1)} %bitcast.25, f32[1,256]{1,0:T(1,128)S(1)} %bitcast.26, ...), custom_call_target="tpu_custom_call" | custom-call | tf_op jit(solution)/shard_map/cells/pallas_call | solution.py:473
  18.2 0.0 collective-permute-done.3
  18.2 1.0 %collective-permute-done.2 = f32[3,4,896]{2,1,0:T(4,128)S(1)} collective-permute-done((f32[3,4,896]{2,1,0:T(4,128)S(1)}, f32[3,4,896]{2,1,0:T(4,128)S(1)}, u32[]{:S(2)}, u32[]{:S(2)}) %collective-permute-start.2) | collective-permute-done | bytes 43040 | tf_op jit(solution)/shard_map/ppermute | solution.py:467
  19.3 0.0 copy-done.5
  19.3 0.0 copy-start.4
  19.3 7.6 %steps.1 = (f32[3,64,768]{2,1,0:T(8,128)}, f32[768,128]{1,0:T(8,128)}) custom-call(f32[3,64,768]{2,1,0:T(8,128)S(1)} %get-tuple-element.12.cells, f32[4,64,768]{2,1,0:T(8,128)S(1)} %get-tuple-element.13.props, f32[96,128]{1,0:T(8,128)S(1)} %get-tuple-element.28.from_high, f32[96,128]{1,0:T(8,128)S(1)} %get-tuple-element.27.from_low, ...), custom_call_target="tpu_custom_call" | custom-call | tf_op jit(solution)/shard_map/steps/pallas_call | solution.py:481
  26.9 0.0 copy-start.3
  26.9 3.8 %all-to-all-start = ((f32[16,48,128]{2,1,0:T(8,128)}), f32[16,48,128]{2,1,0:T(8,128)S(1)}, u32[]{:S(2)}, u32[]{:S(2)}) async-start(f32[16,48,128]{2,1,0:T(8,128)} %bitcast.13), calls=%async_computation | async-start | bytes 786432 | tf_op jit(solution)/shard_map/all_to_all | solution.py:493
  30.7 9.1 %all-to-all-done = f32[16,48,128]{2,1,0:T(8,128)S(1)} async-done(((f32[16,48,128]{2,1,0:T(8,128)}), f32[16,48,128]{2,1,0:T(8,128)S(1)}, u32[]{:S(2)}, u32[]{:S(2)}) %all-to-all-start) | async-done | bytes 393248 | tf_op jit(solution)/shard_map/all_to_all | solution.py:493
  39.8 0.0 copy-done.4
  39.8 0.0 copy-done.3
  39.8 1.7 %along_x.1 = f32[256,128]{1,0:T(8,128)} custom-call(s32[1]{0:T(128)} %bitcast.12.pair, f32[768,128]{1,0:T(8,128)S(1)} %bitcast.23, bf16[256,1024]{1,0:T(8,128)(2,1)S(1)} %copy-done.4, bf16[256,1024]{1,0:T(8,128)(2,1)S(1)} %copy-done.3), custom_call_target="tpu_custom_call" | custom-call | tf_op jit(solution)/shard_map/along_x/pallas_call | solution.py:496
  41.6 0.0 copy-start.10
  41.6 13.7 %all-to-all-start.1 = ((f32[32,8,128]{2,1,0:T(8,128)}), f32[32,8,128]{2,1,0:T(8,128)S(1)}, u32[]{:S(2)}, u32[]{:S(2)}) async-start(f32[32,8,128]{2,1,0:T(8,128)} %bitcast.15), calls=%async_computation.1 | async-start | bytes 262144 | tf_op jit(solution)/shard_map/all_to_all | solution.py:508
  55.3 8.4 %all-to-all-done.1 = f32[32,8,128]{2,1,0:T(8,128)S(1)} async-done(((f32[32,8,128]{2,1,0:T(8,128)}), f32[32,8,128]{2,1,0:T(8,128)S(1)}, u32[]{:S(2)}, u32[]{:S(2)}) %all-to-all-start.1) | async-done | bytes 131104 | tf_op jit(solution)/shard_map/all_to_all | solution.py:508
  63.8 0.0 copy-done.6
  63.8 0.0 copy-done.7
  63.8 0.0 copy-done.8
  63.8 0.0 copy-done.9
  63.8 0.0 copy-done.10
  63.8 1.2 %along_y.1 = (f32[4,1024]{1,0:T(4,128)}, f32[4,1024]{1,0:T(4,128)}) custom-call(s32[1]{0:T(128)} %bitcast.11.first_row, f32[256,128]{1,0:T(8,128)S(1)} %bitcast.24, bf16[128,256]{1,0:T(8,128)(2,1)S(1)} %copy-done.7, bf16[128,256]{1,0:T(8,128)(2,1)S(1)} %copy-done.6, f32[64,128]{1,0:T(8,128)S(1)} %copy-done.8, bf16[64,64]{1,0:T(8,128)(2,1)S(1)} %copy-done.10, ...), custom_call_target="tpu_custom_call" | custom-call | tf_op jit(solution)/shard_map/along_y/pallas_call | solution.py:512
  (10 shorter events, 0.1 us)
Async XLA Ops:
  0.6 5.8 %copy-start = (f32[64,768]{1,0:T(8,128)S(1)}, f32[64,768]{1,0:T(8,128)}, u32[]{:S(2)}) copy-start(f32[64,768]{1,0:T(8,128)} %p_high.1) | copy-start | bytes 589828
  0.7 5.8 %copy-start.1 = (f32[64,768]{1,0:T(8,128)S(1)}, f32[64,768]{1,0:T(8,128)}, u32[]{:S(2)}) copy-start(f32[64,768]{1,0:T(8,128)} %a_high.1) | copy-start | bytes 589828
  0.7 5.8 %copy-start.2 = (s32[64,768]{1,0:T(8,128)S(1)}, s32[64,768]{1,0:T(8,128)}, u32[]{:S(2)}) copy-start(s32[64,768]{1,0:T(8,128)} %g_high.1) | copy-start | bytes 589828
  2.3 4.3 %collective-permute-start = (f32[96,128]{1,0:T(8,128)}, f32[96,128]{1,0:T(8,128)S(1)}, u32[]{:S(2)}, u32[]{:S(2)}) collective-permute-start(f32[96,128]{1,0:T(8,128)} %get-tuple-element.14), channel_id=1, source_target_pairs={{0,1},{1,0},{2,3},{3,2},{4,5},{5,4},{6,7},{7,6},{8,9},{9,8},{10,11... | collective-permute-start | bytes 147464 | tf_op jit(solution)/shard_map/ppermute | solution.py:442
  5.5 5.2 %collective-permute-start.1 = (f32[96,128]{1,0:T(8,128)}, f32[96,128]{1,0:T(8,128)S(1)}, u32[]{:S(2)}, u32[]{:S(2)}) collective-permute-start(f32[96,128]{1,0:T(8,128)} %get-tuple-element.15), channel_id=1, source_target_pairs={{0,15},{1,2},{2,1},{3,4},{4,3},{5,6},{6,5},{7,8},{8,7},{9,10},{10,... | collective-permute-start | bytes 147464 | tf_op jit(solution)/shard_map/ppermute | solution.py:441
  10.9 5.1 %copy-start.11 = (f32[256]{0:T(256)S(1)}, f32[256]{0:T(256)}, u32[]{:S(2)}) copy-start(f32[256]{0:T(256)} %param.19) | copy-start | bytes 3076
  10.9 5.1 %copy-start.12 = (f32[256]{0:T(256)S(1)}, f32[256]{0:T(256)}, u32[]{:S(2)}) copy-start(f32[256]{0:T(256)} %param.20) | copy-start | bytes 3076
  11.0 5.1 %copy-start.13 = (f32[256]{0:T(256)S(1)}, f32[256]{0:T(256)}, u32[]{:S(2)}) copy-start(f32[256]{0:T(256)} %param.21) | copy-start | bytes 3076
  11.0 5.1 %copy-start.14 = (f32[256]{0:T(256)S(1)}, f32[256]{0:T(256)}, u32[]{:S(2)}) copy-start(f32[256]{0:T(256)} %param.22) | copy-start | bytes 3076
  11.0 5.1 %copy-start.15 = (f32[3]{0:T(128)S(1)}, f32[3]{0:T(128)}, u32[]{:S(2)}) copy-start(f32[3]{0:T(128)} %applied.1) | copy-start | bytes 40
  11.0 8.3 %copy-start.5 = (bf16[768,256]{1,0:T(8,128)(2,1)S(1)}, bf16[768,256]{1,0:T(8,128)(2,1)}, u32[]{:S(2)}) copy-start(bf16[768,256]{1,0:T(8,128)(2,1)} %constant.58.clone.sum_z) | copy-start | bytes 1179652
  11.0 7.2 %collective-permute-start.3 = (f32[3,4,896]{2,1,0:T(4,128)S(1)}, f32[3,4,896]{2,1,0:T(4,128)S(1)}, u32[]{:S(2)}, u32[]{:S(2)}) collective-permute-start(f32[3,4,896]{2,1,0:T(4,128)S(1)} %get-tuple-element.31), channel_id=1, source_target_pairs={{0,240},{16,32},{32,16},{48,64},{64,48},{80,96},{96,80},{112,128},... | collective-permute-start | bytes 129032 | tf_op jit(solution)/shard_map/ppermute | solution.py:466
  16.1 3.2 %collective-permute-start.2 = (f32[3,4,896]{2,1,0:T(4,128)S(1)}, f32[3,4,896]{2,1,0:T(4,128)S(1)}, u32[]{:S(2)}, u32[]{:S(2)}) collective-permute-start(f32[3,4,896]{2,1,0:T(4,128)S(1)} %get-tuple-element.32), channel_id=1, source_target_pairs={{0,16},{16,0},{32,48},{48,32},{64,80},{80,64},{96,112},{112,96},{1... | collective-permute-start | bytes 129032 | tf_op jit(solution)/shard_map/ppermute | solution.py:467
  19.3 20.5 %copy-start.4 = (bf16[256,1024]{1,0:T(8,128)(2,1)S(1)}, bf16[256,1024]{1,0:T(8,128)(2,1)}, u32[]{:S(2)}) copy-start(bf16[256,1024]{1,0:T(8,128)(2,1)} %constant.59.clone.waves_hi) | copy-start | bytes 1572868
  26.9 12.9 %copy-start.3 = (bf16[256,1024]{1,0:T(8,128)(2,1)S(1)}, bf16[256,1024]{1,0:T(8,128)(2,1)}, u32[]{:S(2)}) copy-start(bf16[256,1024]{1,0:T(8,128)(2,1)} %constant.60.clone.waves_lo) | copy-start | bytes 1572868
  26.9 12.9 %all-to-all-start = ((f32[16,48,128]{2,1,0:T(8,128)}), f32[16,48,128]{2,1,0:T(8,128)S(1)}, u32[]{:S(2)}, u32[]{:S(2)}) async-start(f32[16,48,128]{2,1,0:T(8,128)} %bitcast.13), calls=%async_computation | async-start | bytes 786432 | tf_op jit(solution)/shard_map/all_to_all | solution.py:493
  41.6 22.2 %copy-start.6 = (bf16[128,256]{1,0:T(8,128)(2,1)S(1)}, bf16[128,256]{1,0:T(8,128)(2,1)}, u32[]{:S(2)}) copy-start(bf16[128,256]{1,0:T(8,128)(2,1)} %constant.62.clone.waves_lo) | copy-start | bytes 196612
  41.6 22.2 %copy-start.7 = (bf16[128,256]{1,0:T(8,128)(2,1)S(1)}, bf16[128,256]{1,0:T(8,128)(2,1)}, u32[]{:S(2)}) copy-start(bf16[128,256]{1,0:T(8,128)(2,1)} %constant.61.clone.waves_hi) | copy-start | bytes 196612
  41.6 22.2 %copy-start.8 = (f32[64,128]{1,0:T(8,128)S(1)}, f32[64,128]{1,0:T(8,128)}, u32[]{:S(2)}) copy-start(f32[64,128]{1,0:T(8,128)} %constant.63.clone.twiddle) | copy-start | bytes 98308
  41.6 22.2 %copy-start.9 = (bf16[64,64]{1,0:T(8,128)(2,1)S(1)}, bf16[64,64]{1,0:T(8,128)(2,1)}, u32[]{:S(2)}) copy-start(bf16[64,64]{1,0:T(8,128)(2,1)} %constant.65.clone.last_lo) | copy-start | bytes 24580
  41.6 22.2 %copy-start.10 = (bf16[64,64]{1,0:T(8,128)(2,1)S(1)}, bf16[64,64]{1,0:T(8,128)(2,1)}, u32[]{:S(2)}) copy-start(bf16[64,64]{1,0:T(8,128)(2,1)} %constant.64.clone.last_hi) | copy-start | bytes 24580
  41.6 22.2 %all-to-all-start.1 = ((f32[32,8,128]{2,1,0:T(8,128)}), f32[32,8,128]{2,1,0:T(8,128)S(1)}, u32[]{:S(2)}, u32[]{:S(2)}) async-start(f32[32,8,128]{2,1,0:T(8,128)} %bitcast.15), calls=%async_computation.1 | async-start | bytes 262144 | tf_op jit(solution)/shard_map/all_to_all | solution.py:508

commit v4 on v3

--- a/solution.py
+++ b/solution.py
@@ -114,10 +114,10 @@
     return (2.0 * GAIN) * p * q / (p + q)
 
 
-def edges_kernel(is_even, p_low, a_low, g_low, p_high, a_high, g_high, first, second):
+def edges_kernel(p_low, a_low, g_low, p_high, a_high, g_high, first, second):
     half = WX // 2
     lane = iota((half, 128), 1)
-    even = is_even[0] == 1
+    even = lax.axis_index("gy") % 2 == 0
     for i, (l, h) in enumerate(((p_low, p_high), (a_low, a_high), (g_low, g_high))):
         l, h = l[...].astype(jnp.float32), h[...].astype(jnp.float32)
         l = jnp.where(lane < 48, l[0:half, :], pltpu.roll(l[half:WX, :], 48, 1))
@@ -152,10 +152,11 @@
 
 
 def steps_kernel(
-    cells, props, from_high, from_low, halo_xh, halo_xl, tables, sum_z,
-    moment, payload,
-    m0, m1, wt, cxu, cxd, cyu, cyd, czu, czd, cs, ux, uy, uz, raw,
+    cells, props, from_high, from_low, halo_xh, halo_xl, tables, sum_z, *rest
 ):
+    (
+        moment, payload, m0, m1, wt, cxu, cxd, cyu, cyd, czu, czd, cs, ux, uy, uz, raw,
+    ) = rest[-16:]
     tabs = grain_tables([tables[r : r + 1, :] for r in range(4)])
     for c in range(3):
         m0[c, 0:WX, 0:COLS] = cells[c]
@@ -281,8 +282,9 @@
     ]
 
 
-def x_kernel(pair, got, waves_hi, waves_lo, out, d_hi, d_lo):
-    turn = (pair[0] * iota((8, 128), 0) + 4) % 8 - 4
+def x_kernel(got, waves_hi, waves_lo, out, d_hi, d_lo):
+    pair = lax.axis_index("gx") // 2
+    turn = (pair * iota((8, 128), 0) + 4) % 8 - 4
     sine, cosine = sincos(turn.astype(jnp.float32) * (math.pi / 4.0))
     sine = jnp.concatenate([sine] * 2, axis=0)
     cosine = jnp.concatenate([cosine] * 2, axis=0)
@@ -317,7 +319,7 @@
 
 
 def y_kernel(
-    first_row, got, waves_hi, waves_lo, twiddle, last_hi, last_lo,
+    got, waves_hi, waves_lo, twiddle, last_hi, last_lo,
     spin_flip, non_flip, flat, placed,
 ):
     parts = []
@@ -339,7 +341,7 @@
     hi, lo = split(jnp.concatenate(turned, axis=1))
     full = mm(last_hi[...], hi) + (mm(last_hi[...], lo) + mm(last_lo[...], hi))
     lane = iota((32, 128), 1)
-    kx = first_row[0] + lane // 32
+    kx = lax.axis_index("gx") * WX + lax.axis_index("gy") * 4 + lane // 32
     ky = iota((32, 128), 0) * 32 + lane % 32
     wave_x = jnp.where(kx < 512, kx, kx - 1024).astype(jnp.float32)
     wave_y = jnp.where(ky < 512, ky, ky - 1024).astype(jnp.float32)
@@ -434,10 +436,10 @@
         edges_kernel,
         grid=(1,),
         out_shape=(f32(3 * WX // 2, 128), f32(3 * WX // 2, 128)),
-        in_specs=smem + [first] * 3 + [last] * 3,
+        in_specs=[first] * 3 + [last] * 3,
         out_specs=tuple(vmem(2)),
         name="edges",
-    )(even_y.astype(jnp.int32).reshape(1), *fields, *fields)
+    )(*fields, *fields)
     got_second = lax.ppermute(to_second, "gy", odd_pairs)
     got_first = lax.ppermute(to_first, "gy", even_pairs)
     from_high = jnp.where(even_y, got_first, got_second)
@@ -478,17 +480,18 @@
         compiler_params=params,
         name="cells",
     )(*fields, *per_grain, applied_field)
+    tables_x, tables_y = x_tables(), y_tables()
     moment, payload = pl.pallas_call(
         steps_kernel,
         out_shape=(f32(3, WX, COLS), f32(16 * 48, 128)),
-        in_specs=vmem(8),
+        in_specs=vmem(8 + len(tables_x) + len(tables_y)),
         out_specs=tuple(vmem(2)),
         scratch_shapes=[pltpu.VMEM((3, ROWS, LANES), jnp.float32)] * 2
         + [pltpu.VMEM((ROWS, LANES), jnp.float32)] * 11
         + [pltpu.VMEM((3, 8, LANES), jnp.float32)],
         compiler_params=params,
         name="steps",
-    )(cells, props, from_high, from_low, halo_xh, halo_xl, tables, sum_matrix())
+    )(cells, props, from_high, from_low, halo_xh, halo_xl, tables, sum_matrix(), *tables_x, *tables_y)
 
     columns = lax.all_to_all(
         payload.reshape(16, 48, 128), "gx", split_axis=0, concat_axis=0, tiled=True
@@ -496,12 +499,12 @@
     rows = pl.pallas_call(
         x_kernel,
         out_shape=f32(256, 128),
-        in_specs=smem + vmem(3),
+        in_specs=vmem(3),
         out_specs=vmem(1)[0],
         scratch_shapes=[pltpu.VMEM((1024, 256), jnp.bfloat16)] * 2,
         compiler_params=params,
         name="along_x",
-    )((at_x // 2).reshape(1), columns, *x_tables())
+    )(columns, *tables_x)
     groups = [
         [gx * 16 + gy for gx in (base, base + 1) for gy in range(16)] for base in range(0, 16, 2)
     ]
@@ -512,12 +515,12 @@
     spin_flip, non_flip = pl.pallas_call(
         y_kernel,
         out_shape=(f32(4, 1024), f32(4, 1024)),
-        in_specs=smem + vmem(6),
+        in_specs=vmem(6),
         out_specs=tuple(vmem(2)),
         scratch_shapes=[pltpu.VMEM((32, 128), jnp.float32)] * 2,
         compiler_params=params,
         name="along_y",
-    )((at_x * WX + at_y * 4).reshape(1), mine, *y_tables())
+    )(mine, *tables_y)
     return (moment, spin_flip, non_flip)
 
 

time: 65.3 us -> 63.6 us (0.974)
  blocking collectives: 0 us -> 34.4 us
  waiting for transfers between devices: 22.8 us -> 5.09 us
  starting transfers between devices: 26.7 us -> 9.19 us
  Pallas kernels: 14.2 us -> 13.4 us
    all_to_all x0 -> x2, blocking collectives: none -> 34.4 us  [the longest x1 21.8 us: shards(): lax.all_to_all(rows.reshape(32, 8, 128), ('gx', 'gy'), split_axis=0, conc...]
    all_to_all x2 -> x0, waiting for transfers between devices: 17.6 us -> none  [the longest x1 9.15 us: shards(): lax.all_to_all(payload.reshape(16, 48, 128), 'gx', split_axis=0, concat_a...]
    all_to_all x2 -> x0, starting transfers between devices: 17.5 us -> none  [the longest x1 13.7 us: shards(): lax.all_to_all(rows.reshape(32, 8, 128), ('gx', 'gy'), split_axis=0, conc...]
  transfers between devices with their start and end apart: 6 -> 4, of which waited for: 4 -> 2; matrix products, arithmetic and copies ran while one was open for 0% -> 0% of each run, Pallas kernels for 3% -> 3%
where the time goes in v4:
time: 63.6 us; the launch traced here: 63.4 us
  blocking collectives  34.4 us (54%)
  Pallas kernels  13.4 us (21%)
  starting transfers between devices  9.19 us (14%)
  waiting for transfers between devices  5.09 us (8%)
  between operations  0.91 us (1%)
    all_to_all x1, blocking collectives, shards(): lax.all_to_all(rows.reshape(32, 8, 128), ('gx', 'gy'), split_axis=0, conc...  21.8 us
    all_to_all x1, blocking collectives, shards(): lax.all_to_all(payload.reshape(16, 48, 128), 'gx', split_axis=0, concat_a...  12.6 us
    pallas_call x1, Pallas kernels, shards(): pl.pallas_call(steps_kernel, out_shape=(f32(3, WX, COLS), f32(16 * 48, 12...  7.47 us
    ppermute x1, starting transfers between devices, shards(): lax.ppermute(jnp.where(even_x, low_edge, high_edge), 'gx', odd_pairs)  5.05 us
    ppermute x1, waiting for transfers between devices, shards(): got_second = lax.ppermute(to_second, 'gy', odd_pairs)  4.06 us
    ppermute x1, starting transfers between devices, shards(): got_first = lax.ppermute(to_first, 'gy', even_pairs)  3.24 us
    pallas_call x1, Pallas kernels, shards(): pl.pallas_call(cells_kernel, out_shape=(f32(3, WX, COLS), f32(4, WX, COLS...  2.09 us
    pallas_call x1, Pallas kernels, shards(): pl.pallas_call(edges_kernel, grid=(1,), out_shape=(f32(3 * WX // 2, 128),...  1.62 us
  transfers between devices with their start and end apart: 4, of which 2 were waited for; matrix products, arithmetic and copies ran while one was open for 0% of the time, Pallas kernels for 3%

profile of v4, /device:TPU:1, one launch (start us, length us, event | category | flops | bytes accessed | tf_op | source)
XLA Modules:
  0.0 63.4 jit_solution(1585678613521998149)
XLA Ops:
  0.6 0.0 copy-start.4
  0.6 0.0 copy-start.3
  0.7 0.0 copy-start.2
  0.7 1.6 %edges.1 = (f32[96,128]{1,0:T(8,128)}, f32[96,128]{1,0:T(8,128)}) custom-call(f32[64,768]{1,0:T(8,128)} %p_high.1, f32[64,768]{1,0:T(8,128)} %a_high.1, s32[64,768]{1,0:T(8,128)} %g_high.1, f32[64,768]{1,0:T(8,128)} %p_high.1, f32[64,768]{1,0:T(8,128)} %a_high.1, s32[64,768]{1,0:T(8,128)} %g_high.1), custom_call_target="tpu_custom_call" | custom-call | tf_op jit(solution)/shard_map/edges/pallas_call | solution.py:435
  2.3 3.2 %collective-permute-start = (f32[96,128]{1,0:T(8,128)}, f32[96,128]{1,0:T(8,128)S(1)}, u32[]{:S(2)}, u32[]{:S(2)}) collective-permute-start(f32[96,128]{1,0:T(8,128)} %get-tuple-element.14), channel_id=1, source_target_pairs={{0,1},{1,0},{2,3},{3,2},{4,5},{5,4},{6,7},{7,6},{8,9},{9,8},{10,11... | collective-permute-start | bytes 147464 | tf_op jit(solution)/shard_map/ppermute | solution.py:444
  5.5 0.9 %collective-permute-start.1 = (f32[96,128]{1,0:T(8,128)}, f32[96,128]{1,0:T(8,128)S(1)}, u32[]{:S(2)}, u32[]{:S(2)}) collective-permute-start(f32[96,128]{1,0:T(8,128)} %get-tuple-element.15), channel_id=1, source_target_pairs={{0,15},{1,2},{2,1},{3,4},{4,3},{5,6},{6,5},{7,8},{8,7},{9,10},{10,... | collective-permute-start | bytes 147464 | tf_op jit(solution)/shard_map/ppermute | solution.py:443
  6.4 0.0 copy-done.3
  6.4 0.0 copy-done.2
  6.4 0.0 copy-start.15
  6.4 0.0 copy-start.7
  6.4 0.0 copy-start.10
  6.5 0.0 copy-done.4
  6.5 0.0 copy-start.6
  6.5 0.0 copy-start.9
  6.5 0.0 copy-start.11
  6.5 0.0 copy-start.12
  6.5 0.0 copy-start.13
  6.6 0.0 copy-start.14
  6.6 0.0 copy-start.8
  6.6 0.1 pad.28.clone
  6.7 0.0 collective-permute-done
  6.7 4.1 %collective-permute-done.1 = f32[96,128]{1,0:T(8,128)S(1)} collective-permute-done((f32[96,128]{1,0:T(8,128)}, f32[96,128]{1,0:T(8,128)S(1)}, u32[]{:S(2)}, u32[]{:S(2)}) %collective-permute-start.1) | collective-permute-done | bytes 49184 | tf_op jit(solution)/shard_map/ppermute | solution.py:443
  10.8 0.0 copy-start.5
  10.8 0.1 fusion.2
  10.9 0.1 maximum_bitcast_fusion
  11.0 5.1 %collective-permute-start.3 = (f32[3,4,896]{2,1,0:T(4,128)S(1)}, f32[3,4,896]{2,1,0:T(4,128)S(1)}, u32[]{:S(2)}, u32[]{:S(2)}) collective-permute-start(f32[3,4,896]{2,1,0:T(4,128)S(1)} %get-tuple-element.31), channel_id=1, source_target_pairs={{0,240},{16,32},{32,16},{48,64},{64,48},{80,96},{96,80},{112,128},... | collective-permute-start | bytes 129032 | tf_op jit(solution)/shard_map/ppermute | solution.py:468
  16.0 0.0 collective-permute-start.2
  16.0 0.0 copy-done.15
  16.0 0.0 copy-done.11
  16.0 0.0 copy-done.12
  16.0 0.0 copy-done.13
  16.0 0.0 copy-done.14
  16.1 2.1 %cells.1 = (f32[3,64,768]{2,1,0:T(8,128)S(1)}, f32[4,64,768]{2,1,0:T(8,128)S(1)}, f32[8,256]{1,0:T(8,128)S(1)}) custom-call(f32[64,768]{1,0:T(8,128)S(1)} %copy-done.2, f32[64,768]{1,0:T(8,128)S(1)} %copy-done.3, s32[64,768]{1,0:T(8,128)S(1)} %copy-done.4, f32[1,256]{1,0:T(1,128)S(1)} %bitcast.24, f32[1,256]{1,0:T(1,128)S(1)} %bitcast.25, ...), custom_call_target="tpu_custom_call" | custom-call | tf_op jit(solution)/shard_map/cells/pallas_call | solution.py:475
  18.1 0.0 collective-permute-done.3
  18.2 1.0 %collective-permute-done.2 = f32[3,4,896]{2,1,0:T(4,128)S(1)} collective-permute-done((f32[3,4,896]{2,1,0:T(4,128)S(1)}, f32[3,4,896]{2,1,0:T(4,128)S(1)}, u32[]{:S(2)}, u32[]{:S(2)}) %collective-permute-start.2) | collective-permute-done | bytes 43040 | tf_op jit(solution)/shard_map/ppermute | solution.py:469
  19.2 0.0 copy-done.7
  19.2 0.0 copy-done.10
  19.2 0.0 copy-done.6
  19.2 0.0 copy-done.9
  19.2 0.0 copy-done.8
  19.3 0.0 copy-done.5
  19.3 0.0 copy-done.1
  19.3 0.0 copy-done
  19.3 7.5 %steps.1 = (f32[3,64,768]{2,1,0:T(8,128)}, f32[768,128]{1,0:T(8,128)S(1)}) custom-call(f32[3,64,768]{2,1,0:T(8,128)S(1)} %get-tuple-element.12.cells, f32[4,64,768]{2,1,0:T(8,128)S(1)} %get-tuple-element.13.props, f32[96,128]{1,0:T(8,128)S(1)} %get-tuple-element.28.from_high, f32[96,128]{1,0:T(8,128)S(1)} %get-tuple-element.27.from_low, ...), custom_call_target="tpu_custom_call" | custom-call | tf_op jit(solution)/shard_map/steps/pallas_call | solution.py:484
  26.8 12.6 %all_to_all.10 = f32[16,48,128]{2,1,0:T(8,128)S(1)} all-to-all(f32[16,48,128]{2,1,0:T(8,128)S(1)} %bitcast.23), channel_id=1, replica_groups=mesh['gx'=16,'gy'=16] {'gx'}, dimensions={0} | all-to-all | bytes 786432 | tf_op jit(solution)/shard_map/all_to_all | solution.py:496
  39.3 1.1 %along_x.1 = f32[256,128]{1,0:T(8,128)S(1)} custom-call(f32[768,128]{1,0:T(8,128)S(1)} %bitcast.20, bf16[256,1024]{1,0:T(8,128)(2,1)S(1)} %copy-done.1, bf16[256,1024]{1,0:T(8,128)(2,1)S(1)} %copy-done), custom_call_target="tpu_custom_call" | custom-call | tf_op jit(solution)/shard_map/along_x/pallas_call | solution.py:499
  40.4 21.8 %all_to_all.11 = f32[32,8,128]{2,1,0:T(8,128)S(1)} all-to-all(f32[32,8,128]{2,1,0:T(8,128)S(1)} %bitcast.21), channel_id=1, replica_groups={{0,1,2,3,4,5,6,7,8,9,10,11,12,13,14,15,16,17,18,19,20,21,22,23,24,25,26..., dimensions={0} | all-to-all | bytes 262144 | tf_op jit(solution)/shard_map/all_to_all | solution.py:511
  62.2 1.2 %along_y.1 = (f32[4,1024]{1,0:T(4,128)}, f32[4,1024]{1,0:T(4,128)}) custom-call(f32[256,128]{1,0:T(8,128)S(1)} %bitcast.22, bf16[128,256]{1,0:T(8,128)(2,1)S(1)} %copy-done.7, bf16[128,256]{1,0:T(8,128)(2,1)S(1)} %copy-done.6, f32[64,128]{1,0:T(8,128)S(1)} %copy-done.8, bf16[64,64]{1,0:T(8,128)(2,1)S(1)} %copy-done.10, bf16[64,64]{1,0:T(8,128)(2,1)S(1)} %copy-done.9), custom_call_target="tpu_custom_call" | custom-call | tf_op jit(solution)/shard_map/along_y/pallas_call | solution.py:515
  (8 shorter events, 0.1 us)
Async XLA Ops:
  0.6 5.8 %copy-start.4 = (s32[64,768]{1,0:T(8,128)S(1)}, s32[64,768]{1,0:T(8,128)}, u32[]{:S(2)}) copy-start(s32[64,768]{1,0:T(8,128)} %g_high.1) | copy-start | bytes 589828
  0.6 5.8 %copy-start.3 = (f32[64,768]{1,0:T(8,128)S(1)}, f32[64,768]{1,0:T(8,128)}, u32[]{:S(2)}) copy-start(f32[64,768]{1,0:T(8,128)} %a_high.1) | copy-start | bytes 589828
  0.7 5.8 %copy-start.2 = (f32[64,768]{1,0:T(8,128)S(1)}, f32[64,768]{1,0:T(8,128)}, u32[]{:S(2)}) copy-start(f32[64,768]{1,0:T(8,128)} %p_high.1) | copy-start | bytes 589828
  2.3 4.4 %collective-permute-start = (f32[96,128]{1,0:T(8,128)}, f32[96,128]{1,0:T(8,128)S(1)}, u32[]{:S(2)}, u32[]{:S(2)}) collective-permute-start(f32[96,128]{1,0:T(8,128)} %get-tuple-element.14), channel_id=1, source_target_pairs={{0,1},{1,0},{2,3},{3,2},{4,5},{5,4},{6,7},{7,6},{8,9},{9,8},{10,11... | collective-permute-start | bytes 147464 | tf_op jit(solution)/shard_map/ppermute | solution.py:444
  5.5 5.2 %collective-permute-start.1 = (f32[96,128]{1,0:T(8,128)}, f32[96,128]{1,0:T(8,128)S(1)}, u32[]{:S(2)}, u32[]{:S(2)}) collective-permute-start(f32[96,128]{1,0:T(8,128)} %get-tuple-element.15), channel_id=1, source_target_pairs={{0,15},{1,2},{2,1},{3,4},{4,3},{5,6},{6,5},{7,8},{8,7},{9,10},{10,... | collective-permute-start | bytes 147464 | tf_op jit(solution)/shard_map/ppermute | solution.py:443
  6.4 9.6 %copy-start.15 = (f32[3]{0:T(128)S(1)}, f32[3]{0:T(128)}, u32[]{:S(2)}) copy-start(f32[3]{0:T(128)} %applied.1) | copy-start | bytes 40
  6.4 12.8 %copy-start.7 = (bf16[128,256]{1,0:T(8,128)(2,1)S(1)}, bf16[128,256]{1,0:T(8,128)(2,1)}, u32[]{:S(2)}) copy-start(bf16[128,256]{1,0:T(8,128)(2,1)} %constant.45.clone.rest_2_.waves_hi) | copy-start | bytes 196612
  6.4 12.8 %copy-start.10 = (bf16[64,64]{1,0:T(8,128)(2,1)S(1)}, bf16[64,64]{1,0:T(8,128)(2,1)}, u32[]{:S(2)}) copy-start(bf16[64,64]{1,0:T(8,128)(2,1)} %constant.48.clone.rest_5_.last_hi) | copy-start | bytes 24580
  6.5 12.8 %copy-start.6 = (bf16[128,256]{1,0:T(8,128)(2,1)S(1)}, bf16[128,256]{1,0:T(8,128)(2,1)}, u32[]{:S(2)}) copy-start(bf16[128,256]{1,0:T(8,128)(2,1)} %constant.46.clone.rest_3_.waves_lo) | copy-start | bytes 196612
  6.5 12.7 %copy-start.9 = (bf16[64,64]{1,0:T(8,128)(2,1)S(1)}, bf16[64,64]{1,0:T(8,128)(2,1)}, u32[]{:S(2)}) copy-start(bf16[64,64]{1,0:T(8,128)(2,1)} %constant.49.clone.rest_6_.last_lo) | copy-start | bytes 24580
  6.5 9.5 %copy-start.11 = (f32[256]{0:T(256)S(1)}, f32[256]{0:T(256)}, u32[]{:S(2)}) copy-start(f32[256]{0:T(256)} %param.19) | copy-start | bytes 3076
  6.5 9.5 %copy-start.12 = (f32[256]{0:T(256)S(1)}, f32[256]{0:T(256)}, u32[]{:S(2)}) copy-start(f32[256]{0:T(256)} %param.20) | copy-start | bytes 3076
  6.5 9.5 %copy-start.13 = (f32[256]{0:T(256)S(1)}, f32[256]{0:T(256)}, u32[]{:S(2)}) copy-start(f32[256]{0:T(256)} %param.21) | copy-start | bytes 3076
  6.6 9.5 %copy-start.14 = (f32[256]{0:T(256)S(1)}, f32[256]{0:T(256)}, u32[]{:S(2)}) copy-start(f32[256]{0:T(256)} %param.22) | copy-start | bytes 3076
  6.6 12.7 %copy-start.8 = (f32[64,128]{1,0:T(8,128)S(1)}, f32[64,128]{1,0:T(8,128)}, u32[]{:S(2)}) copy-start(f32[64,128]{1,0:T(8,128)} %constant.47.clone.rest_4_.twiddle) | copy-start | bytes 98308
  10.8 8.5 %copy-start.5 = (bf16[768,256]{1,0:T(8,128)(2,1)S(1)}, bf16[768,256]{1,0:T(8,128)(2,1)}, u32[]{:S(2)}) copy-start(bf16[768,256]{1,0:T(8,128)(2,1)} %constant.50.clone.sum_z) | copy-start | bytes 1179652
  10.8 8.4 %copy-start.1 = (bf16[256,1024]{1,0:T(8,128)(2,1)S(1)}, bf16[256,1024]{1,0:T(8,128)(2,1)}, u32[]{:S(2)}) copy-start(bf16[256,1024]{1,0:T(8,128)(2,1)} %constant.43.clone.rest_0_.waves_hi) | copy-start | bytes 1572868
  10.9 8.3 %copy-start = (bf16[256,1024]{1,0:T(8,128)(2,1)S(1)}, bf16[256,1024]{1,0:T(8,128)(2,1)}, u32[]{:S(2)}) copy-start(bf16[256,1024]{1,0:T(8,128)(2,1)} %constant.44.clone.rest_1_.waves_lo) | copy-start | bytes 1572868
  11.0 7.2 %collective-permute-start.3 = (f32[3,4,896]{2,1,0:T(4,128)S(1)}, f32[3,4,896]{2,1,0:T(4,128)S(1)}, u32[]{:S(2)}, u32[]{:S(2)}) collective-permute-start(f32[3,4,896]{2,1,0:T(4,128)S(1)} %get-tuple-element.31), channel_id=1, source_target_pairs={{0,240},{16,32},{32,16},{48,64},{64,48},{80,96},{96,80},{112,128},... | collective-permute-start | bytes 129032 | tf_op jit(solution)/shard_map/ppermute | solution.py:468
  16.0 3.2 %collective-permute-start.2 = (f32[3,4,896]{2,1,0:T(4,128)S(1)}, f32[3,4,896]{2,1,0:T(4,128)S(1)}, u32[]{:S(2)}, u32[]{:S(2)}) collective-permute-start(f32[3,4,896]{2,1,0:T(4,128)S(1)} %get-tuple-element.32), channel_id=1, source_target_pairs={{0,16},{16,0},{32,48},{48,32},{64,80},{80,64},{96,112},{112,96},{1... | collective-permute-start | bytes 129032 | tf_op jit(solution)/shard_map/ppermute | solution.py:469

commit v5 on v4

--- a/solution.py
+++ b/solution.py
@@ -114,7 +114,18 @@
     return (2.0 * GAIN) * p * q / (p + q)
 
 
-def edges_kernel(p_low, a_low, g_low, p_high, a_high, g_high, first, second):
+def edges_kernel(
+    p_low, a_low, g_low, p_high, a_high, g_high,
+    stiffness, anisotropy, axis_polar, axis_azimuth, applied,
+    first, second, tables,
+):
+    ax, ay, az = start_cells(axis_polar[...], axis_azimuth[...])
+    root = jnp.sqrt(GAIN * anisotropy[...])
+    for r, row in enumerate((stiffness[...], root * ax, root * ay, root * az)):
+        tables[r : r + 1, :] = row
+    for c in range(3):
+        tables[4 + c : 5 + c, :] = jnp.full((1, NGRAIN), GAIN * applied[c])
+
     half = WX // 2
     lane = iota((half, 128), 1)
     even = lax.axis_index("gy") % 2 == 0
@@ -126,18 +137,11 @@
         second[i * half : (i + 1) * half, :] = jnp.where(even, l, h)
 
 
-def cells_kernel(
-    polar, azimuth, grains, stiffness, anisotropy, axis_polar, axis_azimuth, applied,
-    cells, props, tables,
-):
-    ax, ay, az = start_cells(axis_polar[...], axis_azimuth[...])
-    root = jnp.sqrt(GAIN * anisotropy[...])
-    rows = [stiffness[...], root * ax, root * ay, root * az]
-    for r, row in enumerate(rows):
-        tables[r : r + 1, :] = row
-    for c in range(3):
-        tables[4 + c : 5 + c, :] = jnp.full((1, NGRAIN), GAIN * applied[c])
-    tabs = grain_tables(rows)
+def cells_kernel(polar, azimuth, grains, tables, cells, props, ends):
+    tabs = grain_tables([tables[r : r + 1, :] for r in range(4)])
+    for i, src in enumerate((polar, azimuth, grains)):
+        ends[0, i] = src[0:4, :].astype(jnp.float32)
+        ends[1, i] = src[WX - 4 : WX, :].astype(jnp.float32)
 
     def body(s, carry):
         start = start_cells(strip(polar, s), strip(azimuth, s))
@@ -151,26 +155,69 @@
     lax.fori_loop(0, WX // 8, body, 0, unroll=2)
 
 
-def steps_kernel(
-    cells, props, from_high, from_low, halo_xh, halo_xl, tables, sum_z, *rest
-):
-    (
-        moment, payload, m0, m1, wt, cxu, cxd, cyu, cyd, czu, czd, cs, ux, uy, uz, raw,
-    ) = rest[-16:]
+def cell_rows(polar, azimuth, labels, tabs):
+    labels = labels.astype(jnp.int32)
+    return start_cells(polar, azimuth), [look_up(tab, labels) for tab in tabs]
+
+
+def coupling_rows(w, after, before):
+    xu = couple(w, up(w, after))
+    xd = couple(w, down(w, before))
+    yu = couple(w, pltpu.roll(w, LANES - NZ, 1))
+    yd = pltpu.roll(yu, NZ, 1)
+    lane = iota(w.shape, 1)
+    depth = jnp.where(lane < COLS + 64, lane, lane - LANES + 6 * NZ + COLS) % NZ
+    zu = jnp.where(depth != NZ - 1, couple(w, pltpu.roll(w, LANES - 1, 1)), 0.0)
+    zd = pltpu.roll(zu, 1, 1)
+    return xu, xd, yu, yd, zu, zd, (xu + xd) + (yu + yd) + (zu + zd)
+
+
+def applied_rows(tables):
+    return [jnp.broadcast_to(tables[4 + c : 5 + c, 0:1], (8, LANES)) for c in range(3)]
+
+
+def step(src, dst, s, after, before, coefs, row, field, width=LANES):
+    whole = [strip(src, s, c) for c in range(3)]
+    m = [v[:, 0:width] for v in whole]
+    xu, xd, yu, yd, zu, zd, total, *u = (
+        strip(coefs, row, r)[:, 0:width] for r in range(1, COEFS)
+    )
+    proj = u[0] * m[0] + u[1] * m[1] + u[2] * m[2]
+    h = []
+    for c in range(3):
+        f = yu * pltpu.roll(whole[c], LANES - NZ, 1)[:, 0:width]
+        f = f + yd * pltpu.roll(whole[c], NZ, 1)[:, 0:width]
+        f = f + zu * pltpu.roll(whole[c], LANES - 1, 1)[:, 0:width]
+        f = f + zd * pltpu.roll(whole[c], 1, 1)[:, 0:width]
+        f = f + xu * up(m[c], strip(src, after, c)[:, 0:width])
+        f = f + xd * down(m[c], strip(src, before, c)[:, 0:width])
+        h.append(f - total * m[c] + proj * u[c] + field[c][:, 0:width])
+    t = cross(m, h)
+    d = cross(m, t)
+    v = [m[c] - (t[c] + DAMPING * d[c]) for c in range(3)]
+    r = lax.rsqrt(v[0] * v[0] + v[1] * v[1] + v[2] * v[2])
+    for c in range(3):
+        put(dst, s, v[c] * r, c)
+
+
+COEFS = 11
+LAST = WX // 8 - 1
+
+
+def inner_strips(body):
+    def one(s, carry):
+        body(s)
+        return carry
+
+    lax.fori_loop(1, LAST, one, 0, unroll=3)
+
+
+def inner_kernel(cells, props, from_high, from_low, tables, m0, m1, coefs):
     tabs = grain_tables([tables[r : r + 1, :] for r in range(4)])
     for c in range(3):
-        m0[c, 0:WX, 0:COLS] = cells[c]
-    for r, ref in enumerate((wt, ux, uy, uz)):
-        ref[0:WX, 0:COLS] = props[r]
-
-    def fill(rows, cols, polar, azimuth, labels):
-        start = start_cells(polar, azimuth)
-        for c in range(3):
-            m0[c, rows, cols] = start[c]
-        labels = labels.astype(jnp.int32)
-        for r, ref in enumerate((wt, ux, uy, uz)):
-            ref[rows, cols] = look_up(tabs[r], labels)
-
+        m0[c, :, 0:COLS] = cells[c]
+    for r, i in enumerate((0, 8, 9, 10)):
+        coefs[i, :, 0:COLS] = props[r]
     near = iota((8, 128), 1) < 64
 
     def side(bottom):
@@ -182,80 +229,71 @@
                 if bottom:
                     high, low = pltpu.roll(high, 80, 1), pltpu.roll(low, 48, 1)
                 values.append(jnp.where(near, high, low))
-            start = s + (WX // 16 if bottom else 0)
-            rows = pl.ds(pl.multiple_of(start * 8, 8), 8)
-            fill(rows, slice(COLS, LANES), *values)
+            start, found = cell_rows(*values, tabs)
+            first = s + (WX // 16 if bottom else 0)
+            rows = pl.ds(pl.multiple_of(first * 8, 8), 8)
+            for c in range(3):
+                m0[c, rows, COLS:LANES] = start[c]
+            for r, i in enumerate((0, 8, 9, 10)):
+                coefs[i, rows, COLS:LANES] = found[r]
             return carry
 
         lax.fori_loop(0, WX // 16, body, 0, unroll=4)
 
     side(False)
     side(True)
+
+    def couplings(s):
+        found = coupling_rows(*(strip(coefs, i, 0) for i in (s, s + 1, s - 1)))
+        for r, value in enumerate(found):
+            put(coefs, s, value, 1 + r)
+
+    inner_strips(couplings)
+    field = applied_rows(tables)
+    inner_strips(lambda s: step(m0, m1, s, s + 1, s - 1, coefs, s, field))
+
+
+def steps_kernel(
+    first0, first1, coefs, halo_xh, halo_xl, tables, sum_z, *rest
+):
+    moment, payload, m0, m1, rim, raw = rest[-6:]
+    tabs = grain_tables([tables[r : r + 1, :] for r in range(4)])
     for i in range(3):
         raw[i, 0:4, :] = halo_xh[i]
         raw[i, 4:8, :] = halo_xl[i]
-    fill(slice(WX, ROWS), slice(0, LANES), raw[0], raw[1], raw[2])
-
-    def nxt(s):
-        return jnp.where(s == STRIPS - 1, 0, s + 1)
-
-    def prv(s):
-        return jnp.where(s == 0, STRIPS - 1, s - 1)
-
-    def couplings(s, carry):
-        w = strip(wt, s)
-        xu = couple(w, up(w, strip(wt, nxt(s))))
-        xd = couple(w, down(w, strip(wt, prv(s))))
-        yu = couple(w, pltpu.roll(w, LANES - NZ, 1))
-        yd = pltpu.roll(yu, NZ, 1)
-        lane = iota(w.shape, 1)
-        depth = jnp.where(lane < COLS + 64, lane, lane - LANES + 6 * NZ + COLS) % NZ
-        zu = jnp.where(depth != NZ - 1, couple(w, pltpu.roll(w, LANES - 1, 1)), 0.0)
-        zd = pltpu.roll(zu, 1, 1)
-        for ref, value in zip((cxu, cxd, cyu, cyd, czu, czd), (xu, xd, yu, yd, zu, zd)):
-            put(ref, s, value)
-        put(cs, s, (xu + xd) + (yu + yd) + (zu + zd))
-        return carry
-
-    lax.fori_loop(0, STRIPS, couplings, 0, unroll=3)
-    field = [jnp.broadcast_to(tables[4 + c : 5 + c, 0:1], (8, LANES)) for c in range(3)]
-
-    def step(src, dst, s, width):
-        after, before = nxt(s), prv(s)
-        whole = [strip(src, s, c) for c in range(3)]
-        m = [v[:, 0:width] for v in whole]
-        u = [strip(r, s)[:, 0:width] for r in (ux, uy, uz)]
-        xu, xd, yu, yd, zu, zd, total = (
-            strip(r, s)[:, 0:width] for r in (cxu, cxd, cyu, cyd, czu, czd, cs)
-        )
-        proj = u[0] * m[0] + u[1] * m[1] + u[2] * m[2]
-        h = []
-        for c in range(3):
-            f = yu * pltpu.roll(whole[c], LANES - NZ, 1)[:, 0:width]
-            f = f + yd * pltpu.roll(whole[c], NZ, 1)[:, 0:width]
-            f = f + zu * pltpu.roll(whole[c], LANES - 1, 1)[:, 0:width]
-            f = f + zd * pltpu.roll(whole[c], 1, 1)[:, 0:width]
-            f = f + xu * up(m[c], strip(src, after, c)[:, 0:width])
-            f = f + xd * down(m[c], strip(src, before, c)[:, 0:width])
-            h.append(f - total * m[c] + proj * u[c] + field[c][:, 0:width])
-        t = cross(m, h)
-        d = cross(m, t)
-        v = [m[c] - (t[c] + DAMPING * d[c]) for c in range(3)]
-        r = lax.rsqrt(v[0] * v[0] + v[1] * v[1] + v[2] * v[2])
-        for c in range(3):
-            put(dst, s, v[c] * r, c)
-
-    def one(src, dst, count, unroll, width=LANES):
-        def body(s, carry):
-            step(src, dst, s, width)
-            return carry
-
-        lax.fori_loop(0, count, body, 0, unroll=unroll)
-
-    one(m0, m1, STRIPS, 3)
-    one(m1, m0, STRIPS, 3)
-    one(m0, m1, STRIPS, 3)
-    one(m1, moment, STRIPS - 1, 4, COLS)
+    start, found = cell_rows(raw[0], raw[1], raw[2], tabs)
+    for c in range(3):
+        m0[c, 0:16, :] = first0[c, 0:16, :]
+        m0[c, WX - 16 : WX, :] = first0[c, WX - 16 : WX, :]
+        m0[c, WX:ROWS, :] = start[c]
+        m1[c, 8 : WX - 8, :] = first1[c, 8 : WX - 8, :]
+    for r, i in enumerate((0, 8, 9, 10)):
+        rim[i, 0:8, :] = coefs[i, WX - 8 : WX, :]
+        rim[i, 8:16, :] = found[r]
+        rim[i, 16:24, :] = coefs[i, 0:8, :]
+    stiff = [coefs[0, WX - 16 : WX - 8, :]]
+    stiff += [rim[0, 8 * i : 8 * i + 8, :] for i in range(3)] + [coefs[0, 8:16, :]]
+    for i in range(3):
+        for r, value in enumerate(coupling_rows(stiff[i + 1], stiff[i + 2], stiff[i])):
+            rim[1 + r, 8 * i : 8 * i + 8, :] = value
+    field = applied_rows(tables)
+
+    def outer(src, dst, width=LANES):
+        for i, s in enumerate((LAST, LAST + 1, 0)):
+            if s > LAST and width < LANES:
+                continue
+            after, before = (s + 1) % STRIPS, (s - 1) % STRIPS
+            step(src, dst, s, after, before, rim, i, field, width)
+
+    def inner(src, dst, width=LANES):
+        inner_strips(lambda s: step(src, dst, s, s + 1, s - 1, coefs, s, field, width))
+
+    outer(m0, m1)
+    for src, dst in ((m1, m0), (m0, m1)):
+        outer(src, dst)
+        inner(src, dst)
+    outer(m1, moment, COLS)
+    inner(m1, moment, COLS)
 
     m = jnp.concatenate([moment[c] for c in range(3)], axis=0)
     hi, lo = split(m)
@@ -430,30 +468,42 @@
     fields = (polar, azimuth, grains)
     params = pltpu.CompilerParams(vmem_limit_bytes=16 << 20)
     smem = [pl.BlockSpec(memory_space=pltpu.SMEM)]
+    per_grain = [
+        v.reshape(1, NGRAIN) for v in (stiffness, anisotropy, axis_polar, axis_azimuth)
+    ]
     first = pl.BlockSpec((WX, 128), lambda i: (0, 0))
     last = pl.BlockSpec((WX, 128), lambda i: (0, COLS // 128 - 1))
-    to_first, to_second = pl.pallas_call(
+    to_first, to_second, tables = pl.pallas_call(
         edges_kernel,
         grid=(1,),
-        out_shape=(f32(3 * WX // 2, 128), f32(3 * WX // 2, 128)),
-        in_specs=[first] * 3 + [last] * 3,
-        out_specs=tuple(vmem(2)),
+        out_shape=(f32(3 * WX // 2, 128), f32(3 * WX // 2, 128), f32(8, NGRAIN)),
+        in_specs=[first] * 3 + [last] * 3 + vmem(4) + smem,
+        out_specs=tuple(vmem(3)),
         name="edges",
-    )(*fields, *fields)
+    )(*fields, *fields, *per_grain, applied_field)
     got_second = lax.ppermute(to_second, "gy", odd_pairs)
     got_first = lax.ppermute(to_first, "gy", even_pairs)
     from_high = jnp.where(even_y, got_first, got_second)
     from_low = jnp.where(even_y, got_second, got_first)
 
-    def edge(start, row, high, low):
+    cells, props, ends = pl.pallas_call(
+        cells_kernel,
+        out_shape=(f32(3, WX, COLS), f32(4, WX, COLS), f32(2, 3, 4, COLS)),
+        in_specs=vmem(4),
+        out_specs=tuple(vmem(3)),
+        compiler_params=params,
+        name="cells",
+    )(*fields, tables)
+
+    def edge(end, row, high, low):
         blank = jnp.zeros((4, 32), jnp.float32)
         parts = []
-        for i, f in enumerate(fields):
+        for i in range(3):
             halo = slice(i * WX // 2 + row, i * WX // 2 + row + 4)
             parts.append(
                 jnp.concatenate(
                     [
-                        f[start : start + 4].astype(jnp.float32),
+                        ends[end, i],
                         from_high[halo, high : high + 48],
                         blank,
                         from_low[halo, low : low + 48],
@@ -464,34 +514,31 @@
         return jnp.stack(parts)
 
     low_edge = edge(0, 0, 0, 80)
-    high_edge = edge(WX - 4, WX // 2 - 4, 48, 32)
+    high_edge = edge(1, WX // 2 - 4, 48, 32)
     got_second = lax.ppermute(jnp.where(even_x, low_edge, high_edge), "gx", odd_pairs)
     got_first = lax.ppermute(jnp.where(even_x, high_edge, low_edge), "gx", even_pairs)
     halo_xh = jnp.where(even_x, got_first, got_second)
     halo_xl = jnp.where(even_x, got_second, got_first)
-    per_grain = [
-        v.reshape(1, NGRAIN) for v in (stiffness, anisotropy, axis_polar, axis_azimuth)
-    ]
-    cells, props, tables = pl.pallas_call(
-        cells_kernel,
-        out_shape=(f32(3, WX, COLS), f32(4, WX, COLS), f32(8, NGRAIN)),
-        in_specs=vmem(7) + smem,
+    first0, first1, coefs = pl.pallas_call(
+        inner_kernel,
+        out_shape=(f32(3, WX, LANES), f32(3, WX, LANES), f32(COEFS, WX, LANES)),
+        in_specs=vmem(5),
         out_specs=tuple(vmem(3)),
         compiler_params=params,
-        name="cells",
-    )(*fields, *per_grain, applied_field)
+        name="inner",
+    )(cells, props, from_high, from_low, tables)
     tables_x, tables_y = x_tables(), y_tables()
     moment, payload = pl.pallas_call(
         steps_kernel,
         out_shape=(f32(3, WX, COLS), f32(16 * 48, 128)),
-        in_specs=vmem(8 + len(tables_x) + len(tables_y)),
+        in_specs=vmem(7 + len(tables_x) + len(tables_y)),
         out_specs=tuple(vmem(2)),
         scratch_shapes=[pltpu.VMEM((3, ROWS, LANES), jnp.float32)] * 2
-        + [pltpu.VMEM((ROWS, LANES), jnp.float32)] * 11
+        + [pltpu.VMEM((COEFS, 24, LANES), jnp.float32)]
         + [pltpu.VMEM((3, 8, LANES), jnp.float32)],
         compiler_params=params,
         name="steps",
-    )(cells, props, from_high, from_low, halo_xh, halo_xl, tables, sum_matrix(), *tables_x, *tables_y)
+    )(first0, first1, coefs, halo_xh, halo_xl, tables, sum_matrix(), *tables_x, *tables_y)
 
     columns = lax.all_to_all(
         payload.reshape(16, 48, 128), "gx", split_axis=0, concat_axis=0, tiled=True

time: 63.6 us -> 62.7 us (0.986)
  waiting for transfers between devices: 5.09 us -> 0.01 us
  local copies, waits for them, and re-layouts: 0.25 us -> 4.38 us
  starting transfers between devices: 9.19 us -> 12.1 us
  blocking collectives: 34.4 us -> 31.5 us
    all_to_all x1, blocking collectives: 21.8 us -> 16.5 us  [shards(): lax.all_to_all(rows.reshape(32, 8, 128), ('gx', 'gy'), split_axis=0, conc...]
    unnamed x32 -> x26, local copies, waits for them, and re-layouts: 0.08 us -> 4.22 us
    ppermute x1, waiting for transfers between devices: 4.06 us -> 0.01 us  [shards(): got_second = lax.ppermute(to_second, 'gy', odd_pairs)]
    ppermute x1, starting transfers between devices: 0.9 us -> 4.13 us  [shards(): got_second = lax.ppermute(to_second, 'gy', odd_pairs)]
    all_to_all x1, blocking collectives: 12.6 us -> 15 us  [shards(): lax.all_to_all(payload.reshape(16, 48, 128), 'gx', split_axis=0, concat_a...]
    pallas_call x0 -> x1, Pallas kernels: none -> 2.27 us  [shards(): pl.pallas_call(inner_kernel, out_shape=(f32(3, WX, LANES), f32(3, WX, LAN...]
    pallas_call x1, Pallas kernels: 7.47 us -> 5.73 us  [shards(): pl.pallas_call(steps_kernel, out_shape=(f32(3, WX, COLS), f32(16 * 48, 12...]
    ppermute x1, waiting for transfers between devices: 1.03 us -> 0.01 us  [shards(): lax.ppermute(jnp.where(even_x, high_edge, low_edge), 'gx', even_pairs)]
  transfers between devices with their start and end apart: 4 -> 4, of which waited for: 2 -> 0; matrix products, arithmetic and copies ran while one was open for 0% -> 0% of each run, Pallas kernels for 3% -> 6%
where the time goes in v5:
time: 62.7 us; the launch traced here: 62.4 us
  blocking collectives  31.5 us (50%)
  Pallas kernels  13.5 us (22%)
  starting transfers between devices  12.1 us (19%)
  local copies, waits for them, and re-layouts  4.38 us (7%)
  between operations  0.84 us (1%)
    all_to_all x1, blocking collectives, shards(): lax.all_to_all(rows.reshape(32, 8, 128), ('gx', 'gy'), split_axis=0, conc...  16.5 us
    all_to_all x1, blocking collectives, shards(): lax.all_to_all(payload.reshape(16, 48, 128), 'gx', split_axis=0, concat_a...  15 us
    pallas_call x1, Pallas kernels, shards(): pl.pallas_call(steps_kernel, out_shape=(f32(3, WX, COLS), f32(16 * 48, 12...  5.73 us
    ppermute x1, starting transfers between devices, shards(): lax.ppermute(jnp.where(even_x, low_edge, high_edge), 'gx', odd_pairs)  5.69 us
    unnamed x26, local copies, waits for them, and re-layouts  4.22 us
    ppermute x1, starting transfers between devices, shards(): got_second = lax.ppermute(to_second, 'gy', odd_pairs)  4.13 us
    ppermute x1, starting transfers between devices, shards(): got_first = lax.ppermute(to_first, 'gy', even_pairs)  2.28 us
    pallas_call x1, Pallas kernels, shards(): pl.pallas_call(inner_kernel, out_shape=(f32(3, WX, LANES), f32(3, WX, LAN...  2.27 us
  transfers between devices with their start and end apart: 4, of which 0 were waited for; matrix products, arithmetic and copies ran while one was open for 0% of the time, Pallas kernels for 6%

profile of v5, /device:TPU:1, one launch (start us, length us, event | category | flops | bytes accessed | tf_op | source)
XLA Modules:
  0.0 62.4 jit_solution(7510567783014979813)
XLA Ops:
  0.6 0.0 copy-start
  0.6 0.0 copy-start.1
  0.7 0.0 copy-start.6
  0.7 0.0 copy-start.7
  0.7 0.0 copy-start.11
  0.7 1.7 %edges.1 = (f32[96,128]{1,0:T(8,128)}, f32[96,128]{1,0:T(8,128)}, f32[8,256]{1,0:T(8,128)}) custom-call(f32[64,768]{1,0:T(8,128)} %polar.1, f32[64,768]{1,0:T(8,128)} %azimuth.1, s32[64,768]{1,0:T(8,128)} %grains.1, f32[64,768]{1,0:T(8,128)} %polar.1, f32[64,768]{1,0:T(8,128)} %azimuth.1, s32[64,768]{1,0:T(8,128)} %grains.1, f32[1,256]{1,0:T(1,128)} %bitcast.36, ...), custom_call_target="tpu_custom_call" | custom-call | tf_op jit(solution)/shard_map/edges/pallas_call | solution.py:476
  2.4 4.1 %collective-permute-start.1 = (f32[96,128]{1,0:T(8,128)}, f32[96,128]{1,0:T(8,128)S(1)}, u32[]{:S(2)}, u32[]{:S(2)}) collective-permute-start(f32[96,128]{1,0:T(8,128)} %get-tuple-element.20), channel_id=1, source_target_pairs={{0,15},{1,2},{2,1},{3,4},{4,3},{5,6},{6,5},{7,8},{8,7},{9,10},{10,... | collective-permute-start | bytes 147464 | tf_op jit(solution)/shard_map/ppermute | solution.py:484
  6.5 2.3 %collective-permute-start = (f32[96,128]{1,0:T(8,128)}, f32[96,128]{1,0:T(8,128)S(1)}, u32[]{:S(2)}, u32[]{:S(2)}) collective-permute-start(f32[96,128]{1,0:T(8,128)} %get-tuple-element.19), channel_id=1, source_target_pairs={{0,1},{1,0},{2,3},{3,2},{4,5},{5,4},{6,7},{7,6},{8,9},{9,8},{10,11... | collective-permute-start | bytes 147464 | tf_op jit(solution)/shard_map/ppermute | solution.py:485
  8.8 0.0 copy-start.2
  8.8 0.9 %copy-done.2 = f32[64,768]{1,0:T(8,128)S(1)} copy-done((f32[64,768]{1,0:T(8,128)S(1)}, f32[64,768]{1,0:T(8,128)}, u32[]{:S(2)}) %copy-start.2) | copy-done | bytes 196632
  9.7 0.0 copy-start.3
  9.7 0.9 %copy-done.3 = f32[64,768]{1,0:T(8,128)S(1)} copy-done((f32[64,768]{1,0:T(8,128)S(1)}, f32[64,768]{1,0:T(8,128)}, u32[]{:S(2)}) %copy-start.3) | copy-done | bytes 196632
  10.7 0.0 copy-start.4
  10.7 0.9 %copy-done.4 = s32[64,768]{1,0:T(8,128)S(1)} copy-done((s32[64,768]{1,0:T(8,128)S(1)}, s32[64,768]{1,0:T(8,128)}, u32[]{:S(2)}) %copy-start.4) | copy-done | bytes 196632
  11.6 0.0 copy-start.9
  11.6 0.7 %copy-done.9 = f32[8,256]{1,0:T(8,128)S(1)} copy-done((f32[8,256]{1,0:T(8,128)S(1)}, f32[8,256]{1,0:T(8,128)}, u32[]{:S(2)}) %copy-start.9) | copy-done | bytes 8216
  12.3 0.0 copy-start.5
  12.3 0.0 copy-start.8
  12.3 0.0 copy-start.12
  12.3 1.5 %cells.1 = (f32[3,64,768]{2,1,0:T(8,128)S(1)}, f32[4,64,768]{2,1,0:T(8,128)S(1)}, f32[2,3,4,768]{3,2,1,0:T(4,128)S(1)}) custom-call(f32[64,768]{1,0:T(8,128)S(1)} %copy-done.2, f32[64,768]{1,0:T(8,128)S(1)} %copy-done.3, s32[64,768]{1,0:T(8,128)S(1)} %copy-done.4, f32[8,256]{1,0:T(8,128)S(1)} %copy-done.9), custom_call_target="tpu_custom_call" | custom-call | tf_op jit(solution)/shard_map/cells/pallas_call | solution.py:489
  13.9 0.1 pad.28.clone
  13.9 0.0 collective-permute-done.1
  13.9 0.0 collective-permute-done
  14.0 0.1 fusion
  14.0 0.1 maximum_bitcast_fusion
  14.2 5.7 %collective-permute-start.3 = (f32[3,4,896]{2,1,0:T(4,128)S(1)}, f32[3,4,896]{2,1,0:T(4,128)S(1)}, u32[]{:S(2)}, u32[]{:S(2)}) collective-permute-start(f32[3,4,896]{2,1,0:T(4,128)S(1)} %get-tuple-element.33), channel_id=1, source_target_pairs={{0,240},{16,32},{32,16},{48,64},{64,48},{80,96},{96,80},{112,128},... | collective-permute-start | bytes 129032 | tf_op jit(solution)/shard_map/ppermute | solution.py:518
  19.8 0.0 collective-permute-start.2
  19.9 0.0 copy-start.10
  19.9 0.7 %copy-done.10 = f32[8,256]{1,0:T(8,128)S(1)} copy-done((f32[8,256]{1,0:T(8,128)S(1)}, f32[8,256]{1,0:T(8,128)}, u32[]{:S(2)}) %copy-start.10) | copy-done | bytes 8216
  20.5 2.3 %inner.1 = (f32[3,64,896]{2,1,0:T(8,128)S(1)}, f32[3,64,896]{2,1,0:T(8,128)S(1)}, f32[11,64,896]{2,1,0:T(8,128)S(1)}) custom-call(f32[3,64,768]{2,1,0:T(8,128)S(1)} %get-tuple-element.17.cells, f32[4,64,768]{2,1,0:T(8,128)S(1)} %get-tuple-element.18.props, f32[96,128]{1,0:T(8,128)S(1)} %get-tuple-element.30.from_high, ...), custom_call_target="tpu_custom_call" | custom-call | tf_op jit(solution)/shard_map/inner/pallas_call | solution.py:522
  22.8 0.0 collective-permute-done.3
  22.8 0.0 collective-permute-done.2
  22.9 0.0 copy-done
  22.9 0.0 copy-done.1
  22.9 0.0 copy-done.6
  22.9 0.0 copy-done.7
  22.9 0.0 copy-done.11
  22.9 0.0 copy-done.5
  22.9 0.0 copy-done.8
  22.9 0.0 copy-done.12
  23.0 5.7 %steps.1 = (f32[3,64,768]{2,1,0:T(8,128)}, f32[768,128]{1,0:T(8,128)S(1)}) custom-call(f32[3,64,896]{2,1,0:T(8,128)S(1)} %get-tuple-element.21.first0, f32[3,64,896]{2,1,0:T(8,128)S(1)} %get-tuple-element.22.first1, f32[11,64,896]{2,1,0:T(8,128)S(1)} %get-tuple-element.23.coefs, f32[3,4,896]{2,1,0:T(4,128)S(1)} %get-tuple-element.32.halo_xh, ...), custom_call_target="tpu_custom_call" | custom-call | tf_op jit(solution)/shard_map/steps/pallas_call | solution.py:531
  28.7 15.0 %all_to_all.10 = f32[16,48,128]{2,1,0:T(8,128)S(1)} all-to-all(f32[16,48,128]{2,1,0:T(8,128)S(1)} %bitcast.35), channel_id=1, replica_groups=mesh['gx'=16,'gy'=16] {'gx'}, dimensions={0} | all-to-all | bytes 786432 | tf_op jit(solution)/shard_map/all_to_all | solution.py:543
  43.7 1.1 %along_x.1 = f32[256,128]{1,0:T(8,128)S(1)} custom-call(f32[768,128]{1,0:T(8,128)S(1)} %bitcast.32, bf16[256,1024]{1,0:T(8,128)(2,1)S(1)} %copy-done, bf16[256,1024]{1,0:T(8,128)(2,1)S(1)} %copy-done.1), custom_call_target="tpu_custom_call" | custom-call | tf_op jit(solution)/shard_map/along_x/pallas_call | solution.py:546
  44.8 16.5 %all_to_all.11 = f32[32,8,128]{2,1,0:T(8,128)S(1)} all-to-all(f32[32,8,128]{2,1,0:T(8,128)S(1)} %bitcast.33), channel_id=1, replica_groups={{0,1,2,3,4,5,6,7,8,9,10,11,12,13,14,15,16,17,18,19,20,21,22,23,24,25,26..., dimensions={0} | all-to-all | bytes 262144 | tf_op jit(solution)/shard_map/all_to_all | solution.py:558
  61.2 1.2 %along_y.1 = (f32[4,1024]{1,0:T(4,128)}, f32[4,1024]{1,0:T(4,128)}) custom-call(f32[256,128]{1,0:T(8,128)S(1)} %bitcast.34, bf16[128,256]{1,0:T(8,128)(2,1)S(1)} %copy-done.6, bf16[128,256]{1,0:T(8,128)(2,1)S(1)} %copy-done.7, f32[64,128]{1,0:T(8,128)S(1)} %copy-done.8, bf16[64,64]{1,0:T(8,128)(2,1)S(1)} %copy-done.11, bf16[64,64]{1,0:T(8,128)(2,1)S(1)} %copy-done.12), custom_call_target="tpu_custom_call" | custom-call | tf_op jit(solution)/shard_map/along_y/pallas_call | solution.py:562
  (5 shorter events, 0.1 us)
Async XLA Ops:
  0.6 22.2 %copy-start = (bf16[256,1024]{1,0:T(8,128)(2,1)S(1)}, bf16[256,1024]{1,0:T(8,128)(2,1)}, u32[]{:S(2)}) copy-start(bf16[256,1024]{1,0:T(8,128)(2,1)} %constant.43.clone.rest_0_.waves_hi) | copy-start | bytes 1572868
  0.6 22.2 %copy-start.1 = (bf16[256,1024]{1,0:T(8,128)(2,1)S(1)}, bf16[256,1024]{1,0:T(8,128)(2,1)}, u32[]{:S(2)}) copy-start(bf16[256,1024]{1,0:T(8,128)(2,1)} %constant.44.clone.rest_1_.waves_lo) | copy-start | bytes 1572868
  0.7 22.2 %copy-start.6 = (bf16[128,256]{1,0:T(8,128)(2,1)S(1)}, bf16[128,256]{1,0:T(8,128)(2,1)}, u32[]{:S(2)}) copy-start(bf16[128,256]{1,0:T(8,128)(2,1)} %constant.45.clone.rest_2_.waves_hi) | copy-start | bytes 196612
  0.7 22.2 %copy-start.7 = (bf16[128,256]{1,0:T(8,128)(2,1)S(1)}, bf16[128,256]{1,0:T(8,128)(2,1)}, u32[]{:S(2)}) copy-start(bf16[128,256]{1,0:T(8,128)(2,1)} %constant.46.clone.rest_3_.waves_lo) | copy-start | bytes 196612
  0.7 22.2 %copy-start.11 = (bf16[64,64]{1,0:T(8,128)(2,1)S(1)}, bf16[64,64]{1,0:T(8,128)(2,1)}, u32[]{:S(2)}) copy-start(bf16[64,64]{1,0:T(8,128)(2,1)} %constant.48.clone.rest_5_.last_hi) | copy-start | bytes 24580
  2.4 11.6 %collective-permute-start.1 = (f32[96,128]{1,0:T(8,128)}, f32[96,128]{1,0:T(8,128)S(1)}, u32[]{:S(2)}, u32[]{:S(2)}) collective-permute-start(f32[96,128]{1,0:T(8,128)} %get-tuple-element.20), channel_id=1, source_target_pairs={{0,15},{1,2},{2,1},{3,4},{4,3},{5,6},{6,5},{7,8},{8,7},{9,10},{10,... | collective-permute-start | bytes 147464 | tf_op jit(solution)/shard_map/ppermute | solution.py:484
  6.5 7.4 %collective-permute-start = (f32[96,128]{1,0:T(8,128)}, f32[96,128]{1,0:T(8,128)S(1)}, u32[]{:S(2)}, u32[]{:S(2)}) collective-permute-start(f32[96,128]{1,0:T(8,128)} %get-tuple-element.19), channel_id=1, source_target_pairs={{0,1},{1,0},{2,3},{3,2},{4,5},{5,4},{6,7},{7,6},{8,9},{9,8},{10,11... | collective-permute-start | bytes 147464 | tf_op jit(solution)/shard_map/ppermute | solution.py:485
  8.8 0.9 %copy-start.2 = (f32[64,768]{1,0:T(8,128)S(1)}, f32[64,768]{1,0:T(8,128)}, u32[]{:S(2)}) copy-start(f32[64,768]{1,0:T(8,128)} %polar.1) | copy-start | bytes 589828
  9.7 0.9 %copy-start.3 = (f32[64,768]{1,0:T(8,128)S(1)}, f32[64,768]{1,0:T(8,128)}, u32[]{:S(2)}) copy-start(f32[64,768]{1,0:T(8,128)} %azimuth.1) | copy-start | bytes 589828
  10.7 0.9 %copy-start.4 = (s32[64,768]{1,0:T(8,128)S(1)}, s32[64,768]{1,0:T(8,128)}, u32[]{:S(2)}) copy-start(s32[64,768]{1,0:T(8,128)} %grains.1) | copy-start | bytes 589828
  11.6 0.7 %copy-start.9 = (f32[8,256]{1,0:T(8,128)S(1)}, f32[8,256]{1,0:T(8,128)}, u32[]{:S(2)}) copy-start(f32[8,256]{1,0:T(8,128)} %get-tuple-element.16.tables) | copy-start | bytes 24580
  12.3 10.7 %copy-start.5 = (bf16[768,256]{1,0:T(8,128)(2,1)S(1)}, bf16[768,256]{1,0:T(8,128)(2,1)}, u32[]{:S(2)}) copy-start(bf16[768,256]{1,0:T(8,128)(2,1)} %constant.50.clone.sum_z) | copy-start | bytes 1179652
  12.3 10.7 %copy-start.8 = (f32[64,128]{1,0:T(8,128)S(1)}, f32[64,128]{1,0:T(8,128)}, u32[]{:S(2)}) copy-start(f32[64,128]{1,0:T(8,128)} %constant.47.clone.rest_4_.twiddle) | copy-start | bytes 98308
  12.3 10.7 %copy-start.12 = (bf16[64,64]{1,0:T(8,128)(2,1)S(1)}, bf16[64,64]{1,0:T(8,128)(2,1)}, u32[]{:S(2)}) copy-start(bf16[64,64]{1,0:T(8,128)(2,1)} %constant.49.clone.rest_6_.last_lo) | copy-start | bytes 24580
  14.2 8.7 %collective-permute-start.3 = (f32[3,4,896]{2,1,0:T(4,128)S(1)}, f32[3,4,896]{2,1,0:T(4,128)S(1)}, u32[]{:S(2)}, u32[]{:S(2)}) collective-permute-start(f32[3,4,896]{2,1,0:T(4,128)S(1)} %get-tuple-element.33), channel_id=1, source_target_pairs={{0,240},{16,32},{32,16},{48,64},{64,48},{80,96},{96,80},{112,128},... | collective-permute-start | bytes 129032 | tf_op jit(solution)/shard_map/ppermute | solution.py:518
  19.8 3.0 %collective-permute-start.2 = (f32[3,4,896]{2,1,0:T(4,128)S(1)}, f32[3,4,896]{2,1,0:T(4,128)S(1)}, u32[]{:S(2)}, u32[]{:S(2)}) collective-permute-start(f32[3,4,896]{2,1,0:T(4,128)S(1)} %get-tuple-element.34), channel_id=1, source_target_pairs={{0,16},{16,0},{32,48},{48,32},{64,80},{80,64},{96,112},{112,96},{1... | collective-permute-start | bytes 129032 | tf_op jit(solution)/shard_map/ppermute | solution.py:519
  19.9 0.7 %copy-start.10 = (f32[8,256]{1,0:T(8,128)S(1)}, f32[8,256]{1,0:T(8,128)}, u32[]{:S(2)}) copy-start(f32[8,256]{1,0:T(8,128)} %get-tuple-element.16.tables) | copy-start | bytes 24580

commit v6 on v5

--- a/solution.py
+++ b/solution.py
@@ -137,7 +137,8 @@
         second[i * half : (i + 1) * half, :] = jnp.where(even, l, h)
 
 
-def cells_kernel(polar, azimuth, grains, tables, cells, props, ends):
+def cells_kernel(polar, azimuth, grains, tables, cells, props, ends, same_tables):
+    same_tables[...] = tables[...]
     tabs = grain_tables([tables[r : r + 1, :] for r in range(4)])
     for i, src in enumerate((polar, azimuth, grains)):
         ends[0, i] = src[0:4, :].astype(jnp.float32)
@@ -308,7 +309,7 @@
             merged = rows[3]
             for g in range(3):
                 merged = jnp.where(block == (g + c) % 4, rows[g], merged)
-            for peer in range(half, 16, 2):
+            for peer in range(8 * half, 8 * half + 8):
                 payload[peer * 48 + 16 * c : peer * 48 + 16 * c + 16, :] = merged
 
 
@@ -321,11 +322,9 @@
 
 
 def x_kernel(got, waves_hi, waves_lo, out, d_hi, d_lo):
-    pair = lax.axis_index("gx") // 2
-    turn = (pair * iota((8, 128), 0) + 4) % 8 - 4
-    sine, cosine = sincos(turn.astype(jnp.float32) * (math.pi / 4.0))
-    sine = jnp.concatenate([sine] * 2, axis=0)
-    cosine = jnp.concatenate([cosine] * 2, axis=0)
+    pair = lax.axis_index("gx") % 8
+    turn = (pair * iota((16, 128), 0) + 8) % 16 - 8
+    sine, cosine = sincos(turn.astype(jnp.float32) * (math.pi / 8.0))
     block = iota((16, 128), 1) // 32
 
     def unpack(source, carry):
@@ -427,7 +426,7 @@
 
 def x_tables():
     row = np.arange(256)
-    k = row // 8 * 4 + row % 4
+    k = row // 128 * 512 + row // 8 % 16 * 4 + row % 4
     phase = 2.0 * np.pi * (np.outer(k, np.arange(1024)) % 1024) / 1024.0
     real = (row % 8 < 4)[:, None]
     return pieces(np.where(real, np.cos(phase), -np.sin(phase)))
@@ -486,11 +485,11 @@
     from_high = jnp.where(even_y, got_first, got_second)
     from_low = jnp.where(even_y, got_second, got_first)
 
-    cells, props, ends = pl.pallas_call(
+    cells, props, ends, tables = pl.pallas_call(
         cells_kernel,
-        out_shape=(f32(3, WX, COLS), f32(4, WX, COLS), f32(2, 3, 4, COLS)),
+        out_shape=(f32(3, WX, COLS), f32(4, WX, COLS), f32(2, 3, 4, COLS), f32(8, NGRAIN)),
         in_specs=vmem(4),
-        out_specs=tuple(vmem(3)),
+        out_specs=tuple(vmem(4)),
         compiler_params=params,
         name="cells",
     )(*fields, tables)
@@ -553,7 +552,7 @@
         name="along_x",
     )(columns, *tables_x)
     groups = [
-        [gx * 16 + gy for gx in (base, base + 1) for gy in range(16)] for base in range(0, 16, 2)
+        [gx * 16 + gy for gx in (base, base + 8) for gy in range(16)] for base in range(8)
     ]
     mine = lax.all_to_all(
         rows.reshape(32, 8, 128), ("gx", "gy"), split_axis=0, concat_axis=0, tiled=True,

time: 62.7 us -> 60.3 us (0.962)
  blocking collectives: 31.5 us -> 29.2 us
  local copies, waits for them, and re-layouts: 4.38 us -> 3.69 us
    all_to_all x1, blocking collectives: 16.5 us -> 14.7 us  [shards(): lax.all_to_all(rows.reshape(32, 8, 128), ('gx', 'gy'), split_axis=0, conc...]
    unnamed x26 -> x24, local copies, waits for them, and re-layouts: 4.22 us -> 3.52 us
  transfers between devices with their start and end apart: 4 -> 4, of which waited for: 0 -> 1; matrix products, arithmetic and copies ran while one was open for 0% -> 0% of each run, Pallas kernels for 6% -> 6%
where the time goes in v6:
time: 60.3 us; the launch traced here: 60 us
  blocking collectives  29.2 us (48%)
  Pallas kernels  13.5 us (22%)
  starting transfers between devices  12.1 us (20%)
  local copies, waits for them, and re-layouts  3.69 us (6%)
  between operations  0.83 us (1%)
    all_to_all x1, blocking collectives, shards(): lax.all_to_all(rows.reshape(32, 8, 128), ('gx', 'gy'), split_axis=0, conc...  14.7 us
    all_to_all x1, blocking collectives, shards(): lax.all_to_all(payload.reshape(16, 48, 128), 'gx', split_axis=0, concat_a...  14.5 us
    pallas_call x1, Pallas kernels, shards(): pl.pallas_call(steps_kernel, out_shape=(f32(3, WX, COLS), f32(16 * 48, 12...  5.72 us
    ppermute x1, starting transfers between devices, shards(): lax.ppermute(jnp.where(even_x, low_edge, high_edge), 'gx', odd_pairs)  5.69 us
    ppermute x1, starting transfers between devices, shards(): got_second = lax.ppermute(to_second, 'gy', odd_pairs)  4.13 us
    unnamed x24, local copies, waits for them, and re-layouts  3.52 us
    ppermute x1, starting transfers between devices, shards(): got_first = lax.ppermute(to_first, 'gy', even_pairs)  2.28 us
    pallas_call x1, Pallas kernels, shards(): pl.pallas_call(inner_kernel, out_shape=(f32(3, WX, LANES), f32(3, WX, LAN...  2.27 us
  transfers between devices with their start and end apart: 4, of which 1 were waited for; matrix products, arithmetic and copies ran while one was open for 0% of the time, Pallas kernels for 6%

profile of v6, /device:TPU:1, one launch (start us, length us, event | category | flops | bytes accessed | tf_op | source)
XLA Modules:
  0.0 60.0 jit_solution(10793054037448349131)
XLA Ops:
  0.6 0.0 copy-start
  0.6 0.0 copy-start.1
  0.7 0.0 copy-start.6
  0.7 0.0 copy-start.7
  0.7 0.0 copy-start.9
  0.7 1.7 %edges.1 = (f32[96,128]{1,0:T(8,128)}, f32[96,128]{1,0:T(8,128)}, f32[8,256]{1,0:T(8,128)}) custom-call(f32[64,768]{1,0:T(8,128)} %polar.1, f32[64,768]{1,0:T(8,128)} %azimuth.1, s32[64,768]{1,0:T(8,128)} %grains.1, f32[64,768]{1,0:T(8,128)} %polar.1, f32[64,768]{1,0:T(8,128)} %azimuth.1, s32[64,768]{1,0:T(8,128)} %grains.1, f32[1,256]{1,0:T(1,128)} %bitcast.36, ...), custom_call_target="tpu_custom_call" | custom-call | tf_op jit(solution)/shard_map/edges/pallas_call | solution.py:475
  2.4 4.1 %collective-permute-start.1 = (f32[96,128]{1,0:T(8,128)}, f32[96,128]{1,0:T(8,128)S(1)}, u32[]{:S(2)}, u32[]{:S(2)}) collective-permute-start(f32[96,128]{1,0:T(8,128)} %get-tuple-element.21), channel_id=1, source_target_pairs={{0,15},{1,2},{2,1},{3,4},{4,3},{5,6},{6,5},{7,8},{8,7},{9,10},{10,... | collective-permute-start | bytes 147464 | tf_op jit(solution)/shard_map/ppermute | solution.py:483
  6.5 2.3 %collective-permute-start = (f32[96,128]{1,0:T(8,128)}, f32[96,128]{1,0:T(8,128)S(1)}, u32[]{:S(2)}, u32[]{:S(2)}) collective-permute-start(f32[96,128]{1,0:T(8,128)} %get-tuple-element.20), channel_id=1, source_target_pairs={{0,1},{1,0},{2,3},{3,2},{4,5},{5,4},{6,7},{7,6},{8,9},{9,8},{10,11... | collective-permute-start | bytes 147464 | tf_op jit(solution)/shard_map/ppermute | solution.py:484
  8.8 0.0 copy-start.2
  8.8 0.9 %copy-done.2 = f32[64,768]{1,0:T(8,128)S(1)} copy-done((f32[64,768]{1,0:T(8,128)S(1)}, f32[64,768]{1,0:T(8,128)}, u32[]{:S(2)}) %copy-start.2) | copy-done | bytes 196632
  9.7 0.0 copy-start.3
  9.7 0.9 %copy-done.3 = f32[64,768]{1,0:T(8,128)S(1)} copy-done((f32[64,768]{1,0:T(8,128)S(1)}, f32[64,768]{1,0:T(8,128)}, u32[]{:S(2)}) %copy-start.3) | copy-done | bytes 196632
  10.7 0.0 copy-start.4
  10.7 0.9 %copy-done.4 = s32[64,768]{1,0:T(8,128)S(1)} copy-done((s32[64,768]{1,0:T(8,128)S(1)}, s32[64,768]{1,0:T(8,128)}, u32[]{:S(2)}) %copy-start.4) | copy-done | bytes 196632
  11.6 0.0 copy-start.11
  11.6 0.7 %copy-done.11 = f32[8,256]{1,0:T(8,128)S(1)} copy-done((f32[8,256]{1,0:T(8,128)S(1)}, f32[8,256]{1,0:T(8,128)}, u32[]{:S(2)}) %copy-start.11) | copy-done | bytes 8216
  12.3 0.0 copy-start.5
  12.3 0.0 copy-start.8
  12.3 0.0 copy-start.10
  12.3 1.5 %cells.1 = (f32[3,64,768]{2,1,0:T(8,128)S(1)}, f32[4,64,768]{2,1,0:T(8,128)S(1)}, f32[2,3,4,768]{3,2,1,0:T(4,128)S(1)}, f32[8,256]{1,0:T(8,128)S(1)}) custom-call(f32[64,768]{1,0:T(8,128)S(1)} %copy-done.2, f32[64,768]{1,0:T(8,128)S(1)} %copy-done.3, s32[64,768]{1,0:T(8,128)S(1)} %copy-done.4, f32[8,256]{1,0:T(8,128)S(1)} %copy-done.11), custom_call_target="tpu_custom_call" | custom-call | tf_op jit(solution)/shard_map/cells/pallas_call | solution.py:488
  13.9 0.1 pad.28.clone
  13.9 0.0 collective-permute-done.1
  13.9 0.0 collective-permute-done
  14.0 0.1 fusion
  14.0 0.1 maximum_bitcast_fusion
  14.2 5.7 %collective-permute-start.3 = (f32[3,4,896]{2,1,0:T(4,128)S(1)}, f32[3,4,896]{2,1,0:T(4,128)S(1)}, u32[]{:S(2)}, u32[]{:S(2)}) collective-permute-start(f32[3,4,896]{2,1,0:T(4,128)S(1)} %get-tuple-element.35), channel_id=1, source_target_pairs={{0,240},{16,32},{32,16},{48,64},{64,48},{80,96},{96,80},{112,128},... | collective-permute-start | bytes 129032 | tf_op jit(solution)/shard_map/ppermute | solution.py:517
  19.8 0.0 collective-permute-start.2
  19.9 2.3 %inner.1 = (f32[3,64,896]{2,1,0:T(8,128)S(1)}, f32[3,64,896]{2,1,0:T(8,128)S(1)}, f32[11,64,896]{2,1,0:T(8,128)S(1)}) custom-call(f32[3,64,768]{2,1,0:T(8,128)S(1)} %get-tuple-element.18.cells, f32[4,64,768]{2,1,0:T(8,128)S(1)} %get-tuple-element.19.props, f32[96,128]{1,0:T(8,128)S(1)} %get-tuple-element.32.from_high, ...), custom_call_target="tpu_custom_call" | custom-call | tf_op jit(solution)/shard_map/inner/pallas_call | solution.py:521
  22.1 0.0 collective-permute-done.3
  22.1 0.6 collective-permute-done.2
  22.7 0.0 copy-done
  22.8 0.0 copy-done.1
  22.8 0.0 copy-done.6
  22.8 0.0 copy-done.7
  22.8 0.0 copy-done.9
  22.8 0.0 copy-done.5
  22.8 0.0 copy-done.8
  22.8 0.0 copy-done.10
  22.8 5.7 %steps.1 = (f32[3,64,768]{2,1,0:T(8,128)}, f32[768,128]{1,0:T(8,128)S(1)}) custom-call(f32[3,64,896]{2,1,0:T(8,128)S(1)} %get-tuple-element.23.first0, f32[3,64,896]{2,1,0:T(8,128)S(1)} %get-tuple-element.24.first1, f32[11,64,896]{2,1,0:T(8,128)S(1)} %get-tuple-element.25.coefs, f32[3,4,896]{2,1,0:T(4,128)S(1)} %get-tuple-element.34.halo_xh, ...), custom_call_target="tpu_custom_call" | custom-call | tf_op jit(solution)/shard_map/steps/pallas_call | solution.py:530
  28.5 14.5 %all_to_all.10 = f32[16,48,128]{2,1,0:T(8,128)S(1)} all-to-all(f32[16,48,128]{2,1,0:T(8,128)S(1)} %bitcast.35), channel_id=1, replica_groups=mesh['gx'=16,'gy'=16] {'gx'}, dimensions={0} | all-to-all | bytes 786432 | tf_op jit(solution)/shard_map/all_to_all | solution.py:542
  43.1 1.1 %along_x.1 = f32[256,128]{1,0:T(8,128)S(1)} custom-call(f32[768,128]{1,0:T(8,128)S(1)} %bitcast.32, bf16[256,1024]{1,0:T(8,128)(2,1)S(1)} %copy-done, bf16[256,1024]{1,0:T(8,128)(2,1)S(1)} %copy-done.1), custom_call_target="tpu_custom_call" | custom-call | tf_op jit(solution)/shard_map/along_x/pallas_call | solution.py:545
  44.1 14.7 %all_to_all.11 = f32[32,8,128]{2,1,0:T(8,128)S(1)} all-to-all(f32[32,8,128]{2,1,0:T(8,128)S(1)} %bitcast.33), channel_id=1, replica_groups={{0,1,2,3,4,5,6,7,8,9,10,11,12,13,14,15,128,129,130,131,132,133,134,135,..., dimensions={0} | all-to-all | bytes 262144 | tf_op jit(solution)/shard_map/all_to_all | solution.py:557
  58.9 1.2 %along_y.1 = (f32[4,1024]{1,0:T(4,128)}, f32[4,1024]{1,0:T(4,128)}) custom-call(f32[256,128]{1,0:T(8,128)S(1)} %bitcast.34, bf16[128,256]{1,0:T(8,128)(2,1)S(1)} %copy-done.6, bf16[128,256]{1,0:T(8,128)(2,1)S(1)} %copy-done.7, f32[64,128]{1,0:T(8,128)S(1)} %copy-done.8, bf16[64,64]{1,0:T(8,128)(2,1)S(1)} %copy-done.9, bf16[64,64]{1,0:T(8,128)(2,1)S(1)} %copy-done.10), custom_call_target="tpu_custom_call" | custom-call | tf_op jit(solution)/shard_map/along_y/pallas_call | solution.py:561
  (5 shorter events, 0.1 us)
Async XLA Ops:
  0.6 22.1 %copy-start = (bf16[256,1024]{1,0:T(8,128)(2,1)S(1)}, bf16[256,1024]{1,0:T(8,128)(2,1)}, u32[]{:S(2)}) copy-start(bf16[256,1024]{1,0:T(8,128)(2,1)} %constant.43.clone.rest_0_.waves_hi) | copy-start | bytes 1572868
  0.6 22.1 %copy-start.1 = (bf16[256,1024]{1,0:T(8,128)(2,1)S(1)}, bf16[256,1024]{1,0:T(8,128)(2,1)}, u32[]{:S(2)}) copy-start(bf16[256,1024]{1,0:T(8,128)(2,1)} %constant.44.clone.rest_1_.waves_lo) | copy-start | bytes 1572868
  0.7 22.1 %copy-start.6 = (bf16[128,256]{1,0:T(8,128)(2,1)S(1)}, bf16[128,256]{1,0:T(8,128)(2,1)}, u32[]{:S(2)}) copy-start(bf16[128,256]{1,0:T(8,128)(2,1)} %constant.45.clone.rest_2_.waves_hi) | copy-start | bytes 196612
  0.7 22.1 %copy-start.7 = (bf16[128,256]{1,0:T(8,128)(2,1)S(1)}, bf16[128,256]{1,0:T(8,128)(2,1)}, u32[]{:S(2)}) copy-start(bf16[128,256]{1,0:T(8,128)(2,1)} %constant.46.clone.rest_3_.waves_lo) | copy-start | bytes 196612
  0.7 22.1 %copy-start.9 = (bf16[64,64]{1,0:T(8,128)(2,1)S(1)}, bf16[64,64]{1,0:T(8,128)(2,1)}, u32[]{:S(2)}) copy-start(bf16[64,64]{1,0:T(8,128)(2,1)} %constant.48.clone.rest_5_.last_hi) | copy-start | bytes 24580
  2.4 11.6 %collective-permute-start.1 = (f32[96,128]{1,0:T(8,128)}, f32[96,128]{1,0:T(8,128)S(1)}, u32[]{:S(2)}, u32[]{:S(2)}) collective-permute-start(f32[96,128]{1,0:T(8,128)} %get-tuple-element.21), channel_id=1, source_target_pairs={{0,15},{1,2},{2,1},{3,4},{4,3},{5,6},{6,5},{7,8},{8,7},{9,10},{10,... | collective-permute-start | bytes 147464 | tf_op jit(solution)/shard_map/ppermute | solution.py:483
  6.5 7.4 %collective-permute-start = (f32[96,128]{1,0:T(8,128)}, f32[96,128]{1,0:T(8,128)S(1)}, u32[]{:S(2)}, u32[]{:S(2)}) collective-permute-start(f32[96,128]{1,0:T(8,128)} %get-tuple-element.20), channel_id=1, source_target_pairs={{0,1},{1,0},{2,3},{3,2},{4,5},{5,4},{6,7},{7,6},{8,9},{9,8},{10,11... | collective-permute-start | bytes 147464 | tf_op jit(solution)/shard_map/ppermute | solution.py:484
  8.8 0.9 %copy-start.2 = (f32[64,768]{1,0:T(8,128)S(1)}, f32[64,768]{1,0:T(8,128)}, u32[]{:S(2)}) copy-start(f32[64,768]{1,0:T(8,128)} %polar.1) | copy-start | bytes 589828
  9.7 0.9 %copy-start.3 = (f32[64,768]{1,0:T(8,128)S(1)}, f32[64,768]{1,0:T(8,128)}, u32[]{:S(2)}) copy-start(f32[64,768]{1,0:T(8,128)} %azimuth.1) | copy-start | bytes 589828
  10.7 0.9 %copy-start.4 = (s32[64,768]{1,0:T(8,128)S(1)}, s32[64,768]{1,0:T(8,128)}, u32[]{:S(2)}) copy-start(s32[64,768]{1,0:T(8,128)} %grains.1) | copy-start | bytes 589828
  11.6 0.7 %copy-start.11 = (f32[8,256]{1,0:T(8,128)S(1)}, f32[8,256]{1,0:T(8,128)}, u32[]{:S(2)}) copy-start(f32[8,256]{1,0:T(8,128)} %get-tuple-element.17.tables) | copy-start | bytes 24580
  12.3 10.5 %copy-start.5 = (bf16[768,256]{1,0:T(8,128)(2,1)S(1)}, bf16[768,256]{1,0:T(8,128)(2,1)}, u32[]{:S(2)}) copy-start(bf16[768,256]{1,0:T(8,128)(2,1)} %constant.50.clone.sum_z) | copy-start | bytes 1179652
  12.3 10.5 %copy-start.8 = (f32[64,128]{1,0:T(8,128)S(1)}, f32[64,128]{1,0:T(8,128)}, u32[]{:S(2)}) copy-start(f32[64,128]{1,0:T(8,128)} %constant.47.clone.rest_4_.twiddle) | copy-start | bytes 98308
  12.3 10.5 %copy-start.10 = (bf16[64,64]{1,0:T(8,128)(2,1)S(1)}, bf16[64,64]{1,0:T(8,128)(2,1)}, u32[]{:S(2)}) copy-start(bf16[64,64]{1,0:T(8,128)(2,1)} %constant.49.clone.rest_6_.last_lo) | copy-start | bytes 24580
  14.2 8.0 %collective-permute-start.3 = (f32[3,4,896]{2,1,0:T(4,128)S(1)}, f32[3,4,896]{2,1,0:T(4,128)S(1)}, u32[]{:S(2)}, u32[]{:S(2)}) collective-permute-start(f32[3,4,896]{2,1,0:T(4,128)S(1)} %get-tuple-element.35), channel_id=1, source_target_pairs={{0,240},{16,32},{32,16},{48,64},{64,48},{80,96},{96,80},{112,128},... | collective-permute-start | bytes 129032 | tf_op jit(solution)/shard_map/ppermute | solution.py:517
  19.8 2.9 %collective-permute-start.2 = (f32[3,4,896]{2,1,0:T(4,128)S(1)}, f32[3,4,896]{2,1,0:T(4,128)S(1)}, u32[]{:S(2)}, u32[]{:S(2)}) collective-permute-start(f32[3,4,896]{2,1,0:T(4,128)S(1)} %get-tuple-element.36), channel_id=1, source_target_pairs={{0,16},{16,0},{32,48},{48,32},{64,80},{80,64},{96,112},{112,96},{1... | collective-permute-start | bytes 129032 | tf_op jit(solution)/shard_map/ppermute | solution.py:518

commit v7 on v6

--- a/solution.py
+++ b/solution.py
@@ -210,7 +210,7 @@
         body(s)
         return carry
 
-    lax.fori_loop(1, LAST, one, 0, unroll=3)
+    lax.fori_loop(1, LAST, one, 0, unroll=6)
 
 
 def inner_kernel(cells, props, from_high, from_low, tables, m0, m1, coefs):

time: 60.3 us -> 59.3 us (0.983)
  Pallas kernels: 13.5 us -> 12.3 us
    pallas_call x1, Pallas kernels: 5.72 us -> 4.7 us  [shards(): pl.pallas_call(steps_kernel, out_shape=(f32(3, WX, COLS), f32(16 * 48, 12...]
where the time goes in v7:
time: 59.3 us; the launch traced here: 59 us
  blocking collectives  29.2 us (49%)
  Pallas kernels  12.3 us (21%)
  starting transfers between devices  12.1 us (20%)
  local copies, waits for them, and re-layouts  3.69 us (6%)
  between operations  0.83 us (1%)
  waiting for transfers between devices  0.75 us (1%)
    all_to_all x1, blocking collectives, shards(): lax.all_to_all(rows.reshape(32, 8, 128), ('gx', 'gy'), split_axis=0, conc...  14.7 us
    all_to_all x1, blocking collectives, shards(): lax.all_to_all(payload.reshape(16, 48, 128), 'gx', split_axis=0, concat_a...  14.5 us
    ppermute x1, starting transfers between devices, shards(): lax.ppermute(jnp.where(even_x, low_edge, high_edge), 'gx', odd_pairs)  5.69 us
    pallas_call x1, Pallas kernels, shards(): pl.pallas_call(steps_kernel, out_shape=(f32(3, WX, COLS), f32(16 * 48, 12...  4.7 us
    ppermute x1, starting transfers between devices, shards(): got_second = lax.ppermute(to_second, 'gy', odd_pairs)  4.13 us
    unnamed x24, local copies, waits for them, and re-layouts  3.52 us
    ppermute x1, starting transfers between devices, shards(): got_first = lax.ppermute(to_first, 'gy', even_pairs)  2.28 us
    pallas_call x1, Pallas kernels, shards(): pl.pallas_call(inner_kernel, out_shape=(f32(3, WX, LANES), f32(3, WX, LAN...  2.11 us
  transfers between devices with their start and end apart: 4, of which 1 were waited for; matrix products, arithmetic and copies ran while one was open for 0% of the time, Pallas kernels for 6%

profile of v7, /device:TPU:1, one launch (start us, length us, event | category | flops | bytes accessed | tf_op | source)
XLA Modules:
  0.0 59.0 jit_solution(9670503024481880136)
XLA Ops:
  0.6 0.0 copy-start
  0.6 0.0 copy-start.1
  0.7 0.0 copy-start.6
  0.7 0.0 copy-start.7
  0.7 0.0 copy-start.9
  0.7 1.7 %edges.1 = (f32[96,128]{1,0:T(8,128)}, f32[96,128]{1,0:T(8,128)}, f32[8,256]{1,0:T(8,128)}) custom-call(f32[64,768]{1,0:T(8,128)} %polar.1, f32[64,768]{1,0:T(8,128)} %azimuth.1, s32[64,768]{1,0:T(8,128)} %grains.1, f32[64,768]{1,0:T(8,128)} %polar.1, f32[64,768]{1,0:T(8,128)} %azimuth.1, s32[64,768]{1,0:T(8,128)} %grains.1, f32[1,256]{1,0:T(1,128)} %bitcast.36, ...), custom_call_target="tpu_custom_call" | custom-call | tf_op jit(solution)/shard_map/edges/pallas_call | solution.py:475
  2.4 4.1 %collective-permute-start.1 = (f32[96,128]{1,0:T(8,128)}, f32[96,128]{1,0:T(8,128)S(1)}, u32[]{:S(2)}, u32[]{:S(2)}) collective-permute-start(f32[96,128]{1,0:T(8,128)} %get-tuple-element.21), channel_id=1, source_target_pairs={{0,15},{1,2},{2,1},{3,4},{4,3},{5,6},{6,5},{7,8},{8,7},{9,10},{10,... | collective-permute-start | bytes 147464 | tf_op jit(solution)/shard_map/ppermute | solution.py:483
  6.5 2.3 %collective-permute-start = (f32[96,128]{1,0:T(8,128)}, f32[96,128]{1,0:T(8,128)S(1)}, u32[]{:S(2)}, u32[]{:S(2)}) collective-permute-start(f32[96,128]{1,0:T(8,128)} %get-tuple-element.20), channel_id=1, source_target_pairs={{0,1},{1,0},{2,3},{3,2},{4,5},{5,4},{6,7},{7,6},{8,9},{9,8},{10,11... | collective-permute-start | bytes 147464 | tf_op jit(solution)/shard_map/ppermute | solution.py:484
  8.8 0.0 copy-start.2
  8.8 0.9 %copy-done.2 = f32[64,768]{1,0:T(8,128)S(1)} copy-done((f32[64,768]{1,0:T(8,128)S(1)}, f32[64,768]{1,0:T(8,128)}, u32[]{:S(2)}) %copy-start.2) | copy-done | bytes 196632
  9.7 0.0 copy-start.3
  9.7 0.9 %copy-done.3 = f32[64,768]{1,0:T(8,128)S(1)} copy-done((f32[64,768]{1,0:T(8,128)S(1)}, f32[64,768]{1,0:T(8,128)}, u32[]{:S(2)}) %copy-start.3) | copy-done | bytes 196632
  10.7 0.0 copy-start.4
  10.7 0.9 %copy-done.4 = s32[64,768]{1,0:T(8,128)S(1)} copy-done((s32[64,768]{1,0:T(8,128)S(1)}, s32[64,768]{1,0:T(8,128)}, u32[]{:S(2)}) %copy-start.4) | copy-done | bytes 196632
  11.6 0.0 copy-start.11
  11.6 0.7 %copy-done.11 = f32[8,256]{1,0:T(8,128)S(1)} copy-done((f32[8,256]{1,0:T(8,128)S(1)}, f32[8,256]{1,0:T(8,128)}, u32[]{:S(2)}) %copy-start.11) | copy-done | bytes 8216
  12.3 0.0 copy-start.5
  12.3 0.0 copy-start.8
  12.3 0.0 copy-start.10
  12.3 1.5 %cells.1 = (f32[3,64,768]{2,1,0:T(8,128)S(1)}, f32[4,64,768]{2,1,0:T(8,128)S(1)}, f32[2,3,4,768]{3,2,1,0:T(4,128)S(1)}, f32[8,256]{1,0:T(8,128)S(1)}) custom-call(f32[64,768]{1,0:T(8,128)S(1)} %copy-done.2, f32[64,768]{1,0:T(8,128)S(1)} %copy-done.3, s32[64,768]{1,0:T(8,128)S(1)} %copy-done.4, f32[8,256]{1,0:T(8,128)S(1)} %copy-done.11), custom_call_target="tpu_custom_call" | custom-call | tf_op jit(solution)/shard_map/cells/pallas_call | solution.py:488
  13.9 0.1 pad.28.clone
  13.9 0.0 collective-permute-done.1
  13.9 0.0 collective-permute-done
  14.0 0.1 fusion
  14.0 0.1 maximum_bitcast_fusion
  14.2 5.7 %collective-permute-start.3 = (f32[3,4,896]{2,1,0:T(4,128)S(1)}, f32[3,4,896]{2,1,0:T(4,128)S(1)}, u32[]{:S(2)}, u32[]{:S(2)}) collective-permute-start(f32[3,4,896]{2,1,0:T(4,128)S(1)} %get-tuple-element.35), channel_id=1, source_target_pairs={{0,240},{16,32},{32,16},{48,64},{64,48},{80,96},{96,80},{112,128},... | collective-permute-start | bytes 129032 | tf_op jit(solution)/shard_map/ppermute | solution.py:517
  19.8 0.0 collective-permute-start.2
  19.9 2.1 %inner.1 = (f32[3,64,896]{2,1,0:T(8,128)S(1)}, f32[3,64,896]{2,1,0:T(8,128)S(1)}, f32[11,64,896]{2,1,0:T(8,128)S(1)}) custom-call(f32[3,64,768]{2,1,0:T(8,128)S(1)} %get-tuple-element.18.cells, f32[4,64,768]{2,1,0:T(8,128)S(1)} %get-tuple-element.19.props, f32[96,128]{1,0:T(8,128)S(1)} %get-tuple-element.32.from_high, ...), custom_call_target="tpu_custom_call" | custom-call | tf_op jit(solution)/shard_map/inner/pallas_call | solution.py:521
  22.0 0.0 collective-permute-done.3
  22.0 0.7 %collective-permute-done.2 = f32[3,4,896]{2,1,0:T(4,128)S(1)} collective-permute-done((f32[3,4,896]{2,1,0:T(4,128)S(1)}, f32[3,4,896]{2,1,0:T(4,128)S(1)}, u32[]{:S(2)}, u32[]{:S(2)}) %collective-permute-start.2) | collective-permute-done | bytes 43040 | tf_op jit(solution)/shard_map/ppermute | solution.py:518
  22.7 0.0 copy-done
  22.8 0.0 copy-done.1
  22.8 0.0 copy-done.6
  22.8 0.0 copy-done.7
  22.8 0.0 copy-done.9
  22.8 0.0 copy-done.5
  22.8 0.0 copy-done.8
  22.8 0.0 copy-done.10
  22.8 4.7 %steps.1 = (f32[3,64,768]{2,1,0:T(8,128)}, f32[768,128]{1,0:T(8,128)S(1)}) custom-call(f32[3,64,896]{2,1,0:T(8,128)S(1)} %get-tuple-element.23.first0, f32[3,64,896]{2,1,0:T(8,128)S(1)} %get-tuple-element.24.first1, f32[11,64,896]{2,1,0:T(8,128)S(1)} %get-tuple-element.25.coefs, f32[3,4,896]{2,1,0:T(4,128)S(1)} %get-tuple-element.34.halo_xh, ...), custom_call_target="tpu_custom_call" | custom-call | tf_op jit(solution)/shard_map/steps/pallas_call | solution.py:530
  27.5 14.5 %all_to_all.10 = f32[16,48,128]{2,1,0:T(8,128)S(1)} all-to-all(f32[16,48,128]{2,1,0:T(8,128)S(1)} %bitcast.35), channel_id=1, replica_groups=mesh['gx'=16,'gy'=16] {'gx'}, dimensions={0} | all-to-all | bytes 786432 | tf_op jit(solution)/shard_map/all_to_all | solution.py:542
  42.0 1.1 %along_x.1 = f32[256,128]{1,0:T(8,128)S(1)} custom-call(f32[768,128]{1,0:T(8,128)S(1)} %bitcast.32, bf16[256,1024]{1,0:T(8,128)(2,1)S(1)} %copy-done, bf16[256,1024]{1,0:T(8,128)(2,1)S(1)} %copy-done.1), custom_call_target="tpu_custom_call" | custom-call | tf_op jit(solution)/shard_map/along_x/pallas_call | solution.py:545
  43.1 14.7 %all_to_all.11 = f32[32,8,128]{2,1,0:T(8,128)S(1)} all-to-all(f32[32,8,128]{2,1,0:T(8,128)S(1)} %bitcast.33), channel_id=1, replica_groups={{0,1,2,3,4,5,6,7,8,9,10,11,12,13,14,15,128,129,130,131,132,133,134,135,..., dimensions={0} | all-to-all | bytes 262144 | tf_op jit(solution)/shard_map/all_to_all | solution.py:557
  57.9 1.2 %along_y.1 = (f32[4,1024]{1,0:T(4,128)}, f32[4,1024]{1,0:T(4,128)}) custom-call(f32[256,128]{1,0:T(8,128)S(1)} %bitcast.34, bf16[128,256]{1,0:T(8,128)(2,1)S(1)} %copy-done.6, bf16[128,256]{1,0:T(8,128)(2,1)S(1)} %copy-done.7, f32[64,128]{1,0:T(8,128)S(1)} %copy-done.8, bf16[64,64]{1,0:T(8,128)(2,1)S(1)} %copy-done.9, bf16[64,64]{1,0:T(8,128)(2,1)S(1)} %copy-done.10), custom_call_target="tpu_custom_call" | custom-call | tf_op jit(solution)/shard_map/along_y/pallas_call | solution.py:561
  (5 shorter events, 0.1 us)
Async XLA Ops:
  0.6 22.1 %copy-start = (bf16[256,1024]{1,0:T(8,128)(2,1)S(1)}, bf16[256,1024]{1,0:T(8,128)(2,1)}, u32[]{:S(2)}) copy-start(bf16[256,1024]{1,0:T(8,128)(2,1)} %constant.43.clone.rest_0_.waves_hi) | copy-start | bytes 1572868
  0.6 22.1 %copy-start.1 = (bf16[256,1024]{1,0:T(8,128)(2,1)S(1)}, bf16[256,1024]{1,0:T(8,128)(2,1)}, u32[]{:S(2)}) copy-start(bf16[256,1024]{1,0:T(8,128)(2,1)} %constant.44.clone.rest_1_.waves_lo) | copy-start | bytes 1572868
  0.7 22.1 %copy-start.6 = (bf16[128,256]{1,0:T(8,128)(2,1)S(1)}, bf16[128,256]{1,0:T(8,128)(2,1)}, u32[]{:S(2)}) copy-start(bf16[128,256]{1,0:T(8,128)(2,1)} %constant.45.clone.rest_2_.waves_hi) | copy-start | bytes 196612
  0.7 22.1 %copy-start.7 = (bf16[128,256]{1,0:T(8,128)(2,1)S(1)}, bf16[128,256]{1,0:T(8,128)(2,1)}, u32[]{:S(2)}) copy-start(bf16[128,256]{1,0:T(8,128)(2,1)} %constant.46.clone.rest_3_.waves_lo) | copy-start | bytes 196612
  0.7 22.1 %copy-start.9 = (bf16[64,64]{1,0:T(8,128)(2,1)S(1)}, bf16[64,64]{1,0:T(8,128)(2,1)}, u32[]{:S(2)}) copy-start(bf16[64,64]{1,0:T(8,128)(2,1)} %constant.48.clone.rest_5_.last_hi) | copy-start | bytes 24580
  2.4 11.6 %collective-permute-start.1 = (f32[96,128]{1,0:T(8,128)}, f32[96,128]{1,0:T(8,128)S(1)}, u32[]{:S(2)}, u32[]{:S(2)}) collective-permute-start(f32[96,128]{1,0:T(8,128)} %get-tuple-element.21), channel_id=1, source_target_pairs={{0,15},{1,2},{2,1},{3,4},{4,3},{5,6},{6,5},{7,8},{8,7},{9,10},{10,... | collective-permute-start | bytes 147464 | tf_op jit(solution)/shard_map/ppermute | solution.py:483
  6.5 7.4 %collective-permute-start = (f32[96,128]{1,0:T(8,128)}, f32[96,128]{1,0:T(8,128)S(1)}, u32[]{:S(2)}, u32[]{:S(2)}) collective-permute-start(f32[96,128]{1,0:T(8,128)} %get-tuple-element.20), channel_id=1, source_target_pairs={{0,1},{1,0},{2,3},{3,2},{4,5},{5,4},{6,7},{7,6},{8,9},{9,8},{10,11... | collective-permute-start | bytes 147464 | tf_op jit(solution)/shard_map/ppermute | solution.py:484
  8.8 0.9 %copy-start.2 = (f32[64,768]{1,0:T(8,128)S(1)}, f32[64,768]{1,0:T(8,128)}, u32[]{:S(2)}) copy-start(f32[64,768]{1,0:T(8,128)} %polar.1) | copy-start | bytes 589828
  9.7 0.9 %copy-start.3 = (f32[64,768]{1,0:T(8,128)S(1)}, f32[64,768]{1,0:T(8,128)}, u32[]{:S(2)}) copy-start(f32[64,768]{1,0:T(8,128)} %azimuth.1) | copy-start | bytes 589828
  10.7 0.9 %copy-start.4 = (s32[64,768]{1,0:T(8,128)S(1)}, s32[64,768]{1,0:T(8,128)}, u32[]{:S(2)}) copy-start(s32[64,768]{1,0:T(8,128)} %grains.1) | copy-start | bytes 589828
  11.6 0.7 %copy-start.11 = (f32[8,256]{1,0:T(8,128)S(1)}, f32[8,256]{1,0:T(8,128)}, u32[]{:S(2)}) copy-start(f32[8,256]{1,0:T(8,128)} %get-tuple-element.17.tables) | copy-start | bytes 24580
  12.3 10.5 %copy-start.5 = (bf16[768,256]{1,0:T(8,128)(2,1)S(1)}, bf16[768,256]{1,0:T(8,128)(2,1)}, u32[]{:S(2)}) copy-start(bf16[768,256]{1,0:T(8,128)(2,1)} %constant.50.clone.sum_z) | copy-start | bytes 1179652
  12.3 10.5 %copy-start.8 = (f32[64,128]{1,0:T(8,128)S(1)}, f32[64,128]{1,0:T(8,128)}, u32[]{:S(2)}) copy-start(f32[64,128]{1,0:T(8,128)} %constant.47.clone.rest_4_.twiddle) | copy-start | bytes 98308
  12.3 10.5 %copy-start.10 = (bf16[64,64]{1,0:T(8,128)(2,1)S(1)}, bf16[64,64]{1,0:T(8,128)(2,1)}, u32[]{:S(2)}) copy-start(bf16[64,64]{1,0:T(8,128)(2,1)} %constant.49.clone.rest_6_.last_lo) | copy-start | bytes 24580
  14.2 7.8 %collective-permute-start.3 = (f32[3,4,896]{2,1,0:T(4,128)S(1)}, f32[3,4,896]{2,1,0:T(4,128)S(1)}, u32[]{:S(2)}, u32[]{:S(2)}) collective-permute-start(f32[3,4,896]{2,1,0:T(4,128)S(1)} %get-tuple-element.35), channel_id=1, source_target_pairs={{0,240},{16,32},{32,16},{48,64},{64,48},{80,96},{96,80},{112,128},... | collective-permute-start | bytes 129032 | tf_op jit(solution)/shard_map/ppermute | solution.py:517
  19.8 2.9 %collective-permute-start.2 = (f32[3,4,896]{2,1,0:T(4,128)S(1)}, f32[3,4,896]{2,1,0:T(4,128)S(1)}, u32[]{:S(2)}, u32[]{:S(2)}) collective-permute-start(f32[3,4,896]{2,1,0:T(4,128)S(1)} %get-tuple-element.36), channel_id=1, source_target_pairs={{0,16},{16,0},{32,48},{48,32},{64,80},{80,64},{96,112},{112,96},{1... | collective-permute-start | bytes 129032 | tf_op jit(solution)/shard_map/ppermute | solution.py:518

commit v8 on v7

--- a/solution.py
+++ b/solution.py
@@ -153,7 +153,7 @@
             put(props, s, look_up(tabs[r], labels), r)
         return carry
 
-    lax.fori_loop(0, WX // 8, body, 0, unroll=2)
+    lax.fori_loop(0, WX // 8, body, 0, unroll=4)
 
 
 def cell_rows(polar, azimuth, labels, tabs):
@@ -345,7 +345,7 @@
                 d_lo[pl.ds(start, 16), 128 * i : 128 * i + 128] = lo
         return carry
 
-    lax.fori_loop(0, 16, unpack, 0, unroll=4)
+    lax.fori_loop(0, 16, unpack, 0, unroll=8)
     both = mm(waves_hi[...], d_hi[...]) + (
         mm(waves_hi[...], d_lo[...]) + mm(waves_lo[...], d_hi[...])
     )

time: 59.3 us -> 58.9 us (level)
  no operation moved by 1% of the time
where the time goes in v8:
time: 58.9 us; the launch traced here: 58.6 us
  blocking collectives  29.3 us (50%)
  starting transfers between devices  12.1 us (21%)
  Pallas kernels  11.8 us (20%)
  local copies, waits for them, and re-layouts  3.69 us (6%)
  between operations  0.83 us (1%)
  waiting for transfers between devices  0.75 us (1%)
    all_to_all x1, blocking collectives, shards(): lax.all_to_all(rows.reshape(32, 8, 128), ('gx', 'gy'), split_axis=0, conc...  14.8 us
    all_to_all x1, blocking collectives, shards(): lax.all_to_all(payload.reshape(16, 48, 128), 'gx', split_axis=0, concat_a...  14.5 us
    ppermute x1, starting transfers between devices, shards(): lax.ppermute(jnp.where(even_x, low_edge, high_edge), 'gx', odd_pairs)  5.69 us
    pallas_call x1, Pallas kernels, shards(): pl.pallas_call(steps_kernel, out_shape=(f32(3, WX, COLS), f32(16 * 48, 12...  4.7 us
    ppermute x1, starting transfers between devices, shards(): got_second = lax.ppermute(to_second, 'gy', odd_pairs)  4.13 us
    unnamed x24, local copies, waits for them, and re-layouts  3.52 us
    ppermute x1, starting transfers between devices, shards(): got_first = lax.ppermute(to_first, 'gy', even_pairs)  2.28 us
    pallas_call x1, Pallas kernels, shards(): pl.pallas_call(inner_kernel, out_shape=(f32(3, WX, LANES), f32(3, WX, LAN...  2.11 us
  transfers between devices with their start and end apart: 4, of which 1 were waited for; matrix products, arithmetic and copies ran while one was open for 0% of the time, Pallas kernels for 6%

profile of v8, /device:TPU:1, one launch (start us, length us, event | category | flops | bytes accessed | tf_op | source)
XLA Modules:
  0.0 58.6 jit_solution(6601810626599183866)
XLA Ops:
  0.6 0.0 copy-start
  0.6 0.0 copy-start.1
  0.7 0.0 copy-start.6
  0.7 0.0 copy-start.7
  0.7 0.0 copy-start.9
  0.7 1.7 %edges.1 = (f32[96,128]{1,0:T(8,128)}, f32[96,128]{1,0:T(8,128)}, f32[8,256]{1,0:T(8,128)}) custom-call(f32[64,768]{1,0:T(8,128)} %polar.1, f32[64,768]{1,0:T(8,128)} %azimuth.1, s32[64,768]{1,0:T(8,128)} %grains.1, f32[64,768]{1,0:T(8,128)} %polar.1, f32[64,768]{1,0:T(8,128)} %azimuth.1, s32[64,768]{1,0:T(8,128)} %grains.1, f32[1,256]{1,0:T(1,128)} %bitcast.36, ...), custom_call_target="tpu_custom_call" | custom-call | tf_op jit(solution)/shard_map/edges/pallas_call | solution.py:475
  2.4 4.1 %collective-permute-start.1 = (f32[96,128]{1,0:T(8,128)}, f32[96,128]{1,0:T(8,128)S(1)}, u32[]{:S(2)}, u32[]{:S(2)}) collective-permute-start(f32[96,128]{1,0:T(8,128)} %get-tuple-element.21), channel_id=1, source_target_pairs={{0,15},{1,2},{2,1},{3,4},{4,3},{5,6},{6,5},{7,8},{8,7},{9,10},{10,... | collective-permute-start | bytes 147464 | tf_op jit(solution)/shard_map/ppermute | solution.py:483
  6.5 2.3 %collective-permute-start = (f32[96,128]{1,0:T(8,128)}, f32[96,128]{1,0:T(8,128)S(1)}, u32[]{:S(2)}, u32[]{:S(2)}) collective-permute-start(f32[96,128]{1,0:T(8,128)} %get-tuple-element.20), channel_id=1, source_target_pairs={{0,1},{1,0},{2,3},{3,2},{4,5},{5,4},{6,7},{7,6},{8,9},{9,8},{10,11... | collective-permute-start | bytes 147464 | tf_op jit(solution)/shard_map/ppermute | solution.py:484
  8.8 0.0 copy-start.2
  8.8 0.9 %copy-done.2 = f32[64,768]{1,0:T(8,128)S(1)} copy-done((f32[64,768]{1,0:T(8,128)S(1)}, f32[64,768]{1,0:T(8,128)}, u32[]{:S(2)}) %copy-start.2) | copy-done | bytes 196632
  9.7 0.0 copy-start.3
  9.7 0.9 %copy-done.3 = f32[64,768]{1,0:T(8,128)S(1)} copy-done((f32[64,768]{1,0:T(8,128)S(1)}, f32[64,768]{1,0:T(8,128)}, u32[]{:S(2)}) %copy-start.3) | copy-done | bytes 196632
  10.7 0.0 copy-start.4
  10.7 0.9 %copy-done.4 = s32[64,768]{1,0:T(8,128)S(1)} copy-done((s32[64,768]{1,0:T(8,128)S(1)}, s32[64,768]{1,0:T(8,128)}, u32[]{:S(2)}) %copy-start.4) | copy-done | bytes 196632
  11.6 0.0 copy-start.11
  11.6 0.7 %copy-done.11 = f32[8,256]{1,0:T(8,128)S(1)} copy-done((f32[8,256]{1,0:T(8,128)S(1)}, f32[8,256]{1,0:T(8,128)}, u32[]{:S(2)}) %copy-start.11) | copy-done | bytes 8216
  12.3 0.0 copy-start.5
  12.3 0.0 copy-start.8
  12.3 0.0 copy-start.10
  12.3 1.1 %cells.1 = (f32[3,64,768]{2,1,0:T(8,128)S(1)}, f32[4,64,768]{2,1,0:T(8,128)S(1)}, f32[2,3,4,768]{3,2,1,0:T(4,128)S(1)}, f32[8,256]{1,0:T(8,128)S(1)}) custom-call(f32[64,768]{1,0:T(8,128)S(1)} %copy-done.2, f32[64,768]{1,0:T(8,128)S(1)} %copy-done.3, s32[64,768]{1,0:T(8,128)S(1)} %copy-done.4, f32[8,256]{1,0:T(8,128)S(1)} %copy-done.11), custom_call_target="tpu_custom_call" | custom-call | tf_op jit(solution)/shard_map/cells/pallas_call | solution.py:488
  13.5 0.1 pad.28.clone
  13.6 0.0 collective-permute-done.1
  13.6 0.0 collective-permute-done
  13.6 0.1 fusion
  13.7 0.1 maximum_bitcast_fusion
  13.8 5.7 %collective-permute-start.3 = (f32[3,4,896]{2,1,0:T(4,128)S(1)}, f32[3,4,896]{2,1,0:T(4,128)S(1)}, u32[]{:S(2)}, u32[]{:S(2)}) collective-permute-start(f32[3,4,896]{2,1,0:T(4,128)S(1)} %get-tuple-element.35), channel_id=1, source_target_pairs={{0,240},{16,32},{32,16},{48,64},{64,48},{80,96},{96,80},{112,128},... | collective-permute-start | bytes 129032 | tf_op jit(solution)/shard_map/ppermute | solution.py:517
  19.5 0.0 collective-permute-start.2
  19.5 2.1 %inner.1 = (f32[3,64,896]{2,1,0:T(8,128)S(1)}, f32[3,64,896]{2,1,0:T(8,128)S(1)}, f32[11,64,896]{2,1,0:T(8,128)S(1)}) custom-call(f32[3,64,768]{2,1,0:T(8,128)S(1)} %get-tuple-element.18.cells, f32[4,64,768]{2,1,0:T(8,128)S(1)} %get-tuple-element.19.props, f32[96,128]{1,0:T(8,128)S(1)} %get-tuple-element.32.from_high, ...), custom_call_target="tpu_custom_call" | custom-call | tf_op jit(solution)/shard_map/inner/pallas_call | solution.py:521
  21.6 0.0 collective-permute-done.3
  21.6 0.7 %collective-permute-done.2 = f32[3,4,896]{2,1,0:T(4,128)S(1)} collective-permute-done((f32[3,4,896]{2,1,0:T(4,128)S(1)}, f32[3,4,896]{2,1,0:T(4,128)S(1)}, u32[]{:S(2)}, u32[]{:S(2)}) %collective-permute-start.2) | collective-permute-done | bytes 43040 | tf_op jit(solution)/shard_map/ppermute | solution.py:518
  22.4 0.0 copy-done
  22.4 0.0 copy-done.1
  22.4 0.0 copy-done.6
  22.4 0.0 copy-done.7
  22.4 0.0 copy-done.9
  22.4 0.0 copy-done.5
  22.4 0.0 copy-done.8
  22.4 0.0 copy-done.10
  22.4 4.7 %steps.1 = (f32[3,64,768]{2,1,0:T(8,128)}, f32[768,128]{1,0:T(8,128)S(1)}) custom-call(f32[3,64,896]{2,1,0:T(8,128)S(1)} %get-tuple-element.23.first0, f32[3,64,896]{2,1,0:T(8,128)S(1)} %get-tuple-element.24.first1, f32[11,64,896]{2,1,0:T(8,128)S(1)} %get-tuple-element.25.coefs, f32[3,4,896]{2,1,0:T(4,128)S(1)} %get-tuple-element.34.halo_xh, ...), custom_call_target="tpu_custom_call" | custom-call | tf_op jit(solution)/shard_map/steps/pallas_call | solution.py:530
  27.1 14.5 %all_to_all.10 = f32[16,48,128]{2,1,0:T(8,128)S(1)} all-to-all(f32[16,48,128]{2,1,0:T(8,128)S(1)} %bitcast.35), channel_id=1, replica_groups=mesh['gx'=16,'gy'=16] {'gx'}, dimensions={0} | all-to-all | bytes 786432 | tf_op jit(solution)/shard_map/all_to_all | solution.py:542
  41.6 1.0 %along_x.1 = f32[256,128]{1,0:T(8,128)S(1)} custom-call(f32[768,128]{1,0:T(8,128)S(1)} %bitcast.32, bf16[256,1024]{1,0:T(8,128)(2,1)S(1)} %copy-done, bf16[256,1024]{1,0:T(8,128)(2,1)S(1)} %copy-done.1), custom_call_target="tpu_custom_call" | custom-call | tf_op jit(solution)/shard_map/along_x/pallas_call | solution.py:545
  42.6 14.8 %all_to_all.11 = f32[32,8,128]{2,1,0:T(8,128)S(1)} all-to-all(f32[32,8,128]{2,1,0:T(8,128)S(1)} %bitcast.33), channel_id=1, replica_groups={{0,1,2,3,4,5,6,7,8,9,10,11,12,13,14,15,128,129,130,131,132,133,134,135,..., dimensions={0} | all-to-all | bytes 262144 | tf_op jit(solution)/shard_map/all_to_all | solution.py:557
  57.4 1.2 %along_y.1 = (f32[4,1024]{1,0:T(4,128)}, f32[4,1024]{1,0:T(4,128)}) custom-call(f32[256,128]{1,0:T(8,128)S(1)} %bitcast.34, bf16[128,256]{1,0:T(8,128)(2,1)S(1)} %copy-done.6, bf16[128,256]{1,0:T(8,128)(2,1)S(1)} %copy-done.7, f32[64,128]{1,0:T(8,128)S(1)} %copy-done.8, bf16[64,64]{1,0:T(8,128)(2,1)S(1)} %copy-done.9, bf16[64,64]{1,0:T(8,128)(2,1)S(1)} %copy-done.10), custom_call_target="tpu_custom_call" | custom-call | tf_op jit(solution)/shard_map/along_y/pallas_call | solution.py:561
  (5 shorter events, 0.1 us)
Async XLA Ops:
  0.6 21.7 %copy-start = (bf16[256,1024]{1,0:T(8,128)(2,1)S(1)}, bf16[256,1024]{1,0:T(8,128)(2,1)}, u32[]{:S(2)}) copy-start(bf16[256,1024]{1,0:T(8,128)(2,1)} %constant.43.clone.rest_0_.waves_hi) | copy-start | bytes 1572868
  0.6 21.7 %copy-start.1 = (bf16[256,1024]{1,0:T(8,128)(2,1)S(1)}, bf16[256,1024]{1,0:T(8,128)(2,1)}, u32[]{:S(2)}) copy-start(bf16[256,1024]{1,0:T(8,128)(2,1)} %constant.44.clone.rest_1_.waves_lo) | copy-start | bytes 1572868
  0.7 21.7 %copy-start.6 = (bf16[128,256]{1,0:T(8,128)(2,1)S(1)}, bf16[128,256]{1,0:T(8,128)(2,1)}, u32[]{:S(2)}) copy-start(bf16[128,256]{1,0:T(8,128)(2,1)} %constant.45.clone.rest_2_.waves_hi) | copy-start | bytes 196612
  0.7 21.7 %copy-start.7 = (bf16[128,256]{1,0:T(8,128)(2,1)S(1)}, bf16[128,256]{1,0:T(8,128)(2,1)}, u32[]{:S(2)}) copy-start(bf16[128,256]{1,0:T(8,128)(2,1)} %constant.46.clone.rest_3_.waves_lo) | copy-start | bytes 196612
  0.7 21.7 %copy-start.9 = (bf16[64,64]{1,0:T(8,128)(2,1)S(1)}, bf16[64,64]{1,0:T(8,128)(2,1)}, u32[]{:S(2)}) copy-start(bf16[64,64]{1,0:T(8,128)(2,1)} %constant.48.clone.rest_5_.last_hi) | copy-start | bytes 24580
  2.4 11.2 %collective-permute-start.1 = (f32[96,128]{1,0:T(8,128)}, f32[96,128]{1,0:T(8,128)S(1)}, u32[]{:S(2)}, u32[]{:S(2)}) collective-permute-start(f32[96,128]{1,0:T(8,128)} %get-tuple-element.21), channel_id=1, source_target_pairs={{0,15},{1,2},{2,1},{3,4},{4,3},{5,6},{6,5},{7,8},{8,7},{9,10},{10,... | collective-permute-start | bytes 147464 | tf_op jit(solution)/shard_map/ppermute | solution.py:483
  6.5 7.0 %collective-permute-start = (f32[96,128]{1,0:T(8,128)}, f32[96,128]{1,0:T(8,128)S(1)}, u32[]{:S(2)}, u32[]{:S(2)}) collective-permute-start(f32[96,128]{1,0:T(8,128)} %get-tuple-element.20), channel_id=1, source_target_pairs={{0,1},{1,0},{2,3},{3,2},{4,5},{5,4},{6,7},{7,6},{8,9},{9,8},{10,11... | collective-permute-start | bytes 147464 | tf_op jit(solution)/shard_map/ppermute | solution.py:484
  8.8 0.9 %copy-start.2 = (f32[64,768]{1,0:T(8,128)S(1)}, f32[64,768]{1,0:T(8,128)}, u32[]{:S(2)}) copy-start(f32[64,768]{1,0:T(8,128)} %polar.1) | copy-start | bytes 589828
  9.7 0.9 %copy-start.3 = (f32[64,768]{1,0:T(8,128)S(1)}, f32[64,768]{1,0:T(8,128)}, u32[]{:S(2)}) copy-start(f32[64,768]{1,0:T(8,128)} %azimuth.1) | copy-start | bytes 589828
  10.7 0.9 %copy-start.4 = (s32[64,768]{1,0:T(8,128)S(1)}, s32[64,768]{1,0:T(8,128)}, u32[]{:S(2)}) copy-start(s32[64,768]{1,0:T(8,128)} %grains.1) | copy-start | bytes 589828
  11.6 0.7 %copy-start.11 = (f32[8,256]{1,0:T(8,128)S(1)}, f32[8,256]{1,0:T(8,128)}, u32[]{:S(2)}) copy-start(f32[8,256]{1,0:T(8,128)} %get-tuple-element.17.tables) | copy-start | bytes 24580
  12.3 10.1 %copy-start.5 = (bf16[768,256]{1,0:T(8,128)(2,1)S(1)}, bf16[768,256]{1,0:T(8,128)(2,1)}, u32[]{:S(2)}) copy-start(bf16[768,256]{1,0:T(8,128)(2,1)} %constant.50.clone.sum_z) | copy-start | bytes 1179652
  12.3 10.1 %copy-start.8 = (f32[64,128]{1,0:T(8,128)S(1)}, f32[64,128]{1,0:T(8,128)}, u32[]{:S(2)}) copy-start(f32[64,128]{1,0:T(8,128)} %constant.47.clone.rest_4_.twiddle) | copy-start | bytes 98308
  12.3 10.1 %copy-start.10 = (bf16[64,64]{1,0:T(8,128)(2,1)S(1)}, bf16[64,64]{1,0:T(8,128)(2,1)}, u32[]{:S(2)}) copy-start(bf16[64,64]{1,0:T(8,128)(2,1)} %constant.49.clone.rest_6_.last_lo) | copy-start | bytes 24580
  13.8 7.8 %collective-permute-start.3 = (f32[3,4,896]{2,1,0:T(4,128)S(1)}, f32[3,4,896]{2,1,0:T(4,128)S(1)}, u32[]{:S(2)}, u32[]{:S(2)}) collective-permute-start(f32[3,4,896]{2,1,0:T(4,128)S(1)} %get-tuple-element.35), channel_id=1, source_target_pairs={{0,240},{16,32},{32,16},{48,64},{64,48},{80,96},{96,80},{112,128},... | collective-permute-start | bytes 129032 | tf_op jit(solution)/shard_map/ppermute | solution.py:517
  19.5 2.9 %collective-permute-start.2 = (f32[3,4,896]{2,1,0:T(4,128)S(1)}, f32[3,4,896]{2,1,0:T(4,128)S(1)}, u32[]{:S(2)}, u32[]{:S(2)}) collective-permute-start(f32[3,4,896]{2,1,0:T(4,128)S(1)} %get-tuple-element.36), channel_id=1, source_target_pairs={{0,16},{16,0},{32,48},{48,32},{64,80},{80,64},{96,112},{112,96},{1... | collective-permute-start | bytes 129032 | tf_op jit(solution)/shard_map/ppermute | solution.py:518
